TPU v7x, 256 devices: a whole 4x4x8 slice. The times are simulated.
256 devices in a mesh: ctx: 32 (over x, y, core), head: 8 (over z).
Axes of the slice: x: 4, y: 4, z: 8, core: 2. Of those that a mesh axis runs over, the one named last changes fastest.
Arguments:
- queries: bfloat16 [2, 6144, 4096], P(None, 'ctx', 'head'), may hold values from -6 to 6
- key_rows: bfloat16 [2, 6144, 4096], P(None, 'ctx', 'head'), may hold values from -6 to 6
- value_rows: bfloat16 [2, 6144, 4096], P(None, 'ctx', 'head'), may hold values from -6 to 6
- out_weight: bfloat16 [4096, 4096], P('head'), may hold values from -0.09375 to 0.09375
- cotangent: bfloat16 [2, 6144, 4096], P(None, 'ctx', 'head'), may hold values from -6 to 6
Outputs:
- layer_output: bfloat16 [2, 6144, 4096], P(None, 'ctx', 'head')
- query_grad: bfloat16 [2, 6144, 4096], P(None, 'ctx', 'head')
- key_grad: bfloat16 [2, 6144, 4096], P(None, 'ctx', 'head')
- value_grad: bfloat16 [2, 6144, 4096], P(None, 'ctx', 'head')
- weight_grad: float32 [4096, 4096], P('head', 'ctx')
All inputs are finite; a program needn't handle non-finite values.
Results may differ from a plain program's by a relative error of at most 0.015.
Values may be sent and summed in bfloat16 or wider, within the bound.
No kernel may reach another device: no remote copies, remote signals or barrier semaphores. Data moves between devices by JAX's collectives and lax.ppermute only.
A program may use at most 128 MiB of HBM per device.

v0:
```python
import functools

import jax
import jax.numpy as jnp
from jax import lax
from jax.experimental import pallas as pl
from jax.experimental.pallas import tpu as pltpu
from jax.sharding import Mesh
from jax.sharding import PartitionSpec as P

DH = 128
CTX = ("ctx_0", "ctx_1", "ctx_2")
SCALE = DH ** (-0.5)
EPS = 1e-06
F32, BF16 = jnp.float32, jnp.bfloat16
VMEM = pltpu.VMEM
LIMIT, FULL = 24 << 20, 123 << 19


def dot(a, b, ca, cb):
    return lax.dot_general(a, b, (((ca,), (cb,)), ((), ())), preferred_element_type=F32)


def call(body, outs, args, flops, limit=LIMIT, **kw):
    size = sum(a.size * a.dtype.itemsize for a in args)
    size += sum(o.size * o.dtype.itemsize for o in outs)
    cost = pl.CostEstimate(flops=flops, bytes_accessed=size, transcendentals=0)
    params = pltpu.CompilerParams(vmem_limit_bytes=limit)
    return pl.pallas_call(body, out_shape=outs, cost_estimate=cost, compiler_params=params, **kw)(*args)


def shape(dims, dtype):
    return jax.ShapeDtypeStruct(dims, dtype)


def lower_mask(n):
    return lax.broadcasted_iota(jnp.int32, (n, n), 0) >= lax.broadcasted_iota(jnp.int32, (n, n), 1)


def heads(width):
    return [(b, h, slice(h * DH, (h + 1) * DH)) for b in range(2) for h in range(width // DH)]


def state_body(k_ref, v_ref, out_ref):
    for i, (b, _, s) in enumerate(heads(k_ref.shape[2])):
        out_ref[i] = dot(k_ref[b, :, s], v_ref[b, :, s], 0, 0).astype(BF16)


def scan_body(reverse, x_ref, out_ref):
    total = jnp.zeros(x_ref.shape[1:], F32)
    n = x_ref.shape[0]
    for k in reversed(range(n)) if reverse else range(n):
        out_ref[k] = total.astype(BF16)
        total = total + x_ref[k].astype(F32)


def forward_body(q_ref, k_ref, v_ref, state_ref, normed_ref, attended_ref, scores_ref):
    lower = lower_mask(q_ref.shape[1])
    for i, (b, _, s) in enumerate(heads(q_ref.shape[2])):
        q, v = q_ref[b, :, s], v_ref[b, :, s]
        scores = jnp.where(lower, dot(q, k_ref[b, :, s], 1, 1) * SCALE, 0.0).astype(BF16)
        scores_ref[i] = scores
        attended = dot(scores, v, 1, 0) + SCALE * dot(q, state_ref[i], 1, 0)
        attended_ref[b, :, s] = attended
        mean = jnp.mean(attended * attended, axis=-1, keepdims=True)
        normed_ref[b, :, s] = (attended / jnp.sqrt(mean + EPS)).astype(BF16)


def project_body(n_ref, w_hbm, out_hbm, w_buf, out_buf, w_sem, out_sem):
    chunks, _, width = w_buf.shape
    copies = []
    for k in range(chunks):
        copies.append(
            pltpu.make_async_copy(w_hbm.at[:, k * width : (k + 1) * width], w_buf.at[k], w_sem.at[k])
        )
        copies[k].start()
    done = []
    for k in range(chunks):
        copies[k].wait()
        out_buf[k] = dot(n_ref[...], w_buf[k], 1, 0).astype(BF16)
        done.append(pltpu.make_async_copy(out_buf.at[k], out_hbm.at[k], out_sem.at[k]))
        done[k].start()
    for copy in done:
        copy.wait()


def grad_body(c_hbm, w_hbm, a_ref, q_ref, ag_ref, gs_ref, c_buf, w_buf, c_sem, w_sem):
    chunks, rows, width = c_buf.shape
    copies = []
    for k in range(chunks):
        cols = slice(k * width, (k + 1) * width)
        pair = (
            pltpu.make_async_copy(c_hbm.at[k], c_buf.at[k], c_sem.at[k]),
            pltpu.make_async_copy(w_hbm.at[:, cols], w_buf.at[k], w_sem.at[k]),
        )
        for copy in pair:
            copy.start()
        copies.append(pair)
    total = jnp.zeros((rows, width), F32)
    for k in range(chunks):
        for copy in copies[k]:
            copy.wait()
        total = total + dot(c_buf[k], w_buf[k], 1, 1)
    n = rows // 2
    for i, (b, _, s) in enumerate(heads(width)):
        part = slice(b * n, (b + 1) * n)
        a, g = a_ref[part, s], total[part, s]
        root = 1.0 / jnp.sqrt(jnp.mean(a * a, axis=-1, keepdims=True) + EPS)
        inner = jnp.mean(g * a, axis=-1, keepdims=True)
        ag = (g * root - a * (inner * root * root * root)).astype(BF16)
        ag_ref[part, s] = ag
        gs_ref[i] = dot(q_ref[part, s], ag, 0, 0).astype(BF16)


def weight_pieces(place, n_ref, c_hbm, c_buf, c_sem):
    chunks = c_buf.shape[0]
    copies = [pltpu.make_async_copy(c_hbm.at[k], c_buf.at[k], c_sem.at[k]) for k in range(chunks)]
    for copy in copies:
        copy.start()
    left = n_ref[...].T
    mx, my, mc = place[0], place[1], place[2]
    low = pl.multiple_of(mc * DH, DH)
    high = pl.multiple_of(mc * DH + 2 * DH, DH)
    for k in range(chunks):
        copies[k].wait()
        pick = jnp.concatenate([c_buf[k, :, pl.ds(low, DH)], c_buf[k, :, pl.ds(high, DH)]], axis=1)
        r = dot(left, pick, 1, 0)
        x = k // 2
        for j in range(2):
            y = 2 * (k % 2) + j
            far = jnp.where(mc == 0, (y - my + 4) % 4, (x - mx + 4) % 4)
            yield far, jnp.where(mc == 0, x, y), r[:, j * DH : (j + 1) * DH]


def weight_body(place, n_ref, c_hbm, out_ref, c_buf, c_sem):
    for far, other, piece in weight_pieces(place, n_ref, c_hbm, c_buf, c_sem):
        out_ref[far, other] = piece.astype(BF16)


def weight_add_body(place, n_ref, c_hbm, in_ref, o0, o1, o2, o3, c_buf, c_sem):
    def put(far, other, value):
        for d, ref in enumerate((o0, o1, o2, o3)):

            @pl.when(far == d)
            def _():
                ref[other] = value

    for far, other, piece in weight_pieces(place, n_ref, c_hbm, c_buf, c_sem):
        put(far, other, (piece + in_ref[far, other].astype(F32)).astype(BF16))


def backward_body(q_ref, k_ref, v_ref, sc_ref, ag_ref, st_ref, gs_ref, dq_ref, dk_ref, dv_ref):
    lower = lower_mask(q_ref.shape[1])
    for i, (b, _, s) in enumerate(heads(q_ref.shape[2])):
        q, k, v, ag = q_ref[b, :, s], k_ref[b, :, s], v_ref[b, :, s], ag_ref[b, :, s]
        sg = jnp.where(lower, dot(ag, v, 1, 1) * SCALE, 0.0).astype(BF16)
        dq_ref[b, :, s] = (dot(sg, k, 1, 0) + SCALE * dot(ag, st_ref[i], 1, 1)).astype(BF16)
        dk_ref[b, :, s] = (dot(sg, q, 0, 0) + SCALE * dot(v, gs_ref[i], 1, 1)).astype(BF16)
        dv_ref[b, :, s] = (dot(sc_ref[i], ag, 0, 0) + SCALE * dot(k, gs_ref[i], 1, 0)).astype(BF16)


def exclusive(local, reverse):
    n = lax.axis_size(CTX)
    pieces = local.reshape(n, -1, DH)
    got = lax.all_to_all(pieces, CTX, split_axis=0, concat_axis=0, tiled=True)
    sums = call(
        functools.partial(scan_body, reverse), [shape(got.shape, BF16)], [got], got.size
    )[0]
    back = lax.all_to_all(sums, CTX, split_axis=0, concat_axis=0, tiled=True)
    return back.reshape(local.shape)


def shift(value, axis, step):
    n = lax.axis_size(axis)
    return lax.ppermute(value, axis, [(i, (i + step) % n) for i in range(n)])


def shift_by_core(value, first, step):
    def target(x, y, c):
        along_y = (c == 0) == first
        return (x, (y + step) % 4, c) if along_y else ((x + step) % 4, y, c)

    def index(x, y, c):
        return (x * 4 + y) * 2 + c

    places = [(x, y, c) for x in range(4) for y in range(4) for c in range(2)]
    return lax.ppermute(value, CTX, [(index(*p), index(*target(*p))) for p in places])


def reduce_weight(normed, gathered, factor, after):
    mx, my, mc = (lax.axis_index(a) for a in CTX)
    chunks, rows, width = gathered.shape
    flops = rows * width * width * chunks
    grid = (4, 4, width, DH)
    scratch = [VMEM(gathered.shape, BF16), pltpu.SemaphoreType.DMA((chunks,))]
    smem, vmem, hbm = (pl.BlockSpec(memory_space=m) for m in (pltpu.SMEM, VMEM, pltpu.HBM))
    theirs = call(
        weight_body,
        [shape(grid, BF16)],
        [jnp.stack([mx, my, 1 - mc]).astype(jnp.int32), normed, gathered],
        flops,
        limit=FULL,
        in_specs=[smem, vmem, hbm],
        out_specs=[vmem],
        scratch_shapes=scratch,
    )[0]
    theirs, _ = lax.optimization_barrier((shift(theirs, "ctx_2", 1), after))
    total = call(
        weight_add_body,
        [shape(grid[1:], BF16)] * 4,
        [jnp.stack([mx, my, mc]).astype(jnp.int32), normed, gathered, theirs],
        flops,
        limit=FULL,
        in_specs=[smem, vmem, hbm, vmem],
        out_specs=[vmem] * 4,
        scratch_shapes=scratch,
    )
    got = [shift_by_core(total[d], True, d) for d in (1, 2, 3)]
    part = total[0].astype(F32) + sum(g.astype(F32) for g in got)
    send = part.astype(BF16)
    me = jnp.where(mc == 0, mx, my)
    got = [
        shift_by_core(lax.dynamic_index_in_dim(send, (me + d) % 4, 0, False), False, d)
        for d in (1, 2, 3)
    ]
    own = lax.dynamic_index_in_dim(part, me, 0, False)
    return (own + sum(g.astype(F32) for g in got)) * factor


def layer(queries, key_rows, value_rows, out_weight, cotangent):
    _, length, width = queries.shape
    n_head = lax.axis_size("head")
    rows = 2 * length
    n_mat = 2 * width // DH
    square = (n_mat, DH, DH)
    gathered = lax.all_gather(cotangent, "head", axis=0, tiled=False).reshape(n_head, rows, width)
    mat_flops = 2 * n_mat * length * DH * DH
    local = call(state_body, [shape(square, BF16)], [key_rows, value_rows], mat_flops)[0]
    state = exclusive(local, False)
    normed, attended, scores = call(
        forward_body,
        [shape(queries.shape, BF16), shape(queries.shape, F32), shape((n_mat, length, length), BF16)],
        [queries, key_rows, value_rows, state],
        5 * mat_flops,
    )
    normed = normed.reshape(rows, width)
    big = 2 * rows * width * width * n_head
    partial = call(
        project_body,
        [shape((n_head, rows, width), BF16)],
        [normed, out_weight],
        big,
        limit=FULL,
        in_specs=[pl.BlockSpec(memory_space=VMEM), pl.BlockSpec(memory_space=pltpu.HBM)],
        out_specs=[pl.BlockSpec(memory_space=pltpu.HBM)],
        scratch_shapes=[
            VMEM((n_head, width, width), BF16),
            VMEM((n_head, rows, width), BF16),
            pltpu.SemaphoreType.DMA((n_head,)),
            pltpu.SemaphoreType.DMA((n_head,)),
        ],
    )[0]
    layer_output = lax.psum_scatter(
        partial.reshape(n_head * rows, width), "head", scatter_dimension=0, tiled=True
    ).reshape(queries.shape)
    attended_grad, local_grad = call(
        grad_body,
        [shape((rows, width), BF16), shape(square, BF16)],
        [gathered, out_weight, attended.reshape(rows, width), queries.reshape(rows, width)],
        big,
        limit=FULL,
        in_specs=[pl.BlockSpec(memory_space=m) for m in (pltpu.HBM, pltpu.HBM, VMEM, VMEM)],
        scratch_shapes=[
            VMEM(gathered.shape, BF16),
            VMEM((n_head, width, width), BF16),
            pltpu.SemaphoreType.DMA((n_head,)),
            pltpu.SemaphoreType.DMA((n_head,)),
        ],
    )
    weight_grad = reduce_weight(
        normed, gathered, (rows * lax.axis_size(CTX)) ** (-0.5), local_grad
    )
    grad_state = exclusive(local_grad, True)
    query_grad, key_grad, value_grad = call(
        backward_body,
        [shape(queries.shape, BF16)] * 3,
        [queries, key_rows, value_rows, scores, attended_grad.reshape(queries.shape), state, grad_state],
        10 * mat_flops,
    )
    return (layer_output, query_grad, key_grad, value_grad, weight_grad)


def solution(mesh):
    split = Mesh(
        mesh.devices.reshape(4, 4, 2, mesh.shape["head"]), ("ctx_0", "ctx_1", "ctx_2", "head")
    )
    rows = P(None, CTX, "head")
    return jax.shard_map(
        layer,
        mesh=split,
        in_specs=(rows, rows, rows, P("head", None), rows),
        out_specs=(rows, rows, rows, rows, P("head", CTX)),
        check_vma=False,
    )
```

profile of v0, /device:TPU:1, one launch (start us, length us, event | category | flops | bytes accessed | tf_op | source)
XLA Modules:
  0.0 129.5 jit_solution(8355393271383574230)
XLA Ops:
  10.3 17.3 %all_to_all.20.x_ref = bf16[32,32,128]{2,1,0:T(8,128)(2,1)S(1)} all-to-all(bf16[32,32,128]{2,1,0:T(8,128)(2,1)S(1)} %bitcast.31), channel_id=1, replica_groups=mesh['ctx_0'=4,'ctx_1'=4,'ctx_2'=2,'head'=8] {'ctx_0','ctx_1','ctx_2'}, dimensions={0} | all-to-all | bytes 524288 | tf_op jit(solution)/shard_map/all_to_all | solution.py:165
  27.7 12.4 %all_to_all.21 = bf16[32,32,128]{2,1,0:T(8,128)(2,1)S(1)} all-to-all(bf16[32,32,128]{2,1,0:T(8,128)(2,1)S(1)} %shard_map.93), channel_id=1, replica_groups=mesh['ctx_0'=4,'ctx_1'=4,'ctx_2'=2,'head'=8] {'ctx_0','ctx_1','ctx_2'}, dimensions={0} | all-to-all | bytes 524288 | tf_op jit(solution)/shard_map/all_to_all | solution.py:169
  40.1 1.0 copy-done.3
  41.1 1.0 copy-done.6
  42.1 1.3 %shard_map.94 = (bf16[2,192,512]{2,1,0:T(8,128)(2,1)S(1)}, f32[2,192,512]{2,1,0:T(8,128)S(1)}, bf16[8,192,192]{2,1,0:T(8,128)(2,1)S(1)}) custom-call(bf16[2,192,512]{2,1,0:T(8,128)(2,1)S(1)} %copy-done, bf16[2,192,512]{2,1,0:T(8,128)(2,1)S(1)} %copy-done.3, bf16[2,192,512]{2,1,0:T(8,128)(2,1)S(1)} %copy-done.6, bf16[8,128,128]{2,1,0:T(8,128)(2,1)S(1)} %bitcast.29), custom_call_target="tpu_custom_call" | custom-call | flops 251658240 | bytes 3211264 | tf_op jit(solution)/shard_map/pallas_call | solution.py:29
  45.1 5.9 %shard_map.95 = bf16[8,384,512]{2,1,0:T(8,128)(2,1)} custom-call(bf16[384,512]{1,0:T(8,128)(2,1)} %bitcast.26, bf16[512,4096]{1,0:T(8,128)(2,1)} %w_hbm.3), custom_call_target="tpu_custom_call" | custom-call | flops 1610612736 | bytes 7733248 | tf_op jit(solution)/shard_map/pallas_call | solution.py:29
  51.7 6.4 %all-gather.3.cloned.1.call-done = bf16[16,192,512]{2,1,0:T(8,128)(2,1)} async-done(((bf16[2,192,512]{2,1,0:T(8,128)(2,1)}), bf16[16,192,512]{2,1,0:T(8,128)(2,1)}) %all-gather.3.cloned.1.call-update) | async-done | bytes 3145744 | tf_op jit(solution)/shard_map/all_gather | solution.py:236
  58.0 6.9 %shard_map.99 = bf16[4,4,512,128]{3,2,1,0:T(8,128)(2,1)} custom-call(s32[3]{0:T(128)} %get-tuple-element.37.place, bf16[384,512]{1,0:T(8,128)(2,1)} %bitcast.27, bf16[8,384,512]{2,1,0:T(8,128)(2,1)} %bitcast.35), custom_call_target="tpu_custom_call" | custom-call | flops 805306368 | bytes 5636108 | tf_op jit(solution)/shard_map/pallas_call | solution.py:29
  64.9 1.3 %collective-permute-start = (bf16[4,4,512,128]{3,2,1,0:T(8,128)(2,1)}, bf16[4,4,512,128]{3,2,1,0:T(8,128)(2,1)}, u32[]{:S(2)}, u32[]{:S(2)}) collective-permute-start(bf16[4,4,512,128]{3,2,1,0:T(8,128)(2,1)} %shard_map.99), channel_id=1, source_target_pairs={{0,8},{8,0},{1,9},{9,1},{2,10},{10,2},{3,11},{11,3},{4,12},{12,4},... | collective-permute-start | bytes 6291464 | tf_op jit(solution)/shard_map/ppermute | solution.py:175
  66.3 6.5 %shard_map.96 = (bf16[384,512]{1,0:T(8,128)(2,1)}, bf16[8,128,128]{2,1,0:T(8,128)(2,1)}) custom-call(bf16[8,384,512]{2,1,0:T(8,128)(2,1)} %bitcast.36, bf16[512,4096]{1,0:T(8,128)(2,1)} %w_hbm.3, f32[384,512]{1,0:T(8,128)} %bitcast.33, bf16[384,512]{1,0:T(8,128)(2,1)} %bitcast.25), custom_call_target="tpu_custom_call" | custom-call | flops 1610612736 | bytes 9175040 | tf_op jit(solution)/shard_map/pallas_call | solution.py:29
  72.8 8.1 %shard_map.100 = (bf16[4,512,128]{2,1,0:T(8,128)(2,1)}, bf16[4,512,128]{2,1,0:T(8,128)(2,1)}, bf16[4,512,128]{2,1,0:T(8,128)(2,1)}, bf16[4,512,128]{2,1,0:T(8,128)(2,1)}) custom-call(s32[3]{0:T(128)} %get-tuple-element.36.place, bf16[384,512]{1,0:T(8,128)(2,1)} %bitcast.28, bf16[8,384,512]{2,1,0:T(8,128)(2,1)} %bitcast.37, ...), custom_call_target="tpu_custom_call" | custom-call | flops 805306368 | bytes 7733260 | tf_op jit(solution)/shard_map/pallas_call | solution.py:29
  80.9 1.3 collective-permute-start.1
  82.2 2.4 %collective-permute-start.2 = (bf16[4,512,128]{2,1,0:T(8,128)(2,1)}, bf16[4,512,128]{2,1,0:T(8,128)(2,1)}, u32[]{:S(2)}, u32[]{:S(2)}) collective-permute-start(bf16[4,512,128]{2,1,0:T(8,128)(2,1)} %get-tuple-element.29), channel_id=1, source_target_pairs={{0,32},{8,136},{16,48},{24,152},{32,0},{40,168},{48,16},{56,184},{... | collective-permute-start | bytes 1572872 | tf_op jit(solution)/shard_map/ppermute | solution.py:187
  84.6 1.2 collective-permute-start.3
  85.8 5.3 %all-to-all-start.2 = ((bf16[32,32,128]{2,1,0:T(8,128)(2,1)}), bf16[32,32,128]{2,1,0:T(8,128)(2,1)S(1)}, u32[]{:S(2)}, u32[]{:S(2)}) async-start(bf16[32,32,128]{2,1,0:T(8,128)(2,1)} %bitcast.9), calls=%async_computation.3 | async-start | bytes 524288 | tf_op jit(solution)/shard_map/all_to_all | solution.py:165
  91.2 11.2 %all-to-all-done.2.x_ref = bf16[32,32,128]{2,1,0:T(8,128)(2,1)S(1)} async-done(((bf16[32,32,128]{2,1,0:T(8,128)(2,1)}), bf16[32,32,128]{2,1,0:T(8,128)(2,1)S(1)}, u32[]{:S(2)}, u32[]{:S(2)}) %all-to-all-start.2) | async-done | bytes 262176 | tf_op jit(solution)/shard_map/all_to_all | solution.py:165
  103.1 5.3 %all-to-all-start.3 = ((bf16[32,32,128]{2,1,0:T(8,128)(2,1)}), bf16[32,32,128]{2,1,0:T(8,128)(2,1)S(1)}, u32[]{:S(2)}, u32[]{:S(2)}) async-start(bf16[32,32,128]{2,1,0:T(8,128)(2,1)} %shard_map.97), calls=%async_computation.4 | async-start | bytes 524288 | tf_op jit(solution)/shard_map/all_to_all | solution.py:169
  108.4 2.8 %fusion.1 = (bf16[4,512,128]{2,1,0:T(8,128)(2,1)S(1)}, f32[4,512,128]{2,1,0:T(8,128)}) fusion(bf16[4,512,128]{2,1,0:T(8,128)(2,1)} %collective-permute-done.3, bf16[4,512,128]{2,1,0:T(8,128)(2,1)} %collective-permute-done.2, bf16[4,512,128]{2,1,0:T(8,128)(2,1)} %collective-permute-done.1, bf16[4,512,128]{2,1,0:T(8,128)(2,1)} %get-tuple-element.27), kind=kLoop, calls=%fused_computation.9 | loop fusion | flops 2097152 | bytes 3670016 | tf_op jit(solution)/shard_map/convert_element_type | solution.py:220
  111.9 1.4 %collective-permute-start.4 = (bf16[512,128]{1,0:T(8,128)(2,1)}, bf16[512,128]{1,0:T(8,128)(2,1)S(1)}, u32[]{:S(2)}, u32[]{:S(2)}) collective-permute-start(bf16[512,128]{1,0:T(8,128)(2,1)} %get-tuple-element.33), channel_id=1, source_target_pairs={{0,64},{8,24},{16,80},{24,40},{32,96},{40,56},{48,112},{56,8},{64,... | collective-permute-start | bytes 393224 | tf_op jit(solution)/shard_map/ppermute | solution.py:187
  113.3 1.3 %collective-permute-start.6 = (bf16[512,128]{1,0:T(8,128)(2,1)}, bf16[512,128]{1,0:T(8,128)(2,1)S(1)}, u32[]{:S(2)}, u32[]{:S(2)}) collective-permute-start(bf16[512,128]{1,0:T(8,128)(2,1)} %get-tuple-element.34), channel_id=1, source_target_pairs={{0,192},{8,56},{16,208},{24,8},{32,224},{40,24},{48,240},{56,40},{... | collective-permute-start | bytes 393224 | tf_op jit(solution)/shard_map/ppermute | solution.py:187
  114.6 1.6 %collective-permute-start.5 = (bf16[512,128]{1,0:T(8,128)(2,1)S(1)}, bf16[512,128]{1,0:T(8,128)(2,1)S(1)}, u32[]{:S(2)}, u32[]{:S(2)}) collective-permute-start(bf16[512,128]{1,0:T(8,128)(2,1)S(1)} %get-tuple-element.35), channel_id=1, source_target_pairs={{0,128},{8,40},{16,144},{24,56},{32,160},{40,8},{48,176},{56,24},{... | collective-permute-start | bytes 393224 | tf_op jit(solution)/shard_map/ppermute | solution.py:187
  116.2 1.2 all-to-all-done.3
  117.5 3.4 %shard_map.98 = (bf16[2,192,512]{2,1,0:T(8,128)(2,1)}, bf16[2,192,512]{2,1,0:T(8,128)(2,1)}, bf16[2,192,512]{2,1,0:T(8,128)(2,1)}) custom-call(bf16[2,192,512]{2,1,0:T(8,128)(2,1)S(1)} %copy-done.1, bf16[2,192,512]{2,1,0:T(8,128)(2,1)S(1)} %copy-done.4, bf16[2,192,512]{2,1,0:T(8,128)(2,1)S(1)} %copy-done.7, ...), custom_call_target="tpu_custom_call" | custom-call | flops 503316480 | bytes 3866624 | tf_op jit(solution)/shard_map/pallas_call | solution.py:29
  120.9 1.7 %fusion = f32[512,128]{1,0:T(8,128)} fusion(bf16[512,128]{1,0:T(8,128)(2,1)S(1)} %collective-permute-done.6, bf16[512,128]{1,0:T(8,128)(2,1)S(1)} %collective-permute-done.5, bf16[512,128]{1,0:T(8,128)(2,1)S(1)} %collective-permute-done.4, f32[4,512,128]{2,1,0:T(8,128)} %get-tuple-element.32, s32[]{:T(128)S(6)} %select_n.33), kind=kLoop, calls=%fused_computation.2 | loop fusion | flops 458752 | bytes 917508 | tf_op jit(solution)/shard_map/mul | solution.py:227
  (37 shorter events, 6.9 us)
Async XLA Ops:
  7.2 33.0 %copy-start = (bf16[2,192,512]{2,1,0:T(8,128)(2,1)S(1)}, bf16[2,192,512]{2,1,0:T(8,128)(2,1)}, u32[]{:S(2)}) copy-start(bf16[2,192,512]{2,1,0:T(8,128)(2,1)} %q_ref.3) | copy-start | bytes 1179652
  7.2 50.8 %all-gather.3.cloned.1.call-start = ((), (), s32[]{:S(2)}) async-start(), calls=%async_computation.6 | async-start | bytes 3538944 | tf_op jit(solution)/shard_map/all_gather | solution.py:236
  7.9 114.7 %reduce-scatter.2.cloned.1.call-start = ((), (), s32[]{:S(2)}) async-start(), calls=%async_computation.5 | async-start | bytes 3538944 | tf_op jit(solution)/shard_map/reduce_scatter | solution.py:263
  8.0 1.0 copy-start.2
  9.0 1.0 copy-start.5
  40.1 1.0 copy-start.3
  41.1 1.0 copy-start.6
  43.5 0.7 copy-start.8
  44.2 0.9 copy-start.9
  64.9 7.8 %collective-permute-start = (bf16[4,4,512,128]{3,2,1,0:T(8,128)(2,1)}, bf16[4,4,512,128]{3,2,1,0:T(8,128)(2,1)}, u32[]{:S(2)}, u32[]{:S(2)}) collective-permute-start(bf16[4,4,512,128]{3,2,1,0:T(8,128)(2,1)} %shard_map.99), channel_id=1, source_target_pairs={{0,8},{8,0},{1,9},{9,1},{2,10},{10,2},{3,11},{11,3},{4,12},{12,4},... | collective-permute-start | bytes 6291464 | tf_op jit(solution)/shard_map/ppermute | solution.py:175
  80.9 36.6 %copy-start.1 = (bf16[2,192,512]{2,1,0:T(8,128)(2,1)S(1)}, bf16[2,192,512]{2,1,0:T(8,128)(2,1)}, u32[]{:S(2)}) copy-start(bf16[2,192,512]{2,1,0:T(8,128)(2,1)} %q_ref.3) | copy-start | bytes 1179652
  80.9 36.6 %copy-start.4 = (bf16[2,192,512]{2,1,0:T(8,128)(2,1)S(1)}, bf16[2,192,512]{2,1,0:T(8,128)(2,1)}, u32[]{:S(2)}) copy-start(bf16[2,192,512]{2,1,0:T(8,128)(2,1)} %k_ref.5) | copy-start | bytes 1179652
  80.9 36.6 %copy-start.7 = (bf16[2,192,512]{2,1,0:T(8,128)(2,1)S(1)}, bf16[2,192,512]{2,1,0:T(8,128)(2,1)}, u32[]{:S(2)}) copy-start(bf16[2,192,512]{2,1,0:T(8,128)(2,1)} %v_ref.5) | copy-start | bytes 1179652
  80.9 36.6 %copy-start.10 = (bf16[384,512]{1,0:T(8,128)(2,1)S(1)}, bf16[384,512]{1,0:T(8,128)(2,1)}, u32[]{:S(2)}) copy-start(bf16[384,512]{1,0:T(8,128)(2,1)} %get-tuple-element.21) | copy-start | bytes 1179652
  80.9 27.5 %collective-permute-start.1 = (bf16[4,512,128]{2,1,0:T(8,128)(2,1)}, bf16[4,512,128]{2,1,0:T(8,128)(2,1)}, u32[]{:S(2)}, u32[]{:S(2)}) collective-permute-start(bf16[4,512,128]{2,1,0:T(8,128)(2,1)} %get-tuple-element.28), channel_id=1, source_target_pairs={{0,16},{8,72},{16,32},{24,88},{32,48},{40,104},{48,0},{56,120},{64... | collective-permute-start | bytes 1572872 | tf_op jit(solution)/shard_map/ppermute | solution.py:187
  82.2 26.2 %collective-permute-start.2 = (bf16[4,512,128]{2,1,0:T(8,128)(2,1)}, bf16[4,512,128]{2,1,0:T(8,128)(2,1)}, u32[]{:S(2)}, u32[]{:S(2)}) collective-permute-start(bf16[4,512,128]{2,1,0:T(8,128)(2,1)} %get-tuple-element.29), channel_id=1, source_target_pairs={{0,32},{8,136},{16,48},{24,152},{32,0},{40,168},{48,16},{56,184},{... | collective-permute-start | bytes 1572872 | tf_op jit(solution)/shard_map/ppermute | solution.py:187
  84.6 23.8 %collective-permute-start.3 = (bf16[4,512,128]{2,1,0:T(8,128)(2,1)}, bf16[4,512,128]{2,1,0:T(8,128)(2,1)}, u32[]{:S(2)}, u32[]{:S(2)}) collective-permute-start(bf16[4,512,128]{2,1,0:T(8,128)(2,1)} %get-tuple-element.30), channel_id=1, source_target_pairs={{0,48},{8,200},{16,0},{24,216},{32,16},{40,232},{48,32},{56,248},{... | collective-permute-start | bytes 1572872 | tf_op jit(solution)/shard_map/ppermute | solution.py:187
  85.8 16.5 %all-to-all-start.2 = ((bf16[32,32,128]{2,1,0:T(8,128)(2,1)}), bf16[32,32,128]{2,1,0:T(8,128)(2,1)S(1)}, u32[]{:S(2)}, u32[]{:S(2)}) async-start(bf16[32,32,128]{2,1,0:T(8,128)(2,1)} %bitcast.9), calls=%async_computation.3 | async-start | bytes 524288 | tf_op jit(solution)/shard_map/all_to_all | solution.py:165
  103.1 14.4 %all-to-all-start.3 = ((bf16[32,32,128]{2,1,0:T(8,128)(2,1)}), bf16[32,32,128]{2,1,0:T(8,128)(2,1)S(1)}, u32[]{:S(2)}, u32[]{:S(2)}) async-start(bf16[32,32,128]{2,1,0:T(8,128)(2,1)} %shard_map.97), calls=%async_computation.4 | async-start | bytes 524288 | tf_op jit(solution)/shard_map/all_to_all | solution.py:169
  111.9 9.0 %collective-permute-start.4 = (bf16[512,128]{1,0:T(8,128)(2,1)}, bf16[512,128]{1,0:T(8,128)(2,1)S(1)}, u32[]{:S(2)}, u32[]{:S(2)}) collective-permute-start(bf16[512,128]{1,0:T(8,128)(2,1)} %get-tuple-element.33), channel_id=1, source_target_pairs={{0,64},{8,24},{16,80},{24,40},{32,96},{40,56},{48,112},{56,8},{64,... | collective-permute-start | bytes 393224 | tf_op jit(solution)/shard_map/ppermute | solution.py:187
  113.3 7.7 %collective-permute-start.6 = (bf16[512,128]{1,0:T(8,128)(2,1)}, bf16[512,128]{1,0:T(8,128)(2,1)S(1)}, u32[]{:S(2)}, u32[]{:S(2)}) collective-permute-start(bf16[512,128]{1,0:T(8,128)(2,1)} %get-tuple-element.34), channel_id=1, source_target_pairs={{0,192},{8,56},{16,208},{24,8},{32,224},{40,24},{48,240},{56,40},{... | collective-permute-start | bytes 393224 | tf_op jit(solution)/shard_map/ppermute | solution.py:187
  114.6 6.3 %collective-permute-start.5 = (bf16[512,128]{1,0:T(8,128)(2,1)S(1)}, bf16[512,128]{1,0:T(8,128)(2,1)S(1)}, u32[]{:S(2)}, u32[]{:S(2)}) collective-permute-start(bf16[512,128]{1,0:T(8,128)(2,1)S(1)} %get-tuple-element.35), channel_id=1, source_target_pairs={{0,128},{8,40},{16,144},{24,56},{32,160},{40,8},{48,176},{56,24},{... | collective-permute-start | bytes 393224 | tf_op jit(solution)/shard_map/ppermute | solution.py:187
Sparse Core Ops, SparseCore 0:
  9.8 48.2 all-gather.2
  61.1 43.0 reduce-scatter.1
where the time goes:
time: 130 us; the launch traced here: 129 us
  Pallas kernels  33.3 us (26%)
  blocking collectives  29.8 us (23%)
  starting transfers between devices  21.2 us (16%)
  waiting for transfers between devices  19.5 us (15%)
  between operations  14.3 us (11%)
  local copies, waits for them, and re-layouts  6.4 us (5%)
  other arithmetic  5.08 us (4%)
    pallas_call x9, Pallas kernels, call(): pl.pallas_call(body, out_shape=outs, cost_estimate=cost, compiler_params=...  33.3 us
    all_to_all x1, blocking collectives, exclusive(): got = lax.all_to_all(pieces, CTX, split_axis=0, concat_axis=0, tiled=True)  17.3 us
    all_to_all x1, blocking collectives, exclusive(): back = lax.all_to_all(sums, CTX, split_axis=0, concat_axis=0, tiled=True)  12.4 us
    all_to_all x1, waiting for transfers between devices, exclusive(): got = lax.all_to_all(pieces, CTX, split_axis=0, concat_axis=0, tiled=True)  11.2 us
    ppermute x6, starting transfers between devices, shift_by_core(): lax.ppermute(value, CTX, [(index(*p), index(*target(*p))) for p in places])  9.18 us
    all_gather x1, waiting for transfers between devices, layer(): lax.all_gather(cotangent, 'head', axis=0, tiled=False)  6.36 us
    unnamed x22, local copies, waits for them, and re-layouts  5.66 us
    all_to_all x1, starting transfers between devices, exclusive(): got = lax.all_to_all(pieces, CTX, split_axis=0, concat_axis=0, tiled=True)  5.32 us
  transfers between devices with their start and end apart: 11, of which 3 were waited for; matrix products, arithmetic and copies ran while one was open for 4% of the time, Pallas kernels for 26%

commit v1 on v0

v1 whole, which is shorter than its diff:
```python
import functools

import jax
import jax.numpy as jnp
from jax import lax
from jax.experimental import pallas as pl
from jax.experimental.pallas import tpu as pltpu
from jax.sharding import Mesh
from jax.sharding import PartitionSpec as P

DH = 128
CTX = ("ctx_0", "ctx_1", "ctx_2")
SCALE = DH ** (-0.5)
EPS = 1e-06
F32, BF16 = jnp.float32, jnp.bfloat16
VMEM = pltpu.VMEM
LIMIT = 20 << 20
SMEM = pltpu.SMEM
STEPS = (0, -1, 1, -2, 2, -3, 3)


def dot(a, b, ca, cb):
    return lax.dot_general(a, b, (((ca,), (cb,)), ((), ())), preferred_element_type=F32)


def call(body, outs, args, flops, scalar=False, scratch=()):
    size = sum(a.size * a.dtype.itemsize for a in args)
    size += sum(o.size * o.dtype.itemsize for o in outs)
    cost = pl.CostEstimate(flops=flops, bytes_accessed=size, transcendentals=0)
    specs = [pl.BlockSpec(memory_space=VMEM)] * len(args)
    if scalar:
        specs[0] = pl.BlockSpec(memory_space=SMEM)
    return pl.pallas_call(
        body,
        out_shape=outs,
        in_specs=specs,
        out_specs=[pl.BlockSpec(memory_space=VMEM)] * len(outs),
        scratch_shapes=list(scratch),
        cost_estimate=cost,
        compiler_params=pltpu.CompilerParams(vmem_limit_bytes=LIMIT),
    )(*args)


def shape(dims, dtype):
    return jax.ShapeDtypeStruct(dims, dtype)


def lower_mask(n):
    return lax.broadcasted_iota(jnp.int32, (n, n), 0) >= lax.broadcasted_iota(jnp.int32, (n, n), 1)


def heads(width):
    return [(b, h, slice(h * DH, (h + 1) * DH)) for b in range(2) for h in range(width // DH)]


def local_states(place, left, right, keep_ref, send_ref):
    mc = place[2]
    for h in range(keep_ref.shape[0]):
        s = slice(h * DH, (h + 1) * DH)
        keep_ref[h] = dot(left[mc, :, s], right[mc, :, s], 0, 0)
        send_ref[h] = dot(left[1 - mc, :, s], right[1 - mc, :, s], 0, 0).astype(BF16)


def state_body(place, k_ref, v_ref, keep_ref, send_ref):
    local_states(place, k_ref, v_ref, keep_ref, send_ref)


def chip_body(keep_ref, got_ref, out_ref):
    out_ref[...] = (keep_ref[...] + got_ref[...].astype(F32)).astype(BF16)


def first_axis_body(reverse, place, t_ref, g1, g2, g3, own_ref, m1, m2, m3):
    rows_first = place[2] == 0
    first = jnp.where(rows_first, place[1], place[0])
    second = jnp.where(rows_first, place[0], place[1])
    chip = t_ref[...].astype(F32)
    every, some = chip, jnp.zeros_like(chip)
    for d, g in ((1, g1), (2, g2), (3, g3)):
        value = g[...].astype(F32)
        every = every + value
        taken = first < d if reverse else first >= d
        some = some + jnp.where(taken, value, 0.0)
    own_ref[...] = some
    base = jnp.where(rows_first, 0.0, some)
    extra = jnp.where(rows_first, every, chip)
    for d, m in ((1, m1), (2, m2), (3, m3)):
        given = second + d >= 4 if reverse else second + d < 4
        m[...] = (base + jnp.where(given, extra, 0.0)).astype(BF16)


def second_axis_body(reverse, place, own_ref, g1, g2, g3, keep_ref, got_ref, out_ref, send_ref):
    total = own_ref[...]
    for g in (g1, g2, g3):
        total = total + g[...].astype(F32)
    late = place[2] == (0 if reverse else 1)
    out_ref[...] = (total + jnp.where(late, got_ref[...].astype(F32), 0.0)).astype(BF16)
    send_ref[...] = (total + jnp.where(late, 0.0, keep_ref[...])).astype(BF16)


def pick_state(place, own_ref, other_ref, b, s):
    h = s.start // DH
    return jnp.where(place[2] == b, own_ref[h], other_ref[h])


def each_batch(width, step):
    def body(b, carry):
        for h in range(width // DH):
            step(b, b * (width // DH) + h, slice(h * DH, (h + 1) * DH))
        return carry

    lax.fori_loop(0, 2, body, 0)


def forward_body(place, q_ref, k_ref, v_ref, so_ref, sr_ref, normed_ref, attended_ref, scores_ref):
    lower = lower_mask(q_ref.shape[1])

    def step(b, i, s):
        q, v = q_ref[b, :, s], v_ref[b, :, s]
        scores = jnp.where(lower, dot(q, k_ref[b, :, s], 1, 1) * SCALE, 0.0).astype(BF16)
        scores_ref[i] = scores
        state = pick_state(place, so_ref, sr_ref, b, s)
        attended = dot(scores, v, 1, 0) + SCALE * dot(q, state, 1, 0)
        attended_ref[b, :, s] = attended
        mean = jnp.mean(attended * attended, axis=-1, keepdims=True)
        normed_ref[b, :, s] = (attended / jnp.sqrt(mean + EPS)).astype(BF16)

    each_batch(q_ref.shape[2], step)


def project_body(n_ref, w_ref, out_ref):
    width = n_ref.shape[1]
    for j in range(out_ref.shape[0]):
        out_ref[j] = dot(n_ref[...], w_ref[:, j * width : (j + 1) * width], 1, 0).astype(BF16)


def half_body(first, x_ref, out_ref):
    out_ref[...] = x_ref[:, first : first + out_ref.shape[1]]


def combine_body(place, o_ref, g1, g2, g3, own_ref, s1, s2, s3):
    me = jnp.where(place[2] == 0, place[0], place[1])
    for d, out in enumerate((own_ref, s1, s2, s3)):
        i = (me + d) % 4
        total = o_ref[i].astype(F32)
        for g in (g1, g2, g3):
            total = total + g[i].astype(F32)
        out[...] = total.astype(out.dtype)


def finish_body(factor, own_ref, g1, g2, g3, out_ref):
    total = own_ref[...]
    for g in (g1, g2, g3):
        total = total + g[...].astype(F32)
    out_ref[...] = total * factor


def owner_of(place, step):
    return (place[3] + step + 8) % 8


def block_dot(place, step, ref, w_ref, first=0):
    width = w_ref.shape[0]
    start = pl.multiple_of(owner_of(place, step) * width + first, DH)
    return dot(ref[...], w_ref[:, pl.ds(start, ref.shape[1])], 1, 1)


def grad_near_body(steps, place, *refs):
    *blocks, w_ref, out_ref = refs
    total = block_dot(place, steps[0], blocks[0], w_ref)
    for step, ref in zip(steps[1:], blocks[1:]):
        total = total + block_dot(place, step, ref, w_ref)
    out_ref[...] = total


def grad_far_body(steps, place, *refs):
    *blocks, r4, l4, w_ref, sum_ref, a_ref, q_ref, ag_ref, keep_ref, send_ref = refs
    rows, width = sum_ref.shape
    total = sum_ref[...]
    for step, ref in zip(steps, blocks):
        total = total + block_dot(place, step, ref, w_ref)
    total = total + block_dot(place, 4, r4, w_ref) + block_dot(place, 4, l4, w_ref, width // 2)
    n = rows // 2
    for b, _, s in heads(width):
        part = slice(b * n, (b + 1) * n)
        a, g = a_ref[b, :, s], total[part, s]
        root = 1.0 / jnp.sqrt(jnp.mean(a * a, axis=-1, keepdims=True) + EPS)
        inner = jnp.mean(g * a, axis=-1, keepdims=True)
        ag_ref[b, :, s] = (g * root - a * (inner * root * root * root)).astype(BF16)
    local_states(place, q_ref, ag_ref, keep_ref, send_ref)


def weight_pieces(steps, place, mc, n_ref, blocks):
    mx, my = place[0], place[1]
    *whole, r4, l4 = blocks
    low = pl.multiple_of(mc * DH, DH)
    high = pl.multiple_of(mc * DH + 2 * DH, DH)
    picks = [(s, ref[:, pl.ds(low, DH)], ref[:, pl.ds(high, DH)]) for s, ref in zip(steps, whole)]
    picks.append((4, r4[:, pl.ds(low, DH)], l4[:, pl.ds(low, DH)]))
    for step, left, right in picks:
        k = owner_of(place, step)
        r = dot(n_ref[...], jnp.concatenate([left, right], axis=1), 0, 0)
        x = k // 2
        for j in range(2):
            y = 2 * (k % 2) + j
            far = jnp.where(mc == 0, (y - my + 4) % 4, (x - mx + 4) % 4)
            yield far, jnp.where(mc == 0, x, y), r[:, j * DH : (j + 1) * DH]


def weight_body(steps, place, n_ref, *refs):
    *blocks, out_ref = refs
    for far, other, piece in weight_pieces(steps, place, 1 - place[2], n_ref, blocks):
        out_ref[far, other] = piece.astype(BF16)


def weight_add_body(steps, place, n_ref, *refs):
    *blocks, in_ref, o0, o1, o2, o3, buf, sem = refs
    for far, other, piece in weight_pieces(steps, place, place[2], n_ref, blocks):
        buf[far, other] = (piece + in_ref[far, other].astype(F32)).astype(BF16)
    copies = [
        pltpu.make_async_copy(buf.at[d], o, sem.at[d]) for d, o in enumerate((o0, o1, o2, o3))
    ]
    for copy in copies:
        copy.start()
    for copy in copies:
        copy.wait()


def backward_body(place, q_ref, k_ref, v_ref, sc_ref, ag_ref, so, sr, go, gr, dq_ref, dk_ref, dv_ref):
    lower = lower_mask(q_ref.shape[1])

    def step(b, i, s):
        q, k, v, ag = q_ref[b, :, s], k_ref[b, :, s], v_ref[b, :, s], ag_ref[b, :, s]
        sg = jnp.where(lower, dot(ag, v, 1, 1) * SCALE, 0.0).astype(BF16)
        earlier, later = pick_state(place, so, sr, b, s), pick_state(place, go, gr, b, s)
        dq_ref[b, :, s] = (dot(sg, k, 1, 0) + SCALE * dot(ag, earlier, 1, 1)).astype(BF16)
        dk_ref[b, :, s] = (dot(sg, q, 0, 0) + SCALE * dot(v, later, 1, 1)).astype(BF16)
        dv_ref[b, :, s] = (dot(sc_ref[i], ag, 0, 0) + SCALE * dot(k, later, 1, 0)).astype(BF16)

    each_batch(q_ref.shape[2], step)


def shift(value, axis, step):
    n = lax.axis_size(axis)
    return lax.ppermute(value, axis, [(i, (i + step) % n) for i in range(n)])


def shift_by_core(value, first, step):
    def target(x, y, c):
        along_y = (c == 0) == first
        return (x, (y + step) % 4, c) if along_y else ((x + step) % 4, y, c)

    def index(x, y, c):
        return (x * 4 + y) * 2 + c

    places = [(x, y, c) for x in range(4) for y in range(4) for c in range(2)]
    return lax.ppermute(value, CTX, [(index(*p), index(*target(*p))) for p in places])


def exclusive(place, keep, send, reverse):
    half, size = keep.shape, keep.size
    got = shift(send, "ctx_2", 1)
    chip = call(chip_body, [shape(half, BF16)], [keep, got], size)[0]
    near = []
    for d in (1, 2, 3):
        near.append(shift_by_core(chip, True, d))
    own, *out = call(
        functools.partial(first_axis_body, reverse),
        [shape(half, F32)] + [shape(half, BF16)] * 3,
        [place, chip, *near],
        size * 10,
        True,
    )
    far = []
    for d in (1, 2, 3):
        far.append(shift_by_core(out[d - 1], False, d))
    mine, other = call(
        functools.partial(second_axis_body, reverse),
        [shape(half, BF16)] * 2,
        [place, own, *far, keep, got],
        size * 8,
        True,
    )
    return mine, shift(other, "ctx_2", 1)


def gather_ring(block):
    near, right, left = [block], block, block
    rows, width = block.shape
    for i in (1, 2, 3, 4):
        if i == 4:
            half = [shape((rows, width // 2), BF16)]
            right = call(functools.partial(half_body, 0), half, [right], 0)[0]
            left = call(functools.partial(half_body, width // 2), half, [left], 0)[0]
        right = shift(right, "head", 1)
        left = shift(left, "head", -1)
        near += [right, left]
    return near


def reduce_weight(place, normed, blocks, factor, after):
    rows, width = normed.shape
    flops = rows * width * width * 8
    grid = (4, 4, width, DH)
    theirs = call(
        functools.partial(weight_body, STEPS),
        [shape(grid, BF16)],
        [place, normed, *blocks],
        flops,
        True,
    )[0]
    theirs = shift(theirs, "ctx_2", 1)
    theirs, _ = lax.optimization_barrier((theirs, after))
    total = call(
        functools.partial(weight_add_body, STEPS),
        [shape(grid[1:], BF16)] * 4,
        [place, normed, *blocks, theirs],
        flops,
        True,
        [VMEM(grid, BF16), pltpu.SemaphoreType.DMA((4,))],
    )
    got = [shift_by_core(total[d], True, d) for d in (1, 2, 3)]
    piece = (width, DH)
    own, *send = call(
        combine_body,
        [shape(piece, F32)] + [shape(piece, BF16)] * 3,
        [place, total[0], *got],
        total[0].size * 4,
        True,
    )
    got = [shift_by_core(send[d - 1], False, d) for d in (1, 2, 3)]
    return call(functools.partial(finish_body, factor), [shape(piece, F32)], [own, *got], own.size * 4)[0]


def layer(queries, key_rows, value_rows, out_weight, cotangent):
    _, length, width = queries.shape
    n_head = lax.axis_size("head")
    rows = 2 * length
    n_mat = 2 * width // DH
    half = (n_mat // 2, DH, DH)
    blocks = gather_ring(cotangent.reshape(rows, width))
    mx, my, mc, mz = (lax.axis_index(a) for a in (*CTX, "head"))
    place = jnp.stack([mx, my, mc, mz]).astype(jnp.int32)
    mat_flops = 2 * n_mat * length * DH * DH
    pair = [shape(half, F32), shape(half, BF16)]
    keep, send = call(state_body, pair, [place, key_rows, value_rows], mat_flops, True)
    state = exclusive(place, keep, send, False)
    normed, attended, scores = call(
        forward_body,
        [shape(queries.shape, BF16), shape(queries.shape, F32), shape((n_mat, length, length), BF16)],
        [place, queries, key_rows, value_rows, *state],
        5 * mat_flops,
        True,
    )
    normed = normed.reshape(rows, width)
    big = 2 * rows * width * width * n_head
    partial = call(project_body, [shape((n_head, rows, width), BF16)], [normed, out_weight], big)[0]
    layer_output = lax.psum_scatter(
        partial.reshape(n_head * rows, width), "head", scatter_dimension=0, tiled=True
    ).reshape(queries.shape)
    part_grad = call(
        functools.partial(grad_near_body, STEPS[:5]),
        [shape((rows, width), F32)],
        [place, *blocks[:5], out_weight],
        big * 5 // 8,
        True,
    )[0]
    attended_grad, keep, send = call(
        functools.partial(grad_far_body, STEPS[5:]),
        [shape(queries.shape, BF16), *pair],
        [place, *blocks[5:], out_weight, part_grad, attended, queries],
        big * 3 // 8,
        True,
    )
    factor = (rows * lax.axis_size(CTX)) ** (-0.5)
    weight_grad = reduce_weight(place, normed, blocks, factor, keep)
    grad_state = exclusive(place, keep, send, True)
    query_grad, key_grad, value_grad = call(
        backward_body,
        [shape(queries.shape, BF16)] * 3,
        [place, queries, key_rows, value_rows, scores, attended_grad, *state, *grad_state],
        10 * mat_flops,
        True,
    )
    return (layer_output, query_grad, key_grad, value_grad, weight_grad)


def solution(mesh):
    split = Mesh(
        mesh.devices.reshape(4, 4, 2, mesh.shape["head"]), ("ctx_0", "ctx_1", "ctx_2", "head")
    )
    rows = P(None, CTX, "head")
    return jax.shard_map(
        layer,
        mesh=split,
        in_specs=(rows, rows, rows, P("head", None), rows),
        out_specs=(rows, rows, rows, rows, P("head", CTX)),
        check_vma=False,
    )
```

time: 130 us -> 175 us (1.35)
  waiting for transfers between devices: 19.5 us -> 85.2 us
  blocking collectives: 29.8 us -> 0 us
  starting transfers between devices: 21.2 us -> 46 us
  Pallas kernels: 33.3 us -> 23.1 us
  other arithmetic: 5.08 us -> 0.08 us
    ppermute x1 -> x13, waiting for transfers between devices: 0.01 us -> 53 us  [shift(): return lax.ppermute(value, axis, [(i, (i + step) % n) for i in range(n)])]
    ppermute x6 -> x18, waiting for transfers between devices: 0.02 us -> 32.1 us  [shift_by_core(): lax.ppermute(value, CTX, [(index(*p), index(*target(*p))) for p in places])]
    all_to_all x2 -> x0, blocking collectives: 29.8 us -> none  [the longest x1 17.3 us: exclusive(): got = lax.all_to_all(pieces, CTX, split_axis=0, concat_axis=0, tiled=True)]
    ppermute x1 -> x13, starting transfers between devices: 1.33 us -> 28.7 us  [shift(): return lax.ppermute(value, axis, [(i, (i + step) % n) for i in range(n)])]
    all_to_all x2 -> x0, waiting for transfers between devices: 12.4 us -> none  [the longest x1 11.2 us: exclusive(): got = lax.all_to_all(pieces, CTX, split_axis=0, concat_axis=0, tiled=True)]
    all_to_all x2 -> x0, starting transfers between devices: 10.6 us -> none  [the longest x1 5.32 us: exclusive(): got = lax.all_to_all(pieces, CTX, split_axis=0, concat_axis=0, tiled=True)]
    pallas_call x9 -> x18, Pallas kernels: 33.3 us -> 23.1 us  [call(): pl.pallas_call(body, out_shape=outs, in_specs=specs, out_specs=[pl.BlockS...]
    ppermute x6 -> x18, starting transfers between devices: 9.18 us -> 17.3 us  [shift_by_core(): lax.ppermute(value, CTX, [(index(*p), index(*target(*p))) for p in places])]
  transfers between devices with their start and end apart: 11 -> 32, of which waited for: 3 -> 21; matrix products, arithmetic and copies ran while one was open for 4% -> 0% of each run, Pallas kernels for 26% -> 9%
where the time goes in v1:
time: 175 us
  waiting for transfers between devices  85.2 us (49%)
  starting transfers between devices  46 us (26%)
  Pallas kernels  23.1 us (13%)
  between operations  14.3 us (8%)
  local copies, waits for them, and re-layouts  6.27 us (4%)
    ppermute x13, waiting for transfers between devices, shift(): return lax.ppermute(value, axis, [(i, (i + step) % n) for i in range(n)])  53 us
    ppermute x18, waiting for transfers between devices, shift_by_core(): lax.ppermute(value, CTX, [(index(*p), index(*target(*p))) for p in places])  32.1 us
    ppermute x13, starting transfers between devices, shift(): return lax.ppermute(value, axis, [(i, (i + step) % n) for i in range(n)])  28.7 us
    pallas_call x18, Pallas kernels, call(): pl.pallas_call(body, out_shape=outs, in_specs=specs, out_specs=[pl.BlockS...  23.1 us
    ppermute x18, starting transfers between devices, shift_by_core(): lax.ppermute(value, CTX, [(index(*p), index(*target(*p))) for p in places])  17.3 us
    unnamed x22, local copies, waits for them, and re-layouts  6.27 us
  transfers between devices with their start and end apart: 32, of which 21 were waited for; matrix products, arithmetic and copies ran while one was open for 0% of the time, Pallas kernels for 9%

profile of v1, /device:TPU:1, one launch (start us, length us, event | category | flops | bytes accessed | tf_op | source)
XLA Modules:
  0.0 174.9 jit_solution(3072887642885091843)
XLA Ops:
  10.5 3.3 %collective-permute-start = (bf16[4,128,128]{2,1,0:T(8,128)(2,1)S(1)}, bf16[4,128,128]{2,1,0:T(8,128)(2,1)S(1)}, u32[]{:S(2)}, u32[]{:S(2)}) collective-permute-start(bf16[4,128,128]{2,1,0:T(8,128)(2,1)S(1)} %get-tuple-element.38), channel_id=1, source_target_pairs={{0,8},{8,0},{1,9},{9,1},{2,10},{10,2},{3,11},{11,3},{4,12},{12,4},... | collective-permute-start | bytes 393224 | tf_op jit(solution)/shard_map/ppermute | solution.py:244
  24.5 2.6 %collective-permute-start.5 = (bf16[4,128,128]{2,1,0:T(8,128)(2,1)S(1)}, bf16[4,128,128]{2,1,0:T(8,128)(2,1)S(1)}, u32[]{:S(2)}, u32[]{:S(2)}) collective-permute-start(bf16[4,128,128]{2,1,0:T(8,128)(2,1)S(1)} %get-tuple-element.41), channel_id=1, source_target_pairs={{0,128},{8,40},{16,144},{24,56},{32,160},{40,8},{48,176},{56,24},{... | collective-permute-start | bytes 393224 | tf_op jit(solution)/shard_map/ppermute | solution.py:256
  28.5 2.4 %collective-permute-done.5.g2 = bf16[4,128,128]{2,1,0:T(8,128)(2,1)S(1)} collective-permute-done((bf16[4,128,128]{2,1,0:T(8,128)(2,1)S(1)}, bf16[4,128,128]{2,1,0:T(8,128)(2,1)S(1)}, u32[]{:S(2)}, u32[]{:S(2)}) %collective-permute-start.5) | collective-permute-done | bytes 131104 | tf_op jit(solution)/shard_map/ppermute | solution.py:256
  31.7 3.5 %collective-permute-start.7 = (bf16[4,128,128]{2,1,0:T(8,128)(2,1)S(1)}, bf16[4,128,128]{2,1,0:T(8,128)(2,1)S(1)}, u32[]{:S(2)}, u32[]{:S(2)}) collective-permute-start(bf16[4,128,128]{2,1,0:T(8,128)(2,1)S(1)} %get-tuple-element.44), channel_id=1, source_target_pairs={{0,8},{8,0},{1,9},{9,1},{2,10},{10,2},{3,11},{11,3},{4,12},{12,4},... | collective-permute-start | bytes 393224 | tf_op jit(solution)/shard_map/ppermute | solution.py:244
  39.1 2.3 %shard_map.96 = (bf16[2,192,512]{2,1,0:T(8,128)(2,1)S(1)}, f32[2,192,512]{2,1,0:T(8,128)S(1)}, bf16[8,192,192]{2,1,0:T(8,128)(2,1)S(1)}) custom-call(s32[4]{0:T(128)S(1)} %pad_add_fusion.place, bf16[2,192,512]{2,1,0:T(8,128)(2,1)S(1)} %copy-done.9, bf16[2,192,512]{2,1,0:T(8,128)(2,1)S(1)} %copy-done.4, bf16[2,192,512]{2,1,0:T(8,128)(2,1)S(1)} %copy-done.7, ...), custom_call_target="tpu_custom_call" | custom-call | flops 251658240 | bytes 3211280 | tf_op jit(solution)/shard_map/pallas_call | solution.py:33
  41.5 3.4 %shard_map.97 = bf16[8,384,512]{2,1,0:T(8,128)(2,1)} custom-call(bf16[384,512]{1,0:T(8,128)(2,1)S(1)} %bitcast.13, bf16[512,4096]{1,0:T(8,128)(2,1)S(1)} %copy-done), custom_call_target="tpu_custom_call" | custom-call | flops 1610612736 | bytes 7733248 | tf_op jit(solution)/shard_map/pallas_call | solution.py:33
  45.9 5.6 %collective-permute-start.11 = (bf16[384,512]{1,0:T(8,128)(2,1)S(1)}, bf16[384,512]{1,0:T(8,128)(2,1)S(1)}, u32[]{:S(2)}, u32[]{:S(2)}) collective-permute-start(bf16[384,512]{1,0:T(8,128)(2,1)S(1)} %bitcast.8), channel_id=1, source_target_pairs={{0,7},{1,0},{2,1},{3,2},{4,3},{5,4},{6,5},{7,6},{8,15},{9,8},{10,9... | collective-permute-start | bytes 1179656 | tf_op jit(solution)/shard_map/ppermute | solution.py:244
  51.5 11.5 %collective-permute-done.11.refs_2_ = bf16[384,512]{1,0:T(8,128)(2,1)S(1)} collective-permute-done((bf16[384,512]{1,0:T(8,128)(2,1)S(1)}, bf16[384,512]{1,0:T(8,128)(2,1)S(1)}, u32[]{:S(2)}, u32[]{:S(2)}) %collective-permute-start.11) | collective-permute-done | bytes 393248 | tf_op jit(solution)/shard_map/ppermute | solution.py:244
  62.9 3.5 %collective-permute-start.12 = (bf16[384,512]{1,0:T(8,128)(2,1)S(1)}, bf16[384,512]{1,0:T(8,128)(2,1)S(1)}, u32[]{:S(2)}, u32[]{:S(2)}) collective-permute-start(bf16[384,512]{1,0:T(8,128)(2,1)S(1)} %collective-permute-done.11.refs_2_), channel_id=1, source_target_pairs={{0,7},{1,0},{2,1},{3,2},{4,3},{5,4},{6,5},{7,6},{8,15},{9,8},{10,9... | collective-permute-start | bytes 1179656 | tf_op jit(solution)/shard_map/ppermute | solution.py:244
  66.4 15.4 %collective-permute-done.12.refs_4_ = bf16[384,512]{1,0:T(8,128)(2,1)S(1)} collective-permute-done((bf16[384,512]{1,0:T(8,128)(2,1)S(1)}, bf16[384,512]{1,0:T(8,128)(2,1)S(1)}, u32[]{:S(2)}, u32[]{:S(2)}) %collective-permute-start.12) | collective-permute-done | bytes 393248 | tf_op jit(solution)/shard_map/ppermute | solution.py:244
  81.8 3.5 %collective-permute-start.13 = (bf16[384,512]{1,0:T(8,128)(2,1)S(1)}, bf16[384,512]{1,0:T(8,128)(2,1)S(1)}, u32[]{:S(2)}, u32[]{:S(2)}) collective-permute-start(bf16[384,512]{1,0:T(8,128)(2,1)S(1)} %collective-permute-done.12.refs_4_), channel_id=1, source_target_pairs={{0,7},{1,0},{2,1},{3,2},{4,3},{5,4},{6,5},{7,6},{8,15},{9,8},{10,9... | collective-permute-start | bytes 1179656 | tf_op jit(solution)/shard_map/ppermute | solution.py:244
  86.3 15.1 %collective-permute-done.13.x_ref.refs_1_.refs_6_ = bf16[384,512]{1,0:T(8,128)(2,1)S(1)} collective-permute-done((bf16[384,512]{1,0:T(8,128)(2,1)S(1)}, bf16[384,512]{1,0:T(8,128)(2,1)S(1)}, u32[]{:S(2)}, u32[]{:S(2)}) %collective-permute-start.13) | collective-permute-done | bytes 393248 | tf_op jit(solution)/shard_map/ppermute | solution.py:244
  101.4 3.6 %collective-permute-start.15 = (bf16[384,256]{1,0:T(8,128)(2,1)S(1)}, bf16[384,256]{1,0:T(8,128)(2,1)S(1)}, u32[]{:S(2)}, u32[]{:S(2)}) collective-permute-start(bf16[384,256]{1,0:T(8,128)(2,1)S(1)} %shard_map.99), channel_id=1, source_target_pairs={{0,7},{1,0},{2,1},{3,2},{4,3},{5,4},{6,5},{7,6},{8,15},{9,8},{10,9... | collective-permute-start | bytes 589832 | tf_op jit(solution)/shard_map/ppermute | solution.py:244
  106.1 2.8 %collective-permute-done.15.refs_3_.refs_8_ = bf16[384,256]{1,0:T(8,128)(2,1)S(1)} collective-permute-done((bf16[384,256]{1,0:T(8,128)(2,1)S(1)}, bf16[384,256]{1,0:T(8,128)(2,1)S(1)}, u32[]{:S(2)}, u32[]{:S(2)}) %collective-permute-start.15) | collective-permute-done | bytes 196640 | tf_op jit(solution)/shard_map/ppermute | solution.py:244
  108.9 3.1 %collective-permute-done.14.refs_2_.refs_7_ = bf16[384,256]{1,0:T(8,128)(2,1)S(1)} collective-permute-done((bf16[384,256]{1,0:T(8,128)(2,1)S(1)}, bf16[384,256]{1,0:T(8,128)(2,1)S(1)}, u32[]{:S(2)}, u32[]{:S(2)}) %collective-permute-start.14) | collective-permute-done | bytes 196640 | tf_op jit(solution)/shard_map/ppermute | solution.py:244
  113.9 5.4 %collective-permute-start.24 = (bf16[4,4,512,128]{3,2,1,0:T(8,128)(2,1)S(1)}, bf16[4,4,512,128]{3,2,1,0:T(8,128)(2,1)S(1)}, u32[]{:S(2)}, u32[]{:S(2)}) collective-permute-start(bf16[4,4,512,128]{3,2,1,0:T(8,128)(2,1)S(1)} %shard_map.106), channel_id=1, source_target_pairs={{0,8},{8,0},{1,9},{9,1},{2,10},{10,2},{3,11},{11,3},{4,12},{12,4},... | collective-permute-start | bytes 6291464 | tf_op jit(solution)/shard_map/ppermute | solution.py:244
  124.5 2.4 %collective-permute-start.19 = (bf16[4,128,128]{2,1,0:T(8,128)(2,1)S(1)}, bf16[4,128,128]{2,1,0:T(8,128)(2,1)S(1)}, u32[]{:S(2)}, u32[]{:S(2)}) collective-permute-start(bf16[4,128,128]{2,1,0:T(8,128)(2,1)S(1)} %shard_map.102.t_ref), channel_id=1, source_target_pairs={{0,48},{8,200},{16,0},{24,216},{32,16},{40,232},{48,32},{56,248},{... | collective-permute-start | bytes 393224 | tf_op jit(solution)/shard_map/ppermute | solution.py:256
  131.9 2.4 %collective-permute-start.18 = (bf16[4,128,128]{2,1,0:T(8,128)(2,1)S(1)}, bf16[4,128,128]{2,1,0:T(8,128)(2,1)S(1)}, u32[]{:S(2)}, u32[]{:S(2)}) collective-permute-start(bf16[4,128,128]{2,1,0:T(8,128)(2,1)S(1)} %shard_map.102.t_ref), channel_id=1, source_target_pairs={{0,32},{8,136},{16,48},{24,152},{32,0},{40,168},{48,16},{56,184},{... | collective-permute-start | bytes 393224 | tf_op jit(solution)/shard_map/ppermute | solution.py:256
  134.3 9.8 %collective-permute-done.18.g2 = bf16[4,128,128]{2,1,0:T(8,128)(2,1)S(1)} collective-permute-done((bf16[4,128,128]{2,1,0:T(8,128)(2,1)S(1)}, bf16[4,128,128]{2,1,0:T(8,128)(2,1)S(1)}, u32[]{:S(2)}, u32[]{:S(2)}) %collective-permute-start.18) | collective-permute-done | bytes 131104 | tf_op jit(solution)/shard_map/ppermute | solution.py:256
  144.1 2.8 %collective-permute-done.17.g1 = bf16[4,128,128]{2,1,0:T(8,128)(2,1)S(1)} collective-permute-done((bf16[4,128,128]{2,1,0:T(8,128)(2,1)S(1)}, bf16[4,128,128]{2,1,0:T(8,128)(2,1)S(1)}, u32[]{:S(2)}, u32[]{:S(2)}) %collective-permute-start.17) | collective-permute-done | bytes 131104 | tf_op jit(solution)/shard_map/ppermute | solution.py:256
  147.8 6.6 %collective-permute-done.20.g1 = bf16[4,128,128]{2,1,0:T(8,128)(2,1)S(1)} collective-permute-done((bf16[4,128,128]{2,1,0:T(8,128)(2,1)S(1)}, bf16[4,128,128]{2,1,0:T(8,128)(2,1)S(1)}, u32[]{:S(2)}, u32[]{:S(2)}) %collective-permute-start.20) | collective-permute-done | bytes 131104 | tf_op jit(solution)/shard_map/ppermute | solution.py:256
  154.4 3.8 %collective-permute-done.22.g3 = bf16[4,128,128]{2,1,0:T(8,128)(2,1)S(1)} collective-permute-done((bf16[4,128,128]{2,1,0:T(8,128)(2,1)S(1)}, bf16[4,128,128]{2,1,0:T(8,128)(2,1)S(1)}, u32[]{:S(2)}, u32[]{:S(2)}) %collective-permute-start.22) | collective-permute-done | bytes 131104 | tf_op jit(solution)/shard_map/ppermute | solution.py:256
  160.2 2.3 %collective-permute-start.29 = (bf16[512,128]{1,0:T(8,128)(2,1)S(1)}, bf16[512,128]{1,0:T(8,128)(2,1)S(1)}, u32[]{:S(2)}, u32[]{:S(2)}) collective-permute-start(bf16[512,128]{1,0:T(8,128)(2,1)S(1)} %get-tuple-element.67), channel_id=1, source_target_pairs={{0,128},{8,40},{16,144},{24,56},{32,160},{40,8},{48,176},{56,24},{... | collective-permute-start | bytes 393224 | tf_op jit(solution)/shard_map/ppermute | solution.py:256
  162.7 4.2 %shard_map.105 = (bf16[2,192,512]{2,1,0:T(8,128)(2,1)}, bf16[2,192,512]{2,1,0:T(8,128)(2,1)}, bf16[2,192,512]{2,1,0:T(8,128)(2,1)}) custom-call(s32[4]{0:T(128)S(1)} %pad_add_fusion.place, bf16[2,192,512]{2,1,0:T(8,128)(2,1)S(1)} %copy-done.10, bf16[2,192,512]{2,1,0:T(8,128)(2,1)S(1)} %copy-done.5, bf16[2,192,512]{2,1,0:T(8,128)(2,1)S(1)} %copy-done.8, ...), custom_call_target="tpu_custom_call" | custom-call | flops 503316480 | bytes 3866640 | tf_op jit(solution)/shard_map/pallas_call | solution.py:33
  (82 shorter events, 39.4 us)
Async XLA Ops:
  7.2 160.9 %reduce-scatter.2.cloned.1.call-start = ((), (), s32[]{:S(2)}) async-start(), calls=%async_computation.1 | async-start | bytes 3538944 | tf_op jit(solution)/shard_map/reduce_scatter | solution.py:357
  15.6 5.6 %collective-permute-start.2 = (bf16[4,128,128]{2,1,0:T(8,128)(2,1)S(1)}, bf16[4,128,128]{2,1,0:T(8,128)(2,1)S(1)}, u32[]{:S(2)}, u32[]{:S(2)}) collective-permute-start(bf16[4,128,128]{2,1,0:T(8,128)(2,1)S(1)} %shard_map.93.t_ref), channel_id=1, source_target_pairs={{0,32},{8,136},{16,48},{24,152},{32,0},{40,168},{48,16},{56,184},{... | collective-permute-start | bytes 393224 | tf_op jit(solution)/shard_map/ppermute | solution.py:256
  16.1 6.5 %collective-permute-start.1 = (bf16[4,128,128]{2,1,0:T(8,128)(2,1)S(1)}, bf16[4,128,128]{2,1,0:T(8,128)(2,1)S(1)}, u32[]{:S(2)}, u32[]{:S(2)}) collective-permute-start(bf16[4,128,128]{2,1,0:T(8,128)(2,1)S(1)} %shard_map.93.t_ref), channel_id=1, source_target_pairs={{0,16},{8,72},{16,32},{24,88},{32,48},{40,104},{48,0},{56,120},{64... | collective-permute-start | bytes 393224 | tf_op jit(solution)/shard_map/ppermute | solution.py:256
  23.4 5.1 %collective-permute-start.4 = (bf16[4,128,128]{2,1,0:T(8,128)(2,1)S(1)}, bf16[4,128,128]{2,1,0:T(8,128)(2,1)S(1)}, u32[]{:S(2)}, u32[]{:S(2)}) collective-permute-start(bf16[4,128,128]{2,1,0:T(8,128)(2,1)S(1)} %get-tuple-element.40), channel_id=1, source_target_pairs={{0,64},{8,24},{16,80},{24,40},{32,96},{40,56},{48,112},{56,8},{64,... | collective-permute-start | bytes 393224 | tf_op jit(solution)/shard_map/ppermute | solution.py:256
  24.5 6.4 %collective-permute-start.5 = (bf16[4,128,128]{2,1,0:T(8,128)(2,1)S(1)}, bf16[4,128,128]{2,1,0:T(8,128)(2,1)S(1)}, u32[]{:S(2)}, u32[]{:S(2)}) collective-permute-start(bf16[4,128,128]{2,1,0:T(8,128)(2,1)S(1)} %get-tuple-element.41), channel_id=1, source_target_pairs={{0,128},{8,40},{16,144},{24,56},{32,160},{40,8},{48,176},{56,24},{... | collective-permute-start | bytes 393224 | tf_op jit(solution)/shard_map/ppermute | solution.py:256
  45.9 17.0 %collective-permute-start.11 = (bf16[384,512]{1,0:T(8,128)(2,1)S(1)}, bf16[384,512]{1,0:T(8,128)(2,1)S(1)}, u32[]{:S(2)}, u32[]{:S(2)}) collective-permute-start(bf16[384,512]{1,0:T(8,128)(2,1)S(1)} %bitcast.8), channel_id=1, source_target_pairs={{0,7},{1,0},{2,1},{3,2},{4,3},{5,4},{6,5},{7,6},{8,15},{9,8},{10,9... | collective-permute-start | bytes 1179656 | tf_op jit(solution)/shard_map/ppermute | solution.py:244
  51.5 15.0 %collective-permute-start.8 = (bf16[384,512]{1,0:T(8,128)(2,1)S(1)}, bf16[384,512]{1,0:T(8,128)(2,1)S(1)}, u32[]{:S(2)}, u32[]{:S(2)}) collective-permute-start(bf16[384,512]{1,0:T(8,128)(2,1)S(1)} %bitcast.9), channel_id=1, source_target_pairs={{0,1},{1,2},{2,3},{3,4},{4,5},{5,6},{6,7},{7,0},{8,9},{9,10},{10,1... | collective-permute-start | bytes 1179656 | tf_op jit(solution)/shard_map/ppermute | solution.py:244
  62.9 18.9 %collective-permute-start.12 = (bf16[384,512]{1,0:T(8,128)(2,1)S(1)}, bf16[384,512]{1,0:T(8,128)(2,1)S(1)}, u32[]{:S(2)}, u32[]{:S(2)}) collective-permute-start(bf16[384,512]{1,0:T(8,128)(2,1)S(1)} %collective-permute-done.11.refs_2_), channel_id=1, source_target_pairs={{0,7},{1,0},{2,1},{3,2},{4,3},{5,4},{6,5},{7,6},{8,15},{9,8},{10,9... | collective-permute-start | bytes 1179656 | tf_op jit(solution)/shard_map/ppermute | solution.py:244
  66.4 19.9 %collective-permute-start.9 = (bf16[384,512]{1,0:T(8,128)(2,1)S(1)}, bf16[384,512]{1,0:T(8,128)(2,1)S(1)}, u32[]{:S(2)}, u32[]{:S(2)}) collective-permute-start(bf16[384,512]{1,0:T(8,128)(2,1)S(1)} %collective-permute-done.8.refs_1_), channel_id=1, source_target_pairs={{0,1},{1,2},{2,3},{3,4},{4,5},{5,6},{6,7},{7,0},{8,9},{9,10},{10,1... | collective-permute-start | bytes 1179656 | tf_op jit(solution)/shard_map/ppermute | solution.py:244
  81.8 19.6 %collective-permute-start.13 = (bf16[384,512]{1,0:T(8,128)(2,1)S(1)}, bf16[384,512]{1,0:T(8,128)(2,1)S(1)}, u32[]{:S(2)}, u32[]{:S(2)}) collective-permute-start(bf16[384,512]{1,0:T(8,128)(2,1)S(1)} %collective-permute-done.12.refs_4_), channel_id=1, source_target_pairs={{0,7},{1,0},{2,1},{3,2},{4,3},{5,4},{6,5},{7,6},{8,15},{9,8},{10,9... | collective-permute-start | bytes 1179656 | tf_op jit(solution)/shard_map/ppermute | solution.py:244
  86.3 19.7 %collective-permute-start.10 = (bf16[384,512]{1,0:T(8,128)(2,1)S(1)}, bf16[384,512]{1,0:T(8,128)(2,1)S(1)}, u32[]{:S(2)}, u32[]{:S(2)}) collective-permute-start(bf16[384,512]{1,0:T(8,128)(2,1)S(1)} %collective-permute-done.9.refs_3_), channel_id=1, source_target_pairs={{0,1},{1,2},{2,3},{3,4},{4,5},{5,6},{6,7},{7,0},{8,9},{9,10},{10,1... | collective-permute-start | bytes 1179656 | tf_op jit(solution)/shard_map/ppermute | solution.py:244
  101.4 7.4 %collective-permute-start.15 = (bf16[384,256]{1,0:T(8,128)(2,1)S(1)}, bf16[384,256]{1,0:T(8,128)(2,1)S(1)}, u32[]{:S(2)}, u32[]{:S(2)}) collective-permute-start(bf16[384,256]{1,0:T(8,128)(2,1)S(1)} %shard_map.99), channel_id=1, source_target_pairs={{0,7},{1,0},{2,1},{3,2},{4,3},{5,4},{6,5},{7,6},{8,15},{9,8},{10,9... | collective-permute-start | bytes 589832 | tf_op jit(solution)/shard_map/ppermute | solution.py:244
  106.0 5.9 %collective-permute-start.14 = (bf16[384,256]{1,0:T(8,128)(2,1)S(1)}, bf16[384,256]{1,0:T(8,128)(2,1)S(1)}, u32[]{:S(2)}, u32[]{:S(2)}) collective-permute-start(bf16[384,256]{1,0:T(8,128)(2,1)S(1)} %shard_map.98), channel_id=1, source_target_pairs={{0,1},{1,2},{2,3},{3,4},{4,5},{5,6},{6,7},{7,0},{8,9},{9,10},{10,1... | collective-permute-start | bytes 589832 | tf_op jit(solution)/shard_map/ppermute | solution.py:244
  113.9 13.0 %collective-permute-start.24 = (bf16[4,4,512,128]{3,2,1,0:T(8,128)(2,1)S(1)}, bf16[4,4,512,128]{3,2,1,0:T(8,128)(2,1)S(1)}, u32[]{:S(2)}, u32[]{:S(2)}) collective-permute-start(bf16[4,4,512,128]{3,2,1,0:T(8,128)(2,1)S(1)} %shard_map.106), channel_id=1, source_target_pairs={{0,8},{8,0},{1,9},{9,1},{2,10},{10,2},{3,11},{11,3},{4,12},{12,4},... | collective-permute-start | bytes 6291464 | tf_op jit(solution)/shard_map/ppermute | solution.py:244
  124.5 9.7 %collective-permute-start.19 = (bf16[4,128,128]{2,1,0:T(8,128)(2,1)S(1)}, bf16[4,128,128]{2,1,0:T(8,128)(2,1)S(1)}, u32[]{:S(2)}, u32[]{:S(2)}) collective-permute-start(bf16[4,128,128]{2,1,0:T(8,128)(2,1)S(1)} %shard_map.102.t_ref), channel_id=1, source_target_pairs={{0,48},{8,200},{16,0},{24,216},{32,16},{40,232},{48,32},{56,248},{... | collective-permute-start | bytes 393224 | tf_op jit(solution)/shard_map/ppermute | solution.py:256
  129.1 29.9 %collective-permute-start.25 = (bf16[4,512,128]{2,1,0:T(8,128)(2,1)S(1)}, bf16[4,512,128]{2,1,0:T(8,128)(2,1)S(1)}, u32[]{:S(2)}, u32[]{:S(2)}) collective-permute-start(bf16[4,512,128]{2,1,0:T(8,128)(2,1)S(1)} %get-tuple-element.62), channel_id=1, source_target_pairs={{0,16},{8,72},{16,32},{24,88},{32,48},{40,104},{48,0},{56,120},{64... | collective-permute-start | bytes 1572872 | tf_op jit(solution)/shard_map/ppermute | solution.py:256
  129.2 29.8 %collective-permute-start.26 = (bf16[4,512,128]{2,1,0:T(8,128)(2,1)S(1)}, bf16[4,512,128]{2,1,0:T(8,128)(2,1)S(1)}, u32[]{:S(2)}, u32[]{:S(2)}) collective-permute-start(bf16[4,512,128]{2,1,0:T(8,128)(2,1)S(1)} %get-tuple-element.63), channel_id=1, source_target_pairs={{0,32},{8,136},{16,48},{24,152},{32,0},{40,168},{48,16},{56,184},{... | collective-permute-start | bytes 1572872 | tf_op jit(solution)/shard_map/ppermute | solution.py:256
  130.4 28.6 %collective-permute-start.27 = (bf16[4,512,128]{2,1,0:T(8,128)(2,1)S(1)}, bf16[4,512,128]{2,1,0:T(8,128)(2,1)S(1)}, u32[]{:S(2)}, u32[]{:S(2)}) collective-permute-start(bf16[4,512,128]{2,1,0:T(8,128)(2,1)S(1)} %get-tuple-element.64), channel_id=1, source_target_pairs={{0,48},{8,200},{16,0},{24,216},{32,16},{40,232},{48,32},{56,248},{... | collective-permute-start | bytes 1572872 | tf_op jit(solution)/shard_map/ppermute | solution.py:256
  131.9 12.2 %collective-permute-start.18 = (bf16[4,128,128]{2,1,0:T(8,128)(2,1)S(1)}, bf16[4,128,128]{2,1,0:T(8,128)(2,1)S(1)}, u32[]{:S(2)}, u32[]{:S(2)}) collective-permute-start(bf16[4,128,128]{2,1,0:T(8,128)(2,1)S(1)} %shard_map.102.t_ref), channel_id=1, source_target_pairs={{0,32},{8,136},{16,48},{24,152},{32,0},{40,168},{48,16},{56,184},{... | collective-permute-start | bytes 393224 | tf_op jit(solution)/shard_map/ppermute | solution.py:256
  134.2 12.6 %collective-permute-start.17 = (bf16[4,128,128]{2,1,0:T(8,128)(2,1)S(1)}, bf16[4,128,128]{2,1,0:T(8,128)(2,1)S(1)}, u32[]{:S(2)}, u32[]{:S(2)}) collective-permute-start(bf16[4,128,128]{2,1,0:T(8,128)(2,1)S(1)} %shard_map.102.t_ref), channel_id=1, source_target_pairs={{0,16},{8,72},{16,32},{24,88},{32,48},{40,104},{48,0},{56,120},{64... | collective-permute-start | bytes 393224 | tf_op jit(solution)/shard_map/ppermute | solution.py:256
  147.6 6.8 %collective-permute-start.20 = (bf16[4,128,128]{2,1,0:T(8,128)(2,1)S(1)}, bf16[4,128,128]{2,1,0:T(8,128)(2,1)S(1)}, u32[]{:S(2)}, u32[]{:S(2)}) collective-permute-start(bf16[4,128,128]{2,1,0:T(8,128)(2,1)S(1)} %get-tuple-element.52), channel_id=1, source_target_pairs={{0,64},{8,24},{16,80},{24,40},{32,96},{40,56},{48,112},{56,8},{64,... | collective-permute-start | bytes 393224 | tf_op jit(solution)/shard_map/ppermute | solution.py:256
  147.7 6.7 %collective-permute-start.21 = (bf16[4,128,128]{2,1,0:T(8,128)(2,1)S(1)}, bf16[4,128,128]{2,1,0:T(8,128)(2,1)S(1)}, u32[]{:S(2)}, u32[]{:S(2)}) collective-permute-start(bf16[4,128,128]{2,1,0:T(8,128)(2,1)S(1)} %get-tuple-element.53), channel_id=1, source_target_pairs={{0,128},{8,40},{16,144},{24,56},{32,160},{40,8},{48,176},{56,24},{... | collective-permute-start | bytes 393224 | tf_op jit(solution)/shard_map/ppermute | solution.py:256
  159.8 7.1 %collective-permute-start.28 = (bf16[512,128]{1,0:T(8,128)(2,1)S(1)}, bf16[512,128]{1,0:T(8,128)(2,1)S(1)}, u32[]{:S(2)}, u32[]{:S(2)}) collective-permute-start(bf16[512,128]{1,0:T(8,128)(2,1)S(1)} %get-tuple-element.66), channel_id=1, source_target_pairs={{0,64},{8,24},{16,80},{24,40},{32,96},{40,56},{48,112},{56,8},{64,... | collective-permute-start | bytes 393224 | tf_op jit(solution)/shard_map/ppermute | solution.py:256
  160.2 6.7 %collective-permute-start.29 = (bf16[512,128]{1,0:T(8,128)(2,1)S(1)}, bf16[512,128]{1,0:T(8,128)(2,1)S(1)}, u32[]{:S(2)}, u32[]{:S(2)}) collective-permute-start(bf16[512,128]{1,0:T(8,128)(2,1)S(1)} %get-tuple-element.67), channel_id=1, source_target_pairs={{0,128},{8,40},{16,144},{24,56},{32,160},{40,8},{48,176},{56,24},{... | collective-permute-start | bytes 393224 | tf_op jit(solution)/shard_map/ppermute | solution.py:256
  (19 other events, 163.5 us)
Sparse Core Ops, SparseCore 0:
  45.0 66.0 reduce-scatter.1

commit v2 on v1

--- a/solution.py
+++ b/solution.py
@@ -49,10 +49,6 @@
     return lax.broadcasted_iota(jnp.int32, (n, n), 0) >= lax.broadcasted_iota(jnp.int32, (n, n), 1)
 
 
-def heads(width):
-    return [(b, h, slice(h * DH, (h + 1) * DH)) for b in range(2) for h in range(width // DH)]
-
-
 def local_states(place, left, right, keep_ref, send_ref):
     mc = place[2]
     for h in range(keep_ref.shape[0]):
@@ -61,8 +57,10 @@
         send_ref[h] = dot(left[1 - mc, :, s], right[1 - mc, :, s], 0, 0).astype(BF16)
 
 
-def state_body(place, k_ref, v_ref, keep_ref, send_ref):
+def state_body(place, k_ref, v_ref, keep_ref, send_ref, k_out, v_out):
     local_states(place, k_ref, v_ref, keep_ref, send_ref)
+    k_out[...] = k_ref[...]
+    v_out[...] = v_ref[...]
 
 
 def chip_body(keep_ref, got_ref, out_ref):
@@ -97,53 +95,67 @@
     send_ref[...] = (total + jnp.where(late, 0.0, keep_ref[...])).astype(BF16)
 
 
-def pick_state(place, own_ref, other_ref, b, s):
-    h = s.start // DH
+def pick_state(place, own_ref, other_ref, b, h):
     return jnp.where(place[2] == b, own_ref[h], other_ref[h])
 
 
-def each_batch(width, step):
-    def body(b, carry):
-        for h in range(width // DH):
-            step(b, b * (width // DH) + h, slice(h * DH, (h + 1) * DH))
+def each_head(width, step):
+    n = width // DH
+
+    def body(i, carry):
+        for j in range(2):
+            b, h = i // (n // 2), 2 * (i % (n // 2)) + j
+            step(b, h, b * n + h, pl.ds(pl.multiple_of(h * DH, DH), DH))
         return carry
 
-    lax.fori_loop(0, 2, body, 0)
-
-
-def forward_body(place, q_ref, k_ref, v_ref, so_ref, sr_ref, normed_ref, attended_ref, scores_ref):
+    lax.fori_loop(0, n, body, 0)
+
+
+def intra_body(q_ref, k_ref, v_ref, scores_ref, intra_ref, q_out):
+    q_out[...] = q_ref[...]
     lower = lower_mask(q_ref.shape[1])
 
-    def step(b, i, s):
-        q, v = q_ref[b, :, s], v_ref[b, :, s]
-        scores = jnp.where(lower, dot(q, k_ref[b, :, s], 1, 1) * SCALE, 0.0).astype(BF16)
+    def step(b, h, i, s):
+        raw = dot(q_ref[b, :, s], k_ref[b, :, s], 1, 1) * SCALE
+        scores = jnp.where(lower, raw, 0.0).astype(BF16)
         scores_ref[i] = scores
-        state = pick_state(place, so_ref, sr_ref, b, s)
-        attended = dot(scores, v, 1, 0) + SCALE * dot(q, state, 1, 0)
+        intra_ref[b, :, s] = dot(scores, v_ref[b, :, s], 1, 0)
+
+    each_head(q_ref.shape[2], step)
+
+
+def forward_body(place, q_ref, intra_ref, so_ref, sr_ref, normed_ref, attended_ref):
+    def step(b, h, i, s):
+        state = pick_state(place, so_ref, sr_ref, b, h)
+        attended = intra_ref[b, :, s] + SCALE * dot(q_ref[b, :, s], state, 1, 0)
         attended_ref[b, :, s] = attended
         mean = jnp.mean(attended * attended, axis=-1, keepdims=True)
         normed_ref[b, :, s] = (attended / jnp.sqrt(mean + EPS)).astype(BF16)
 
-    each_batch(q_ref.shape[2], step)
+    each_head(q_ref.shape[2], step)
 
 
 def project_body(n_ref, w_ref, out_ref):
     width = n_ref.shape[1]
-    for j in range(out_ref.shape[0]):
-        out_ref[j] = dot(n_ref[...], w_ref[:, j * width : (j + 1) * width], 1, 0).astype(BF16)
+
+    def body(i, carry):
+        for j in (2 * i, 2 * i + 1):
+            cols = pl.ds(pl.multiple_of(j * width, width), width)
+            out_ref[j] = dot(n_ref[...], w_ref[:, cols], 1, 0).astype(BF16)
+        return carry
+
+    lax.fori_loop(0, out_ref.shape[0] // 2, body, 0)
 
 
 def half_body(first, x_ref, out_ref):
     out_ref[...] = x_ref[:, first : first + out_ref.shape[1]]
 
 
-def combine_body(place, o_ref, g1, g2, g3, own_ref, s1, s2, s3):
+def combine_body(place, o_ref, g1, g2, own_ref, s1, s2, s3):
     me = jnp.where(place[2] == 0, place[0], place[1])
     for d, out in enumerate((own_ref, s1, s2, s3)):
         i = (me + d) % 4
-        total = o_ref[i].astype(F32)
-        for g in (g1, g2, g3):
-            total = total + g[i].astype(F32)
+        total = o_ref[i].astype(F32) + g1[i].astype(F32) + g2[i].astype(F32)
         out[...] = total.astype(out.dtype)
 
 
@@ -172,71 +184,105 @@
     out_ref[...] = total
 
 
-def grad_far_body(steps, place, *refs):
-    *blocks, r4, l4, w_ref, sum_ref, a_ref, q_ref, ag_ref, keep_ref, send_ref = refs
-    rows, width = sum_ref.shape
-    total = sum_ref[...]
-    for step, ref in zip(steps, blocks):
-        total = total + block_dot(place, step, ref, w_ref)
-    total = total + block_dot(place, 4, r4, w_ref) + block_dot(place, 4, l4, w_ref, width // 2)
-    n = rows // 2
-    for b, _, s in heads(width):
-        part = slice(b * n, (b + 1) * n)
-        a, g = a_ref[b, :, s], total[part, s]
+def grad_far_body(place, *refs):
+    r4, l4, w_ref, sum_ref, a_ref, q_ref, ag_ref, keep_ref, send_ref, acc = refs
+    _, width = sum_ref.shape
+    half = block_dot(place, 4, r4, w_ref) + block_dot(place, 4, l4, w_ref, width // 2)
+    acc[...] = (sum_ref[...] + half).reshape(acc.shape)
+
+    def step(b, h, i, s):
+        a, g = a_ref[b, :, s], acc[b, :, s]
         root = 1.0 / jnp.sqrt(jnp.mean(a * a, axis=-1, keepdims=True) + EPS)
         inner = jnp.mean(g * a, axis=-1, keepdims=True)
         ag_ref[b, :, s] = (g * root - a * (inner * root * root * root)).astype(BF16)
+
+    each_head(width, step)
     local_states(place, q_ref, ag_ref, keep_ref, send_ref)
 
 
-def weight_pieces(steps, place, mc, n_ref, blocks):
+def weight_tiles(place, mc, step):
     mx, my = place[0], place[1]
-    *whole, r4, l4 = blocks
-    low = pl.multiple_of(mc * DH, DH)
-    high = pl.multiple_of(mc * DH + 2 * DH, DH)
-    picks = [(s, ref[:, pl.ds(low, DH)], ref[:, pl.ds(high, DH)]) for s, ref in zip(steps, whole)]
-    picks.append((4, r4[:, pl.ds(low, DH)], l4[:, pl.ds(low, DH)]))
-    for step, left, right in picks:
-        k = owner_of(place, step)
-        r = dot(n_ref[...], jnp.concatenate([left, right], axis=1), 0, 0)
-        x = k // 2
-        for j in range(2):
-            y = 2 * (k % 2) + j
-            far = jnp.where(mc == 0, (y - my + 4) % 4, (x - mx + 4) % 4)
-            yield far, jnp.where(mc == 0, x, y), r[:, j * DH : (j + 1) * DH]
-
-
-def weight_body(steps, place, n_ref, *refs):
+    k = owner_of(place, step)
+    x = k // 2
+    for j in range(2):
+        y = 2 * (k % 2) + j
+        far = jnp.where(mc == 0, (y - my + 4) % 4, (x - mx + 4) % 4)
+        yield far, jnp.where(mc == 0, x, y)
+
+
+def weight_pair(mc, n_ref, left, right, left_at, right_at):
+    low = pl.multiple_of(mc * DH + left_at, DH)
+    high = pl.multiple_of(mc * DH + right_at, DH)
+    both = jnp.concatenate([left[:, pl.ds(low, DH)], right[:, pl.ds(high, DH)]], axis=1)
+    r = dot(n_ref[...], both, 0, 0)
+    return r[:, :DH], r[:, DH:]
+
+
+def weight_near_body(steps, place, n_ref, *refs):
     *blocks, out_ref = refs
-    for far, other, piece in weight_pieces(steps, place, 1 - place[2], n_ref, blocks):
-        out_ref[far, other] = piece.astype(BF16)
+    mc = 1 - place[2]
+    for step, ref in zip(steps, blocks):
+        pieces = weight_pair(mc, n_ref, ref, ref, 0, 2 * DH)
+        for (far, other), piece in zip(weight_tiles(place, mc, step), pieces):
+            out_ref[far, other] = piece.astype(BF16)
+    for far, other in weight_tiles(place, mc, 4):
+        out_ref[far, other] = jnp.zeros(out_ref.shape[2:], BF16)
+
+
+def weight_far_body(place, n_ref, r4, l4, out_ref):
+    for j, piece in enumerate(weight_pair(1 - place[2], n_ref, r4, l4, 0, 0)):
+        out_ref[j] = piece.astype(BF16)
 
 
 def weight_add_body(steps, place, n_ref, *refs):
-    *blocks, in_ref, o0, o1, o2, o3, buf, sem = refs
-    for far, other, piece in weight_pieces(steps, place, place[2], n_ref, blocks):
-        buf[far, other] = (piece + in_ref[far, other].astype(F32)).astype(BF16)
-    copies = [
-        pltpu.make_async_copy(buf.at[d], o, sem.at[d]) for d, o in enumerate((o0, o1, o2, o3))
-    ]
+    *blocks, r4, l4, near_ref, far_ref, o0, o1, low2, high2, o3, buf, sem = refs
+    mc = place[2]
+    for step, ref in zip(steps, blocks):
+        pieces = weight_pair(mc, n_ref, ref, ref, 0, 2 * DH)
+        for (far, other), piece in zip(weight_tiles(place, mc, step), pieces):
+            buf[far, other] = (piece + near_ref[far, other].astype(F32)).astype(BF16)
+    pieces = weight_pair(mc, n_ref, r4, l4, 0, 0)
+    for j, ((far, other), piece) in enumerate(zip(weight_tiles(place, mc, 4), pieces)):
+        buf[far, other] = (piece + far_ref[j].astype(F32)).astype(BF16)
+    n = low2.shape[0]
+    moves = [(buf.at[2, :n], low2), (buf.at[2, n:], high2)]
+    moves += [(buf.at[0], o0), (buf.at[1], o1), (buf.at[3], o3)]
+    copies = [pltpu.make_async_copy(a, o, sem.at[d]) for d, (a, o) in enumerate(moves)]
     for copy in copies:
         copy.start()
     for copy in copies:
         copy.wait()
 
 
-def backward_body(place, q_ref, k_ref, v_ref, sc_ref, ag_ref, so, sr, go, gr, dq_ref, dk_ref, dv_ref):
+def relay_body(up_ref, down_ref, from_below, from_above, up_out, down_out):
+    n = from_below.shape[0]
+    up_out[:n] = (up_ref[:n].astype(F32) + from_below[...].astype(F32)).astype(BF16)
+    up_out[n:] = up_ref[n:]
+    down_out[:n] = down_ref[:n]
+    down_out[n:] = (down_ref[n:].astype(F32) + from_above[...].astype(F32)).astype(BF16)
+
+
+def inner_body(place, q_ref, k_ref, v_ref, sc_ref, ag_ref, so, sr, dq_ref, dk_ref, dv_ref):
     lower = lower_mask(q_ref.shape[1])
 
-    def step(b, i, s):
-        q, k, v, ag = q_ref[b, :, s], k_ref[b, :, s], v_ref[b, :, s], ag_ref[b, :, s]
-        sg = jnp.where(lower, dot(ag, v, 1, 1) * SCALE, 0.0).astype(BF16)
-        earlier, later = pick_state(place, so, sr, b, s), pick_state(place, go, gr, b, s)
-        dq_ref[b, :, s] = (dot(sg, k, 1, 0) + SCALE * dot(ag, earlier, 1, 1)).astype(BF16)
-        dk_ref[b, :, s] = (dot(sg, q, 0, 0) + SCALE * dot(v, later, 1, 1)).astype(BF16)
-        dv_ref[b, :, s] = (dot(sc_ref[i], ag, 0, 0) + SCALE * dot(k, later, 1, 0)).astype(BF16)
-
-    each_batch(q_ref.shape[2], step)
+    def step(b, h, i, s):
+        ag = ag_ref[b, :, s]
+        sg = jnp.where(lower, dot(ag, v_ref[b, :, s], 1, 1) * SCALE, 0.0).astype(BF16)
+        earlier = pick_state(place, so, sr, b, h)
+        dq_ref[b, :, s] = (dot(sg, k_ref[b, :, s], 1, 0) + SCALE * dot(ag, earlier, 1, 1)).astype(BF16)
+        dk_ref[b, :, s] = dot(sg, q_ref[b, :, s], 0, 0)
+        dv_ref[b, :, s] = dot(sc_ref[i], ag, 0, 0)
+
+    each_head(q_ref.shape[2], step)
+
+
+def outer_body(place, k_ref, v_ref, ik_ref, iv_ref, go, gr, dk_ref, dv_ref):
+    def step(b, h, i, s):
+        later = pick_state(place, go, gr, b, h)
+        dk_ref[b, :, s] = (ik_ref[b, :, s] + SCALE * dot(v_ref[b, :, s], later, 1, 1)).astype(BF16)
+        dv_ref[b, :, s] = (iv_ref[b, :, s] + SCALE * dot(k_ref[b, :, s], later, 1, 0)).astype(BF16)
+
+    each_head(k_ref.shape[2], step)
 
 
 def shift(value, axis, step):
@@ -297,37 +343,50 @@
     return near
 
 
-def reduce_weight(place, normed, blocks, factor, after):
+def send_near(place, normed, blocks):
     rows, width = normed.shape
-    flops = rows * width * width * 8
-    grid = (4, 4, width, DH)
-    theirs = call(
-        functools.partial(weight_body, STEPS),
-        [shape(grid, BF16)],
-        [place, normed, *blocks],
-        flops,
+    near = call(
+        functools.partial(weight_near_body, STEPS),
+        [shape((4, 4, width, DH), BF16)],
+        [place, normed, *blocks[:7]],
+        rows * width * width * 7,
         True,
     )[0]
-    theirs = shift(theirs, "ctx_2", 1)
-    theirs, _ = lax.optimization_barrier((theirs, after))
-    total = call(
+    return shift(near, "ctx_2", 1)
+
+
+def reduce_weight(place, normed, blocks, near, factor):
+    rows, width = normed.shape
+    flops = rows * width * width
+    far = call(
+        weight_far_body, [shape((2, width, DH), BF16)], [place, normed, *blocks[7:]], flops, True
+    )[0]
+    far = shift(far, "ctx_2", 1)
+    whole, part = (4, width, DH), (2, width, DH)
+    own, up, low, high, down = call(
         functools.partial(weight_add_body, STEPS),
-        [shape(grid[1:], BF16)] * 4,
-        [place, normed, *blocks, theirs],
-        flops,
-        True,
-        [VMEM(grid, BF16), pltpu.SemaphoreType.DMA((4,))],
-    )
-    got = [shift_by_core(total[d], True, d) for d in (1, 2, 3)]
+        [shape(d, BF16) for d in (whole, whole, part, part, whole)],
+        [place, normed, *blocks, near, far],
+        flops * 8,
+        True,
+        [VMEM((4, *whole), BF16), pltpu.SemaphoreType.DMA((5,))],
+    )
+    low = shift_by_core(low, True, 1)
+    high = shift_by_core(high, True, -1)
+    up, down = call(relay_body, [shape(whole, BF16)] * 2, [up, down, low, high], up.size)
+    up = shift_by_core(up, True, 1)
+    down = shift_by_core(down, True, -1)
     piece = (width, DH)
     own, *send = call(
         combine_body,
         [shape(piece, F32)] + [shape(piece, BF16)] * 3,
-        [place, total[0], *got],
-        total[0].size * 4,
-        True,
-    )
-    got = [shift_by_core(send[d - 1], False, d) for d in (1, 2, 3)]
+        [place, own, up, down],
+        own.size * 3,
+        True,
+    )
+    got = []
+    for d in (1, 2, 3):
+        got.append(shift_by_core(send[d - 1], False, d))
     return call(functools.partial(finish_body, factor), [shape(piece, F32)], [own, *got], own.size * 4)[0]
 
 
@@ -342,13 +401,25 @@
     place = jnp.stack([mx, my, mc, mz]).astype(jnp.int32)
     mat_flops = 2 * n_mat * length * DH * DH
     pair = [shape(half, F32), shape(half, BF16)]
-    keep, send = call(state_body, pair, [place, key_rows, value_rows], mat_flops, True)
+    keep, send, near_keys, near_values = call(
+        state_body,
+        pair + [shape(queries.shape, BF16)] * 2,
+        [place, key_rows, value_rows],
+        mat_flops,
+        True,
+    )
+    scores, intra, near_queries = call(
+        intra_body,
+        [shape((n_mat, length, length), BF16), shape(queries.shape, F32), shape(queries.shape, BF16)],
+        [queries, near_keys, near_values],
+        3 * mat_flops,
+    )
     state = exclusive(place, keep, send, False)
-    normed, attended, scores = call(
+    normed, attended = call(
         forward_body,
-        [shape(queries.shape, BF16), shape(queries.shape, F32), shape((n_mat, length, length), BF16)],
-        [place, queries, key_rows, value_rows, *state],
-        5 * mat_flops,
+        [shape(queries.shape, BF16), shape(queries.shape, F32)],
+        [place, near_queries, intra, *state],
+        mat_flops,
         True,
     )
     normed = normed.reshape(rows, width)
@@ -357,28 +428,37 @@
     layer_output = lax.psum_scatter(
         partial.reshape(n_head * rows, width), "head", scatter_dimension=0, tiled=True
     ).reshape(queries.shape)
+    near = send_near(place, normed, blocks)
     part_grad = call(
-        functools.partial(grad_near_body, STEPS[:5]),
+        functools.partial(grad_near_body, STEPS),
         [shape((rows, width), F32)],
-        [place, *blocks[:5], out_weight],
-        big * 5 // 8,
+        [place, *blocks[:7], out_weight],
+        big * 7 // 8,
         True,
     )[0]
     attended_grad, keep, send = call(
-        functools.partial(grad_far_body, STEPS[5:]),
+        grad_far_body,
         [shape(queries.shape, BF16), *pair],
-        [place, *blocks[5:], out_weight, part_grad, attended, queries],
-        big * 3 // 8,
-        True,
+        [place, *blocks[7:], out_weight, part_grad, attended, queries],
+        big // 8,
+        True,
+        [VMEM(queries.shape, F32)],
     )
     factor = (rows * lax.axis_size(CTX)) ** (-0.5)
-    weight_grad = reduce_weight(place, normed, blocks, factor, keep)
+    weight_grad = reduce_weight(place, normed, blocks, near, factor)
     grad_state = exclusive(place, keep, send, True)
-    query_grad, key_grad, value_grad = call(
-        backward_body,
-        [shape(queries.shape, BF16)] * 3,
-        [place, queries, key_rows, value_rows, scores, attended_grad, *state, *grad_state],
-        10 * mat_flops,
+    query_grad, inner_key, inner_value = call(
+        inner_body,
+        [shape(queries.shape, BF16)] + [shape(queries.shape, F32)] * 2,
+        [place, queries, key_rows, value_rows, scores, attended_grad, *state],
+        5 * mat_flops,
+        True,
+    )
+    key_grad, value_grad = call(
+        outer_body,
+        [shape(queries.shape, BF16)] * 2,
+        [place, key_rows, value_rows, inner_key, inner_value, *grad_state],
+        2 * mat_flops,
         True,
     )
     return (layer_output, query_grad, key_grad, value_grad, weight_grad)

time: 175 us -> 180 us (1.029)
  Pallas kernels: 23.1 us -> 28.8 us
  starting transfers between devices: 46 us -> 50.6 us
  waiting for transfers between devices: 85.2 us -> 81.8 us
  local copies, waits for them, and re-layouts: 6.27 us -> 4.28 us
    ppermute x18 -> x19, waiting for transfers between devices: 32.1 us -> 23.4 us  [shift_by_core(): lax.ppermute(value, CTX, [(index(*p), index(*target(*p))) for p in places])]
    pallas_call x18 -> x22, Pallas kernels: 23.1 us -> 28.8 us  [call(): pl.pallas_call(body, out_shape=outs, in_specs=specs, out_specs=[pl.BlockS...]
    ppermute x13 -> x14, waiting for transfers between devices: 53 us -> 58.4 us  [shift(): return lax.ppermute(value, axis, [(i, (i + step) % n) for i in range(n)])]
    ppermute x18 -> x19, starting transfers between devices: 17.3 us -> 21.4 us  [shift_by_core(): lax.ppermute(value, CTX, [(index(*p), index(*target(*p))) for p in places])]
    unnamed x22 -> x18, local copies, waits for them, and re-layouts: 6.27 us -> 4.28 us
    ppermute x13 -> x14, starting transfers between devices: 28.7 us -> 29.2 us  [shift(): return lax.ppermute(value, axis, [(i, (i + step) % n) for i in range(n)])]
  transfers between devices with their start and end apart: 32 -> 34, of which waited for: 21 -> 22; matrix products, arithmetic and copies ran while one was open for 0% -> 0% of each run, Pallas kernels for 9% -> 12%
where the time goes in v2:
time: 180 us
  waiting for transfers between devices  81.8 us (45%)
  starting transfers between devices  50.6 us (28%)
  Pallas kernels  28.8 us (16%)
  between operations  14.3 us (8%)
  local copies, waits for them, and re-layouts  4.28 us (2%)
    ppermute x14, waiting for transfers between devices, shift(): return lax.ppermute(value, axis, [(i, (i + step) % n) for i in range(n)])  58.4 us
    ppermute x14, starting transfers between devices, shift(): return lax.ppermute(value, axis, [(i, (i + step) % n) for i in range(n)])  29.2 us
    pallas_call x22, Pallas kernels, call(): pl.pallas_call(body, out_shape=outs, in_specs=specs, out_specs=[pl.BlockS...  28.8 us
    ppermute x19, waiting for transfers between devices, shift_by_core(): lax.ppermute(value, CTX, [(index(*p), index(*target(*p))) for p in places])  23.4 us
    ppermute x19, starting transfers between devices, shift_by_core(): lax.ppermute(value, CTX, [(index(*p), index(*target(*p))) for p in places])  21.4 us
    unnamed x18, local copies, waits for them, and re-layouts  4.28 us
  transfers between devices with their start and end apart: 34, of which 22 were waited for; matrix products, arithmetic and copies ran while one was open for 0% of the time, Pallas kernels for 12%

profile of v2, /device:TPU:1, one launch (start us, length us, event | category | flops | bytes accessed | tf_op | source)
XLA Modules:
  0.0 179.9 jit_solution(8376830964078358176)
XLA Ops:
  10.5 3.3 %collective-permute-start = (bf16[4,128,128]{2,1,0:T(8,128)(2,1)S(1)}, bf16[4,128,128]{2,1,0:T(8,128)(2,1)S(1)}, u32[]{:S(2)}, u32[]{:S(2)}) collective-permute-start(bf16[4,128,128]{2,1,0:T(8,128)(2,1)S(1)} %get-tuple-element.50), channel_id=1, source_target_pairs={{0,8},{8,0},{1,9},{9,1},{2,10},{10,2},{3,11},{11,3},{4,12},{12,4},... | collective-permute-start | bytes 393224 | tf_op jit(solution)/shard_map/ppermute | solution.py:290
  19.0 2.3 %collective-permute-done.2.g2 = bf16[4,128,128]{2,1,0:T(8,128)(2,1)S(1)} collective-permute-done((bf16[4,128,128]{2,1,0:T(8,128)(2,1)S(1)}, bf16[4,128,128]{2,1,0:T(8,128)(2,1)S(1)}, u32[]{:S(2)}, u32[]{:S(2)}) %collective-permute-start.2) | collective-permute-done | bytes 131104 | tf_op jit(solution)/shard_map/ppermute | solution.py:302
  24.5 2.6 %collective-permute-start.5 = (bf16[4,128,128]{2,1,0:T(8,128)(2,1)S(1)}, bf16[4,128,128]{2,1,0:T(8,128)(2,1)S(1)}, u32[]{:S(2)}, u32[]{:S(2)}) collective-permute-start(bf16[4,128,128]{2,1,0:T(8,128)(2,1)S(1)} %get-tuple-element.53), channel_id=1, source_target_pairs={{0,128},{8,40},{16,144},{24,56},{32,160},{40,8},{48,176},{56,24},{... | collective-permute-start | bytes 393224 | tf_op jit(solution)/shard_map/ppermute | solution.py:302
  28.5 2.4 %collective-permute-done.5.g2 = bf16[4,128,128]{2,1,0:T(8,128)(2,1)S(1)} collective-permute-done((bf16[4,128,128]{2,1,0:T(8,128)(2,1)S(1)}, bf16[4,128,128]{2,1,0:T(8,128)(2,1)S(1)}, u32[]{:S(2)}, u32[]{:S(2)}) %collective-permute-start.5) | collective-permute-done | bytes 131104 | tf_op jit(solution)/shard_map/ppermute | solution.py:302
  31.7 3.5 %collective-permute-start.7 = (bf16[4,128,128]{2,1,0:T(8,128)(2,1)S(1)}, bf16[4,128,128]{2,1,0:T(8,128)(2,1)S(1)}, u32[]{:S(2)}, u32[]{:S(2)}) collective-permute-start(bf16[4,128,128]{2,1,0:T(8,128)(2,1)S(1)} %get-tuple-element.56), channel_id=1, source_target_pairs={{0,8},{8,0},{1,9},{9,1},{2,10},{10,2},{3,11},{11,3},{4,12},{12,4},... | collective-permute-start | bytes 393224 | tf_op jit(solution)/shard_map/ppermute | solution.py:290
  40.0 3.9 %shard_map.98 = bf16[8,384,512]{2,1,0:T(8,128)(2,1)} custom-call(bf16[384,512]{1,0:T(8,128)(2,1)S(1)} %bitcast.8, bf16[512,4096]{1,0:T(8,128)(2,1)S(1)} %copy-done), custom_call_target="tpu_custom_call" | custom-call | flops 1610612736 | bytes 7733248 | tf_op jit(solution)/shard_map/pallas_call | solution.py:33
  45.0 5.6 %collective-permute-start.12 = (bf16[384,512]{1,0:T(8,128)(2,1)S(1)}, bf16[384,512]{1,0:T(8,128)(2,1)S(1)}, u32[]{:S(2)}, u32[]{:S(2)}) collective-permute-start(bf16[384,512]{1,0:T(8,128)(2,1)S(1)} %bitcast.12), channel_id=1, source_target_pairs={{0,7},{1,0},{2,1},{3,2},{4,3},{5,4},{6,5},{7,6},{8,15},{9,8},{10,9... | collective-permute-start | bytes 1179656 | tf_op jit(solution)/shard_map/ppermute | solution.py:290
  50.5 12.3 %collective-permute-done.12.refs_2_ = bf16[384,512]{1,0:T(8,128)(2,1)S(1)} collective-permute-done((bf16[384,512]{1,0:T(8,128)(2,1)S(1)}, bf16[384,512]{1,0:T(8,128)(2,1)S(1)}, u32[]{:S(2)}, u32[]{:S(2)}) %collective-permute-start.12) | collective-permute-done | bytes 393248 | tf_op jit(solution)/shard_map/ppermute | solution.py:290
  62.9 3.5 %collective-permute-start.13 = (bf16[384,512]{1,0:T(8,128)(2,1)S(1)}, bf16[384,512]{1,0:T(8,128)(2,1)S(1)}, u32[]{:S(2)}, u32[]{:S(2)}) collective-permute-start(bf16[384,512]{1,0:T(8,128)(2,1)S(1)} %collective-permute-done.12.refs_2_), channel_id=1, source_target_pairs={{0,7},{1,0},{2,1},{3,2},{4,3},{5,4},{6,5},{7,6},{8,15},{9,8},{10,9... | collective-permute-start | bytes 1179656 | tf_op jit(solution)/shard_map/ppermute | solution.py:290
  66.4 15.9 %collective-permute-done.13.refs_4_ = bf16[384,512]{1,0:T(8,128)(2,1)S(1)} collective-permute-done((bf16[384,512]{1,0:T(8,128)(2,1)S(1)}, bf16[384,512]{1,0:T(8,128)(2,1)S(1)}, u32[]{:S(2)}, u32[]{:S(2)}) %collective-permute-start.13) | collective-permute-done | bytes 393248 | tf_op jit(solution)/shard_map/ppermute | solution.py:290
  82.3 3.5 %collective-permute-start.14 = (bf16[384,512]{1,0:T(8,128)(2,1)S(1)}, bf16[384,512]{1,0:T(8,128)(2,1)S(1)}, u32[]{:S(2)}, u32[]{:S(2)}) collective-permute-start(bf16[384,512]{1,0:T(8,128)(2,1)S(1)} %collective-permute-done.13.refs_4_), channel_id=1, source_target_pairs={{0,7},{1,0},{2,1},{3,2},{4,3},{5,4},{6,5},{7,6},{8,15},{9,8},{10,9... | collective-permute-start | bytes 1179656 | tf_op jit(solution)/shard_map/ppermute | solution.py:290
  86.6 15.6 %collective-permute-done.14.x_ref.refs_6_ = bf16[384,512]{1,0:T(8,128)(2,1)S(1)} collective-permute-done((bf16[384,512]{1,0:T(8,128)(2,1)S(1)}, bf16[384,512]{1,0:T(8,128)(2,1)S(1)}, u32[]{:S(2)}, u32[]{:S(2)}) %collective-permute-start.14) | collective-permute-done | bytes 393248 | tf_op jit(solution)/shard_map/ppermute | solution.py:290
  102.2 4.4 %collective-permute-done.10.x_ref.refs_5_ = bf16[384,512]{1,0:T(8,128)(2,1)S(1)} collective-permute-done((bf16[384,512]{1,0:T(8,128)(2,1)S(1)}, bf16[384,512]{1,0:T(8,128)(2,1)S(1)}, u32[]{:S(2)}, u32[]{:S(2)}) %collective-permute-start.10) | collective-permute-done | bytes 393248 | tf_op jit(solution)/shard_map/ppermute | solution.py:290
  108.5 3.1 %collective-permute-start.24 = (bf16[4,4,512,128]{3,2,1,0:T(8,128)(2,1)S(1)}, bf16[4,4,512,128]{3,2,1,0:T(8,128)(2,1)S(1)}, u32[]{:S(2)}, u32[]{:S(2)}) collective-permute-start(bf16[4,4,512,128]{3,2,1,0:T(8,128)(2,1)S(1)} %shard_map.108), channel_id=1, source_target_pairs={{0,8},{8,0},{1,9},{9,1},{2,10},{10,2},{3,11},{11,3},{4,12},{12,4},... | collective-permute-start | bytes 6291464 | tf_op jit(solution)/shard_map/ppermute | solution.py:290
  113.2 4.9 %collective-permute-done.15.refs_1_.l4.refs_8_ = bf16[384,256]{1,0:T(8,128)(2,1)S(1)} collective-permute-done((bf16[384,256]{1,0:T(8,128)(2,1)S(1)}, bf16[384,256]{1,0:T(8,128)(2,1)S(1)}, u32[]{:S(2)}, u32[]{:S(2)}) %collective-permute-start.15) | collective-permute-done | bytes 196640 | tf_op jit(solution)/shard_map/ppermute | solution.py:290
  127.3 4.1 %collective-permute-done.26.from_below = bf16[2,512,128]{2,1,0:T(8,128)(2,1)S(1)} collective-permute-done((bf16[2,512,128]{2,1,0:T(8,128)(2,1)S(1)}, bf16[2,512,128]{2,1,0:T(8,128)(2,1)S(1)}, u32[]{:S(2)}, u32[]{:S(2)}) %collective-permute-start.26) | collective-permute-done | bytes 262176 | tf_op jit(solution)/shard_map/ppermute | solution.py:302
  141.6 2.4 %collective-permute-start.19 = (bf16[4,128,128]{2,1,0:T(8,128)(2,1)S(1)}, bf16[4,128,128]{2,1,0:T(8,128)(2,1)S(1)}, u32[]{:S(2)}, u32[]{:S(2)}) collective-permute-start(bf16[4,128,128]{2,1,0:T(8,128)(2,1)S(1)} %shard_map.104.t_ref), channel_id=1, source_target_pairs={{0,48},{8,200},{16,0},{24,216},{32,16},{40,232},{48,32},{56,248},{... | collective-permute-start | bytes 393224 | tf_op jit(solution)/shard_map/ppermute | solution.py:302
  144.9 2.4 %collective-permute-done.19.g3 = bf16[4,128,128]{2,1,0:T(8,128)(2,1)S(1)} collective-permute-done((bf16[4,128,128]{2,1,0:T(8,128)(2,1)S(1)}, bf16[4,128,128]{2,1,0:T(8,128)(2,1)S(1)}, u32[]{:S(2)}, u32[]{:S(2)}) %collective-permute-start.19) | collective-permute-done | bytes 131104 | tf_op jit(solution)/shard_map/ppermute | solution.py:302
  147.4 2.3 %collective-permute-done.18.g2 = bf16[4,128,128]{2,1,0:T(8,128)(2,1)S(1)} collective-permute-done((bf16[4,128,128]{2,1,0:T(8,128)(2,1)S(1)}, bf16[4,128,128]{2,1,0:T(8,128)(2,1)S(1)}, u32[]{:S(2)}, u32[]{:S(2)}) %collective-permute-start.18) | collective-permute-done | bytes 131104 | tf_op jit(solution)/shard_map/ppermute | solution.py:302
  151.9 2.5 %collective-permute-start.21 = (bf16[4,128,128]{2,1,0:T(8,128)(2,1)S(1)}, bf16[4,128,128]{2,1,0:T(8,128)(2,1)S(1)}, u32[]{:S(2)}, u32[]{:S(2)}) collective-permute-start(bf16[4,128,128]{2,1,0:T(8,128)(2,1)S(1)} %get-tuple-element.68), channel_id=1, source_target_pairs={{0,128},{8,40},{16,144},{24,56},{32,160},{40,8},{48,176},{56,24},{... | collective-permute-start | bytes 393224 | tf_op jit(solution)/shard_map/ppermute | solution.py:302
  154.7 3.6 %collective-permute-done.20.g1 = bf16[4,128,128]{2,1,0:T(8,128)(2,1)S(1)} collective-permute-done((bf16[4,128,128]{2,1,0:T(8,128)(2,1)S(1)}, bf16[4,128,128]{2,1,0:T(8,128)(2,1)S(1)}, u32[]{:S(2)}, u32[]{:S(2)}) %collective-permute-start.20) | collective-permute-done | bytes 131104 | tf_op jit(solution)/shard_map/ppermute | solution.py:302
  159.9 2.3 %collective-permute-start.23 = (bf16[4,128,128]{2,1,0:T(8,128)(2,1)S(1)}, bf16[4,128,128]{2,1,0:T(8,128)(2,1)S(1)}, u32[]{:S(2)}, u32[]{:S(2)}) collective-permute-start(bf16[4,128,128]{2,1,0:T(8,128)(2,1)S(1)} %get-tuple-element.71), channel_id=1, source_target_pairs={{0,8},{8,0},{1,9},{9,1},{2,10},{10,2},{3,11},{11,3},{4,12},{12,4},... | collective-permute-start | bytes 393224 | tf_op jit(solution)/shard_map/ppermute | solution.py:290
  165.7 4.2 %shard_map.103 = (bf16[2,192,512]{2,1,0:T(8,128)(2,1)}, f32[2,192,512]{2,1,0:T(8,128)S(1)}, f32[2,192,512]{2,1,0:T(8,128)S(1)}) custom-call(s32[4]{0:T(128)S(1)} %pad_add_fusion.place, bf16[2,192,512]{2,1,0:T(8,128)(2,1)S(1)} %copy-done.8, bf16[2,192,512]{2,1,0:T(8,128)(2,1)S(1)} %copy-done.4, bf16[2,192,512]{2,1,0:T(8,128)(2,1)S(1)} %copy-done.6, ...), custom_call_target="tpu_custom_call" | custom-call | flops 251658240 | bytes 4390928 | tf_op jit(solution)/shard_map/pallas_call | solution.py:33
  170.0 2.3 %shard_map.107 = (bf16[2,192,512]{2,1,0:T(8,128)(2,1)}, bf16[2,192,512]{2,1,0:T(8,128)(2,1)}) custom-call(s32[4]{0:T(128)S(1)} %pad_add_fusion.place, bf16[2,192,512]{2,1,0:T(8,128)(2,1)S(1)} %copy-done.4, bf16[2,192,512]{2,1,0:T(8,128)(2,1)S(1)} %copy-done.6, f32[2,192,512]{2,1,0:T(8,128)S(1)} %get-tuple-element.62.ik_ref, ...), custom_call_target="tpu_custom_call" | custom-call | flops 100663296 | bytes 3407888 | tf_op jit(solution)/shard_map/pallas_call | solution.py:33
  (86 shorter events, 52.8 us)
Async XLA Ops:
  7.2 165.9 %reduce-scatter.2.cloned.1.call-start = ((), (), s32[]{:S(2)}) async-start(), calls=%async_computation.1 | async-start | bytes 3538944 | tf_op jit(solution)/shard_map/reduce_scatter | solution.py:428
  16.1 6.5 %collective-permute-start.1 = (bf16[4,128,128]{2,1,0:T(8,128)(2,1)S(1)}, bf16[4,128,128]{2,1,0:T(8,128)(2,1)S(1)}, u32[]{:S(2)}, u32[]{:S(2)}) collective-permute-start(bf16[4,128,128]{2,1,0:T(8,128)(2,1)S(1)} %shard_map.94.t_ref), channel_id=1, source_target_pairs={{0,16},{8,72},{16,32},{24,88},{32,48},{40,104},{48,0},{56,120},{64... | collective-permute-start | bytes 393224 | tf_op jit(solution)/shard_map/ppermute | solution.py:302
  24.5 6.4 %collective-permute-start.5 = (bf16[4,128,128]{2,1,0:T(8,128)(2,1)S(1)}, bf16[4,128,128]{2,1,0:T(8,128)(2,1)S(1)}, u32[]{:S(2)}, u32[]{:S(2)}) collective-permute-start(bf16[4,128,128]{2,1,0:T(8,128)(2,1)S(1)} %get-tuple-element.53), channel_id=1, source_target_pairs={{0,128},{8,40},{16,144},{24,56},{32,160},{40,8},{48,176},{56,24},{... | collective-permute-start | bytes 393224 | tf_op jit(solution)/shard_map/ppermute | solution.py:302
  31.7 6.6 %collective-permute-start.7 = (bf16[4,128,128]{2,1,0:T(8,128)(2,1)S(1)}, bf16[4,128,128]{2,1,0:T(8,128)(2,1)S(1)}, u32[]{:S(2)}, u32[]{:S(2)}) collective-permute-start(bf16[4,128,128]{2,1,0:T(8,128)(2,1)S(1)} %get-tuple-element.56), channel_id=1, source_target_pairs={{0,8},{8,0},{1,9},{9,1},{2,10},{10,2},{3,11},{11,3},{4,12},{12,4},... | collective-permute-start | bytes 393224 | tf_op jit(solution)/shard_map/ppermute | solution.py:290
  45.0 17.9 %collective-permute-start.12 = (bf16[384,512]{1,0:T(8,128)(2,1)S(1)}, bf16[384,512]{1,0:T(8,128)(2,1)S(1)}, u32[]{:S(2)}, u32[]{:S(2)}) collective-permute-start(bf16[384,512]{1,0:T(8,128)(2,1)S(1)} %bitcast.12), channel_id=1, source_target_pairs={{0,7},{1,0},{2,1},{3,2},{4,3},{5,4},{6,5},{7,6},{8,15},{9,8},{10,9... | collective-permute-start | bytes 1179656 | tf_op jit(solution)/shard_map/ppermute | solution.py:290
  50.5 15.9 %collective-permute-start.8 = (bf16[384,512]{1,0:T(8,128)(2,1)S(1)}, bf16[384,512]{1,0:T(8,128)(2,1)S(1)}, u32[]{:S(2)}, u32[]{:S(2)}) collective-permute-start(bf16[384,512]{1,0:T(8,128)(2,1)S(1)} %bitcast.13), channel_id=1, source_target_pairs={{0,1},{1,2},{2,3},{3,4},{4,5},{5,6},{6,7},{7,0},{8,9},{9,10},{10,1... | collective-permute-start | bytes 1179656 | tf_op jit(solution)/shard_map/ppermute | solution.py:290
  62.9 19.4 %collective-permute-start.13 = (bf16[384,512]{1,0:T(8,128)(2,1)S(1)}, bf16[384,512]{1,0:T(8,128)(2,1)S(1)}, u32[]{:S(2)}, u32[]{:S(2)}) collective-permute-start(bf16[384,512]{1,0:T(8,128)(2,1)S(1)} %collective-permute-done.12.refs_2_), channel_id=1, source_target_pairs={{0,7},{1,0},{2,1},{3,2},{4,3},{5,4},{6,5},{7,6},{8,15},{9,8},{10,9... | collective-permute-start | bytes 1179656 | tf_op jit(solution)/shard_map/ppermute | solution.py:290
  66.4 20.2 %collective-permute-start.9 = (bf16[384,512]{1,0:T(8,128)(2,1)S(1)}, bf16[384,512]{1,0:T(8,128)(2,1)S(1)}, u32[]{:S(2)}, u32[]{:S(2)}) collective-permute-start(bf16[384,512]{1,0:T(8,128)(2,1)S(1)} %collective-permute-done.8.refs_1_), channel_id=1, source_target_pairs={{0,1},{1,2},{2,3},{3,4},{4,5},{5,6},{6,7},{7,0},{8,9},{9,10},{10,1... | collective-permute-start | bytes 1179656 | tf_op jit(solution)/shard_map/ppermute | solution.py:290
  82.3 20.0 %collective-permute-start.14 = (bf16[384,512]{1,0:T(8,128)(2,1)S(1)}, bf16[384,512]{1,0:T(8,128)(2,1)S(1)}, u32[]{:S(2)}, u32[]{:S(2)}) collective-permute-start(bf16[384,512]{1,0:T(8,128)(2,1)S(1)} %collective-permute-done.13.refs_4_), channel_id=1, source_target_pairs={{0,7},{1,0},{2,1},{3,2},{4,3},{5,4},{6,5},{7,6},{8,15},{9,8},{10,9... | collective-permute-start | bytes 1179656 | tf_op jit(solution)/shard_map/ppermute | solution.py:290
  86.6 20.0 %collective-permute-start.10 = (bf16[384,512]{1,0:T(8,128)(2,1)S(1)}, bf16[384,512]{1,0:T(8,128)(2,1)S(1)}, u32[]{:S(2)}, u32[]{:S(2)}) collective-permute-start(bf16[384,512]{1,0:T(8,128)(2,1)S(1)} %collective-permute-done.9.refs_3_), channel_id=1, source_target_pairs={{0,1},{1,2},{2,3},{3,4},{4,5},{5,6},{6,7},{7,0},{8,9},{9,10},{10,1... | collective-permute-start | bytes 1179656 | tf_op jit(solution)/shard_map/ppermute | solution.py:290
  108.5 14.0 %collective-permute-start.24 = (bf16[4,4,512,128]{3,2,1,0:T(8,128)(2,1)S(1)}, bf16[4,4,512,128]{3,2,1,0:T(8,128)(2,1)S(1)}, u32[]{:S(2)}, u32[]{:S(2)}) collective-permute-start(bf16[4,4,512,128]{3,2,1,0:T(8,128)(2,1)S(1)} %shard_map.108), channel_id=1, source_target_pairs={{0,8},{8,0},{1,9},{9,1},{2,10},{10,2},{3,11},{11,3},{4,12},{12,4},... | collective-permute-start | bytes 6291464 | tf_op jit(solution)/shard_map/ppermute | solution.py:290
  111.5 6.5 %collective-permute-start.15 = (bf16[384,256]{1,0:T(8,128)(2,1)S(1)}, bf16[384,256]{1,0:T(8,128)(2,1)S(1)}, u32[]{:S(2)}, u32[]{:S(2)}) collective-permute-start(bf16[384,256]{1,0:T(8,128)(2,1)S(1)} %shard_map.100), channel_id=1, source_target_pairs={{0,7},{1,0},{2,1},{3,2},{4,3},{5,4},{6,5},{7,6},{8,15},{9,8},{10,9... | collective-permute-start | bytes 589832 | tf_op jit(solution)/shard_map/ppermute | solution.py:290
  111.7 7.7 %collective-permute-start.11 = (bf16[384,256]{1,0:T(8,128)(2,1)S(1)}, bf16[384,256]{1,0:T(8,128)(2,1)S(1)}, u32[]{:S(2)}, u32[]{:S(2)}) collective-permute-start(bf16[384,256]{1,0:T(8,128)(2,1)S(1)} %shard_map.99), channel_id=1, source_target_pairs={{0,1},{1,2},{2,3},{3,4},{4,5},{5,6},{6,7},{7,0},{8,9},{9,10},{10,1... | collective-permute-start | bytes 589832 | tf_op jit(solution)/shard_map/ppermute | solution.py:290
  124.6 6.8 %collective-permute-start.26 = (bf16[2,512,128]{2,1,0:T(8,128)(2,1)S(1)}, bf16[2,512,128]{2,1,0:T(8,128)(2,1)S(1)}, u32[]{:S(2)}, u32[]{:S(2)}) collective-permute-start(bf16[2,512,128]{2,1,0:T(8,128)(2,1)S(1)} %get-tuple-element.77), channel_id=1, source_target_pairs={{0,16},{8,72},{16,32},{24,88},{32,48},{40,104},{48,0},{56,120},{64... | collective-permute-start | bytes 786440 | tf_op jit(solution)/shard_map/ppermute | solution.py:302
  131.5 30.7 %collective-permute-start.28 = (bf16[4,512,128]{2,1,0:T(8,128)(2,1)S(1)}, bf16[4,512,128]{2,1,0:T(8,128)(2,1)S(1)}, u32[]{:S(2)}, u32[]{:S(2)}) collective-permute-start(bf16[4,512,128]{2,1,0:T(8,128)(2,1)S(1)} %get-tuple-element.79), channel_id=1, source_target_pairs={{0,16},{8,72},{16,32},{24,88},{32,48},{40,104},{48,0},{56,120},{64... | collective-permute-start | bytes 1572872 | tf_op jit(solution)/shard_map/ppermute | solution.py:302
  132.2 30.0 %collective-permute-start.29 = (bf16[4,512,128]{2,1,0:T(8,128)(2,1)S(1)}, bf16[4,512,128]{2,1,0:T(8,128)(2,1)S(1)}, u32[]{:S(2)}, u32[]{:S(2)}) collective-permute-start(bf16[4,512,128]{2,1,0:T(8,128)(2,1)S(1)} %get-tuple-element.80), channel_id=1, source_target_pairs={{0,48},{8,200},{16,0},{24,216},{32,16},{40,232},{48,32},{56,248},{... | collective-permute-start | bytes 1572872 | tf_op jit(solution)/shard_map/ppermute | solution.py:302
  141.6 5.8 %collective-permute-start.19 = (bf16[4,128,128]{2,1,0:T(8,128)(2,1)S(1)}, bf16[4,128,128]{2,1,0:T(8,128)(2,1)S(1)}, u32[]{:S(2)}, u32[]{:S(2)}) collective-permute-start(bf16[4,128,128]{2,1,0:T(8,128)(2,1)S(1)} %shard_map.104.t_ref), channel_id=1, source_target_pairs={{0,48},{8,200},{16,0},{24,216},{32,16},{40,232},{48,32},{56,248},{... | collective-permute-start | bytes 393224 | tf_op jit(solution)/shard_map/ppermute | solution.py:302
  144.5 6.6 %collective-permute-start.17 = (bf16[4,128,128]{2,1,0:T(8,128)(2,1)S(1)}, bf16[4,128,128]{2,1,0:T(8,128)(2,1)S(1)}, u32[]{:S(2)}, u32[]{:S(2)}) collective-permute-start(bf16[4,128,128]{2,1,0:T(8,128)(2,1)S(1)} %shard_map.104.t_ref), channel_id=1, source_target_pairs={{0,16},{8,72},{16,32},{24,88},{32,48},{40,104},{48,0},{56,120},{64... | collective-permute-start | bytes 393224 | tf_op jit(solution)/shard_map/ppermute | solution.py:302
  151.8 6.5 %collective-permute-start.20 = (bf16[4,128,128]{2,1,0:T(8,128)(2,1)S(1)}, bf16[4,128,128]{2,1,0:T(8,128)(2,1)S(1)}, u32[]{:S(2)}, u32[]{:S(2)}) collective-permute-start(bf16[4,128,128]{2,1,0:T(8,128)(2,1)S(1)} %get-tuple-element.67), channel_id=1, source_target_pairs={{0,64},{8,24},{16,80},{24,40},{32,96},{40,56},{48,112},{56,8},{64,... | collective-permute-start | bytes 393224 | tf_op jit(solution)/shard_map/ppermute | solution.py:302
  151.9 6.4 %collective-permute-start.21 = (bf16[4,128,128]{2,1,0:T(8,128)(2,1)S(1)}, bf16[4,128,128]{2,1,0:T(8,128)(2,1)S(1)}, u32[]{:S(2)}, u32[]{:S(2)}) collective-permute-start(bf16[4,128,128]{2,1,0:T(8,128)(2,1)S(1)} %get-tuple-element.68), channel_id=1, source_target_pairs={{0,128},{8,40},{16,144},{24,56},{32,160},{40,8},{48,176},{56,24},{... | collective-permute-start | bytes 393224 | tf_op jit(solution)/shard_map/ppermute | solution.py:302
  159.9 10.1 %collective-permute-start.23 = (bf16[4,128,128]{2,1,0:T(8,128)(2,1)S(1)}, bf16[4,128,128]{2,1,0:T(8,128)(2,1)S(1)}, u32[]{:S(2)}, u32[]{:S(2)}) collective-permute-start(bf16[4,128,128]{2,1,0:T(8,128)(2,1)S(1)} %get-tuple-element.71), channel_id=1, source_target_pairs={{0,8},{8,0},{1,9},{9,1},{2,10},{10,2},{3,11},{11,3},{4,12},{12,4},... | collective-permute-start | bytes 393224 | tf_op jit(solution)/shard_map/ppermute | solution.py:290
  162.9 9.3 %collective-permute-start.30 = (bf16[512,128]{1,0:T(8,128)(2,1)S(1)}, bf16[512,128]{1,0:T(8,128)(2,1)S(1)}, u32[]{:S(2)}, u32[]{:S(2)}) collective-permute-start(bf16[512,128]{1,0:T(8,128)(2,1)S(1)} %get-tuple-element.82), channel_id=1, source_target_pairs={{0,64},{8,24},{16,80},{24,40},{32,96},{40,56},{48,112},{56,8},{64,... | collective-permute-start | bytes 393224 | tf_op jit(solution)/shard_map/ppermute | solution.py:302
  163.0 9.2 %collective-permute-start.31 = (bf16[512,128]{1,0:T(8,128)(2,1)S(1)}, bf16[512,128]{1,0:T(8,128)(2,1)S(1)}, u32[]{:S(2)}, u32[]{:S(2)}) collective-permute-start(bf16[512,128]{1,0:T(8,128)(2,1)S(1)} %get-tuple-element.83), channel_id=1, source_target_pairs={{0,128},{8,40},{16,144},{24,56},{32,160},{40,8},{48,176},{56,24},{... | collective-permute-start | bytes 393224 | tf_op jit(solution)/shard_map/ppermute | solution.py:302
  164.8 7.4 %collective-permute-start.32 = (bf16[512,128]{1,0:T(8,128)(2,1)S(1)}, bf16[512,128]{1,0:T(8,128)(2,1)S(1)}, u32[]{:S(2)}, u32[]{:S(2)}) collective-permute-start(bf16[512,128]{1,0:T(8,128)(2,1)S(1)} %get-tuple-element.84), channel_id=1, source_target_pairs={{0,192},{8,56},{16,208},{24,8},{32,224},{40,24},{48,240},{56,40},{... | collective-permute-start | bytes 393224 | tf_op jit(solution)/shard_map/ppermute | solution.py:302
  (19 other events, 154.0 us)
Sparse Core Ops, SparseCore 0:
  44.1 65.9 reduce-scatter.1

commit v3 on v2

--- a/solution.py
+++ b/solution.py
@@ -111,6 +111,15 @@
     lax.fori_loop(0, n, body, 0)
 
 
+def each_batch(width, step):
+    def body(b, carry):
+        for h in range(width // DH):
+            step(b, h, b * (width // DH) + h, slice(h * DH, (h + 1) * DH))
+        return carry
+
+    lax.fori_loop(0, 2, body, 0)
+
+
 def intra_body(q_ref, k_ref, v_ref, scores_ref, intra_ref, q_out):
     q_out[...] = q_ref[...]
     lower = lower_mask(q_ref.shape[1])
@@ -151,11 +160,13 @@
     out_ref[...] = x_ref[:, first : first + out_ref.shape[1]]
 
 
-def combine_body(place, o_ref, g1, g2, own_ref, s1, s2, s3):
+def combine_body(place, o_ref, g1, g2, g3, own_ref, s1, s2, s3):
     me = jnp.where(place[2] == 0, place[0], place[1])
     for d, out in enumerate((own_ref, s1, s2, s3)):
         i = (me + d) % 4
-        total = o_ref[i].astype(F32) + g1[i].astype(F32) + g2[i].astype(F32)
+        total = o_ref[i].astype(F32)
+        for g in (g1, g2, g3):
+            total = total + g[i].astype(F32)
         out[...] = total.astype(out.dtype)
 
 
@@ -235,7 +246,7 @@
 
 
 def weight_add_body(steps, place, n_ref, *refs):
-    *blocks, r4, l4, near_ref, far_ref, o0, o1, low2, high2, o3, buf, sem = refs
+    *blocks, r4, l4, near_ref, far_ref, o0, o1, o2, o3, buf, sem = refs
     mc = place[2]
     for step, ref in zip(steps, blocks):
         pieces = weight_pair(mc, n_ref, ref, ref, 0, 2 * DH)
@@ -244,22 +255,13 @@
     pieces = weight_pair(mc, n_ref, r4, l4, 0, 0)
     for j, ((far, other), piece) in enumerate(zip(weight_tiles(place, mc, 4), pieces)):
         buf[far, other] = (piece + far_ref[j].astype(F32)).astype(BF16)
-    n = low2.shape[0]
-    moves = [(buf.at[2, :n], low2), (buf.at[2, n:], high2)]
-    moves += [(buf.at[0], o0), (buf.at[1], o1), (buf.at[3], o3)]
-    copies = [pltpu.make_async_copy(a, o, sem.at[d]) for d, (a, o) in enumerate(moves)]
+    copies = [
+        pltpu.make_async_copy(buf.at[d], o, sem.at[d]) for d, o in enumerate((o0, o1, o2, o3))
+    ]
     for copy in copies:
         copy.start()
     for copy in copies:
         copy.wait()
-
-
-def relay_body(up_ref, down_ref, from_below, from_above, up_out, down_out):
-    n = from_below.shape[0]
-    up_out[:n] = (up_ref[:n].astype(F32) + from_below[...].astype(F32)).astype(BF16)
-    up_out[n:] = up_ref[n:]
-    down_out[:n] = down_ref[:n]
-    down_out[n:] = (down_ref[n:].astype(F32) + from_above[...].astype(F32)).astype(BF16)
 
 
 def inner_body(place, q_ref, k_ref, v_ref, sc_ref, ag_ref, so, sr, dq_ref, dk_ref, dv_ref):
@@ -273,7 +275,7 @@
         dk_ref[b, :, s] = dot(sg, q_ref[b, :, s], 0, 0)
         dv_ref[b, :, s] = dot(sc_ref[i], ag, 0, 0)
 
-    each_head(q_ref.shape[2], step)
+    each_batch(q_ref.shape[2], step)
 
 
 def outer_body(place, k_ref, v_ref, ik_ref, iv_ref, go, gr, dk_ref, dv_ref):
@@ -362,26 +364,24 @@
         weight_far_body, [shape((2, width, DH), BF16)], [place, normed, *blocks[7:]], flops, True
     )[0]
     far = shift(far, "ctx_2", 1)
-    whole, part = (4, width, DH), (2, width, DH)
-    own, up, low, high, down = call(
+    whole = (4, width, DH)
+    own, *send = call(
         functools.partial(weight_add_body, STEPS),
-        [shape(d, BF16) for d in (whole, whole, part, part, whole)],
+        [shape(whole, BF16)] * 4,
         [place, normed, *blocks, near, far],
         flops * 8,
         True,
-        [VMEM((4, *whole), BF16), pltpu.SemaphoreType.DMA((5,))],
-    )
-    low = shift_by_core(low, True, 1)
-    high = shift_by_core(high, True, -1)
-    up, down = call(relay_body, [shape(whole, BF16)] * 2, [up, down, low, high], up.size)
-    up = shift_by_core(up, True, 1)
-    down = shift_by_core(down, True, -1)
+        [VMEM((4, *whole), BF16), pltpu.SemaphoreType.DMA((4,))],
+    )
+    got = []
+    for d in (1, 2, 3):
+        got.append(shift_by_core(send[d - 1], True, d))
     piece = (width, DH)
     own, *send = call(
         combine_body,
         [shape(piece, F32)] + [shape(piece, BF16)] * 3,
-        [place, own, up, down],
-        own.size * 3,
+        [place, own, *got],
+        own.size * 4,
         True,
     )
     got = []

time: 180 us -> 179 us (level)
  starting transfers between devices: 50.6 us -> 42.6 us
  waiting for transfers between devices: 81.8 us -> 89.4 us
    ppermute x19 -> x18, waiting for transfers between devices: 23.4 us -> 31.8 us  [shift_by_core(): lax.ppermute(value, CTX, [(index(*p), index(*target(*p))) for p in places])]
    ppermute x19 -> x18, starting transfers between devices: 21.4 us -> 17.3 us  [shift_by_core(): lax.ppermute(value, CTX, [(index(*p), index(*target(*p))) for p in places])]
    ppermute x14, starting transfers between devices: 29.2 us -> 25.2 us  [shift(): return lax.ppermute(value, axis, [(i, (i + step) % n) for i in range(n)])]
    pallas_call x22 -> x21, Pallas kernels: 28.8 us -> 28.2 us  [call(): pl.pallas_call(body, out_shape=outs, in_specs=specs, out_specs=[pl.BlockS...]
  transfers between devices with their start and end apart: 34 -> 33, of which waited for: 22 -> 19; matrix products, arithmetic and copies ran while one was open for 0% -> 0% of each run, Pallas kernels for 12% -> 11%
where the time goes in v3:
time: 179 us
  waiting for transfers between devices  89.4 us (50%)
  starting transfers between devices  42.6 us (24%)
  Pallas kernels  28.2 us (16%)
  between operations  14.3 us (8%)
  local copies, waits for them, and re-layouts  4.28 us (2%)
    ppermute x14, waiting for transfers between devices, shift(): return lax.ppermute(value, axis, [(i, (i + step) % n) for i in range(n)])  57.6 us
    ppermute x18, waiting for transfers between devices, shift_by_core(): lax.ppermute(value, CTX, [(index(*p), index(*target(*p))) for p in places])  31.8 us
    pallas_call x21, Pallas kernels, call(): pl.pallas_call(body, out_shape=outs, in_specs=specs, out_specs=[pl.BlockS...  28.2 us
    ppermute x14, starting transfers between devices, shift(): return lax.ppermute(value, axis, [(i, (i + step) % n) for i in range(n)])  25.2 us
    ppermute x18, starting transfers between devices, shift_by_core(): lax.ppermute(value, CTX, [(index(*p), index(*target(*p))) for p in places])  17.3 us
    unnamed x18, local copies, waits for them, and re-layouts  4.28 us
  transfers between devices with their start and end apart: 33, of which 19 were waited for; matrix products, arithmetic and copies ran while one was open for 0% of the time, Pallas kernels for 11%

profile of v3, /device:TPU:1, one launch (start us, length us, event | category | flops | bytes accessed | tf_op | source)
XLA Modules:
  0.0 178.9 jit_solution(13748225790582436112)
XLA Ops:
  10.5 3.3 %collective-permute-start = (bf16[4,128,128]{2,1,0:T(8,128)(2,1)S(1)}, bf16[4,128,128]{2,1,0:T(8,128)(2,1)S(1)}, u32[]{:S(2)}, u32[]{:S(2)}) collective-permute-start(bf16[4,128,128]{2,1,0:T(8,128)(2,1)S(1)} %get-tuple-element.47), channel_id=1, source_target_pairs={{0,8},{8,0},{1,9},{9,1},{2,10},{10,2},{3,11},{11,3},{4,12},{12,4},... | collective-permute-start | bytes 393224 | tf_op jit(solution)/shard_map/ppermute | solution.py:292
  19.0 2.3 %collective-permute-done.2.g2 = bf16[4,128,128]{2,1,0:T(8,128)(2,1)S(1)} collective-permute-done((bf16[4,128,128]{2,1,0:T(8,128)(2,1)S(1)}, bf16[4,128,128]{2,1,0:T(8,128)(2,1)S(1)}, u32[]{:S(2)}, u32[]{:S(2)}) %collective-permute-start.2) | collective-permute-done | bytes 131104 | tf_op jit(solution)/shard_map/ppermute | solution.py:304
  24.5 2.6 %collective-permute-start.5 = (bf16[4,128,128]{2,1,0:T(8,128)(2,1)S(1)}, bf16[4,128,128]{2,1,0:T(8,128)(2,1)S(1)}, u32[]{:S(2)}, u32[]{:S(2)}) collective-permute-start(bf16[4,128,128]{2,1,0:T(8,128)(2,1)S(1)} %get-tuple-element.50), channel_id=1, source_target_pairs={{0,128},{8,40},{16,144},{24,56},{32,160},{40,8},{48,176},{56,24},{... | collective-permute-start | bytes 393224 | tf_op jit(solution)/shard_map/ppermute | solution.py:304
  28.5 2.4 %collective-permute-done.5.g2 = bf16[4,128,128]{2,1,0:T(8,128)(2,1)S(1)} collective-permute-done((bf16[4,128,128]{2,1,0:T(8,128)(2,1)S(1)}, bf16[4,128,128]{2,1,0:T(8,128)(2,1)S(1)}, u32[]{:S(2)}, u32[]{:S(2)}) %collective-permute-start.5) | collective-permute-done | bytes 131104 | tf_op jit(solution)/shard_map/ppermute | solution.py:304
  31.7 3.5 %collective-permute-start.7 = (bf16[4,128,128]{2,1,0:T(8,128)(2,1)S(1)}, bf16[4,128,128]{2,1,0:T(8,128)(2,1)S(1)}, u32[]{:S(2)}, u32[]{:S(2)}) collective-permute-start(bf16[4,128,128]{2,1,0:T(8,128)(2,1)S(1)} %get-tuple-element.53), channel_id=1, source_target_pairs={{0,8},{8,0},{1,9},{9,1},{2,10},{10,2},{3,11},{11,3},{4,12},{12,4},... | collective-permute-start | bytes 393224 | tf_op jit(solution)/shard_map/ppermute | solution.py:292
  40.0 3.9 %shard_map.98 = bf16[8,384,512]{2,1,0:T(8,128)(2,1)} custom-call(bf16[384,512]{1,0:T(8,128)(2,1)S(1)} %bitcast.8, bf16[512,4096]{1,0:T(8,128)(2,1)S(1)} %copy-done), custom_call_target="tpu_custom_call" | custom-call | flops 1610612736 | bytes 7733248 | tf_op jit(solution)/shard_map/pallas_call | solution.py:33
  45.0 5.6 %collective-permute-start.12 = (bf16[384,512]{1,0:T(8,128)(2,1)S(1)}, bf16[384,512]{1,0:T(8,128)(2,1)S(1)}, u32[]{:S(2)}, u32[]{:S(2)}) collective-permute-start(bf16[384,512]{1,0:T(8,128)(2,1)S(1)} %bitcast.12), channel_id=1, source_target_pairs={{0,7},{1,0},{2,1},{3,2},{4,3},{5,4},{6,5},{7,6},{8,15},{9,8},{10,9... | collective-permute-start | bytes 1179656 | tf_op jit(solution)/shard_map/ppermute | solution.py:292
  50.5 12.4 %collective-permute-done.12.refs_2_ = bf16[384,512]{1,0:T(8,128)(2,1)S(1)} collective-permute-done((bf16[384,512]{1,0:T(8,128)(2,1)S(1)}, bf16[384,512]{1,0:T(8,128)(2,1)S(1)}, u32[]{:S(2)}, u32[]{:S(2)}) %collective-permute-start.12) | collective-permute-done | bytes 393248 | tf_op jit(solution)/shard_map/ppermute | solution.py:292
  62.9 3.5 %collective-permute-start.13 = (bf16[384,512]{1,0:T(8,128)(2,1)S(1)}, bf16[384,512]{1,0:T(8,128)(2,1)S(1)}, u32[]{:S(2)}, u32[]{:S(2)}) collective-permute-start(bf16[384,512]{1,0:T(8,128)(2,1)S(1)} %collective-permute-done.12.refs_2_), channel_id=1, source_target_pairs={{0,7},{1,0},{2,1},{3,2},{4,3},{5,4},{6,5},{7,6},{8,15},{9,8},{10,9... | collective-permute-start | bytes 1179656 | tf_op jit(solution)/shard_map/ppermute | solution.py:292
  66.4 15.9 %collective-permute-done.13.refs_4_ = bf16[384,512]{1,0:T(8,128)(2,1)S(1)} collective-permute-done((bf16[384,512]{1,0:T(8,128)(2,1)S(1)}, bf16[384,512]{1,0:T(8,128)(2,1)S(1)}, u32[]{:S(2)}, u32[]{:S(2)}) %collective-permute-start.13) | collective-permute-done | bytes 393248 | tf_op jit(solution)/shard_map/ppermute | solution.py:292
  82.4 3.5 %collective-permute-start.14 = (bf16[384,512]{1,0:T(8,128)(2,1)S(1)}, bf16[384,512]{1,0:T(8,128)(2,1)S(1)}, u32[]{:S(2)}, u32[]{:S(2)}) collective-permute-start(bf16[384,512]{1,0:T(8,128)(2,1)S(1)} %collective-permute-done.13.refs_4_), channel_id=1, source_target_pairs={{0,7},{1,0},{2,1},{3,2},{4,3},{5,4},{6,5},{7,6},{8,15},{9,8},{10,9... | collective-permute-start | bytes 1179656 | tf_op jit(solution)/shard_map/ppermute | solution.py:292
  86.7 15.7 %collective-permute-done.14.x_ref.refs_6_ = bf16[384,512]{1,0:T(8,128)(2,1)S(1)} collective-permute-done((bf16[384,512]{1,0:T(8,128)(2,1)S(1)}, bf16[384,512]{1,0:T(8,128)(2,1)S(1)}, u32[]{:S(2)}, u32[]{:S(2)}) %collective-permute-start.14) | collective-permute-done | bytes 393248 | tf_op jit(solution)/shard_map/ppermute | solution.py:292
  102.3 4.3 %collective-permute-done.10.x_ref.refs_5_ = bf16[384,512]{1,0:T(8,128)(2,1)S(1)} collective-permute-done((bf16[384,512]{1,0:T(8,128)(2,1)S(1)}, bf16[384,512]{1,0:T(8,128)(2,1)S(1)}, u32[]{:S(2)}, u32[]{:S(2)}) %collective-permute-start.10) | collective-permute-done | bytes 393248 | tf_op jit(solution)/shard_map/ppermute | solution.py:292
  108.5 3.1 %collective-permute-start.24 = (bf16[4,4,512,128]{3,2,1,0:T(8,128)(2,1)S(1)}, bf16[4,4,512,128]{3,2,1,0:T(8,128)(2,1)S(1)}, u32[]{:S(2)}, u32[]{:S(2)}) collective-permute-start(bf16[4,4,512,128]{3,2,1,0:T(8,128)(2,1)S(1)} %shard_map.108), channel_id=1, source_target_pairs={{0,8},{8,0},{1,9},{9,1},{2,10},{10,2},{3,11},{11,3},{4,12},{12,4},... | collective-permute-start | bytes 6291464 | tf_op jit(solution)/shard_map/ppermute | solution.py:292
  113.2 4.9 %collective-permute-done.15.refs_1_.l4.refs_8_ = bf16[384,256]{1,0:T(8,128)(2,1)S(1)} collective-permute-done((bf16[384,256]{1,0:T(8,128)(2,1)S(1)}, bf16[384,256]{1,0:T(8,128)(2,1)S(1)}, u32[]{:S(2)}, u32[]{:S(2)}) %collective-permute-start.15) | collective-permute-done | bytes 196640 | tf_op jit(solution)/shard_map/ppermute | solution.py:292
  127.0 2.4 %collective-permute-start.19 = (bf16[4,128,128]{2,1,0:T(8,128)(2,1)S(1)}, bf16[4,128,128]{2,1,0:T(8,128)(2,1)S(1)}, u32[]{:S(2)}, u32[]{:S(2)}) collective-permute-start(bf16[4,128,128]{2,1,0:T(8,128)(2,1)S(1)} %shard_map.104.t_ref), channel_id=1, source_target_pairs={{0,48},{8,200},{16,0},{24,216},{32,16},{40,232},{48,32},{56,248},{... | collective-permute-start | bytes 393224 | tf_op jit(solution)/shard_map/ppermute | solution.py:304
  134.4 2.4 %collective-permute-start.18 = (bf16[4,128,128]{2,1,0:T(8,128)(2,1)S(1)}, bf16[4,128,128]{2,1,0:T(8,128)(2,1)S(1)}, u32[]{:S(2)}, u32[]{:S(2)}) collective-permute-start(bf16[4,128,128]{2,1,0:T(8,128)(2,1)S(1)} %shard_map.104.t_ref), channel_id=1, source_target_pairs={{0,32},{8,136},{16,48},{24,152},{32,0},{40,168},{48,16},{56,184},{... | collective-permute-start | bytes 393224 | tf_op jit(solution)/shard_map/ppermute | solution.py:304
  136.8 9.9 %collective-permute-done.18.g2 = bf16[4,128,128]{2,1,0:T(8,128)(2,1)S(1)} collective-permute-done((bf16[4,128,128]{2,1,0:T(8,128)(2,1)S(1)}, bf16[4,128,128]{2,1,0:T(8,128)(2,1)S(1)}, u32[]{:S(2)}, u32[]{:S(2)}) %collective-permute-start.18) | collective-permute-done | bytes 131104 | tf_op jit(solution)/shard_map/ppermute | solution.py:304
  146.6 2.8 %collective-permute-done.17.g1 = bf16[4,128,128]{2,1,0:T(8,128)(2,1)S(1)} collective-permute-done((bf16[4,128,128]{2,1,0:T(8,128)(2,1)S(1)}, bf16[4,128,128]{2,1,0:T(8,128)(2,1)S(1)}, u32[]{:S(2)}, u32[]{:S(2)}) %collective-permute-start.17) | collective-permute-done | bytes 131104 | tf_op jit(solution)/shard_map/ppermute | solution.py:304
  150.3 6.6 %collective-permute-done.20.g1 = bf16[4,128,128]{2,1,0:T(8,128)(2,1)S(1)} collective-permute-done((bf16[4,128,128]{2,1,0:T(8,128)(2,1)S(1)}, bf16[4,128,128]{2,1,0:T(8,128)(2,1)S(1)}, u32[]{:S(2)}, u32[]{:S(2)}) %collective-permute-start.20) | collective-permute-done | bytes 131104 | tf_op jit(solution)/shard_map/ppermute | solution.py:304
  157.0 3.8 %collective-permute-done.22.g3 = bf16[4,128,128]{2,1,0:T(8,128)(2,1)S(1)} collective-permute-done((bf16[4,128,128]{2,1,0:T(8,128)(2,1)S(1)}, bf16[4,128,128]{2,1,0:T(8,128)(2,1)S(1)}, u32[]{:S(2)}, u32[]{:S(2)}) %collective-permute-start.22) | collective-permute-done | bytes 131104 | tf_op jit(solution)/shard_map/ppermute | solution.py:304
  162.7 2.3 %collective-permute-start.30 = (bf16[512,128]{1,0:T(8,128)(2,1)S(1)}, bf16[512,128]{1,0:T(8,128)(2,1)S(1)}, u32[]{:S(2)}, u32[]{:S(2)}) collective-permute-start(bf16[512,128]{1,0:T(8,128)(2,1)S(1)} %get-tuple-element.77), channel_id=1, source_target_pairs={{0,128},{8,40},{16,144},{24,56},{32,160},{40,8},{48,176},{56,24},{... | collective-permute-start | bytes 393224 | tf_op jit(solution)/shard_map/ppermute | solution.py:304
  165.2 3.8 %shard_map.103 = (bf16[2,192,512]{2,1,0:T(8,128)(2,1)}, f32[2,192,512]{2,1,0:T(8,128)S(1)}, f32[2,192,512]{2,1,0:T(8,128)S(1)}) custom-call(s32[4]{0:T(128)S(1)} %pad_add_fusion.place, bf16[2,192,512]{2,1,0:T(8,128)(2,1)S(1)} %copy-done.8, bf16[2,192,512]{2,1,0:T(8,128)(2,1)S(1)} %copy-done.4, bf16[2,192,512]{2,1,0:T(8,128)(2,1)S(1)} %copy-done.6, ...), custom_call_target="tpu_custom_call" | custom-call | flops 251658240 | bytes 4390928 | tf_op jit(solution)/shard_map/pallas_call | solution.py:33
  169.0 2.3 %shard_map.107 = (bf16[2,192,512]{2,1,0:T(8,128)(2,1)}, bf16[2,192,512]{2,1,0:T(8,128)(2,1)}) custom-call(s32[4]{0:T(128)S(1)} %pad_add_fusion.place, bf16[2,192,512]{2,1,0:T(8,128)(2,1)S(1)} %copy-done.4, bf16[2,192,512]{2,1,0:T(8,128)(2,1)S(1)} %copy-done.6, f32[2,192,512]{2,1,0:T(8,128)S(1)} %get-tuple-element.59.ik_ref, ...), custom_call_target="tpu_custom_call" | custom-call | flops 100663296 | bytes 3407888 | tf_op jit(solution)/shard_map/pallas_call | solution.py:33
  (83 shorter events, 41.6 us)
Async XLA Ops:
  7.2 164.9 %reduce-scatter.2.cloned.1.call-start = ((), (), s32[]{:S(2)}) async-start(), calls=%async_computation.1 | async-start | bytes 3538944 | tf_op jit(solution)/shard_map/reduce_scatter | solution.py:428
  16.1 6.5 %collective-permute-start.1 = (bf16[4,128,128]{2,1,0:T(8,128)(2,1)S(1)}, bf16[4,128,128]{2,1,0:T(8,128)(2,1)S(1)}, u32[]{:S(2)}, u32[]{:S(2)}) collective-permute-start(bf16[4,128,128]{2,1,0:T(8,128)(2,1)S(1)} %shard_map.94.t_ref), channel_id=1, source_target_pairs={{0,16},{8,72},{16,32},{24,88},{32,48},{40,104},{48,0},{56,120},{64... | collective-permute-start | bytes 393224 | tf_op jit(solution)/shard_map/ppermute | solution.py:304
  31.7 6.6 %collective-permute-start.7 = (bf16[4,128,128]{2,1,0:T(8,128)(2,1)S(1)}, bf16[4,128,128]{2,1,0:T(8,128)(2,1)S(1)}, u32[]{:S(2)}, u32[]{:S(2)}) collective-permute-start(bf16[4,128,128]{2,1,0:T(8,128)(2,1)S(1)} %get-tuple-element.53), channel_id=1, source_target_pairs={{0,8},{8,0},{1,9},{9,1},{2,10},{10,2},{3,11},{11,3},{4,12},{12,4},... | collective-permute-start | bytes 393224 | tf_op jit(solution)/shard_map/ppermute | solution.py:292
  45.0 17.9 %collective-permute-start.12 = (bf16[384,512]{1,0:T(8,128)(2,1)S(1)}, bf16[384,512]{1,0:T(8,128)(2,1)S(1)}, u32[]{:S(2)}, u32[]{:S(2)}) collective-permute-start(bf16[384,512]{1,0:T(8,128)(2,1)S(1)} %bitcast.12), channel_id=1, source_target_pairs={{0,7},{1,0},{2,1},{3,2},{4,3},{5,4},{6,5},{7,6},{8,15},{9,8},{10,9... | collective-permute-start | bytes 1179656 | tf_op jit(solution)/shard_map/ppermute | solution.py:292
  50.5 15.9 %collective-permute-start.8 = (bf16[384,512]{1,0:T(8,128)(2,1)S(1)}, bf16[384,512]{1,0:T(8,128)(2,1)S(1)}, u32[]{:S(2)}, u32[]{:S(2)}) collective-permute-start(bf16[384,512]{1,0:T(8,128)(2,1)S(1)} %bitcast.13), channel_id=1, source_target_pairs={{0,1},{1,2},{2,3},{3,4},{4,5},{5,6},{6,7},{7,0},{8,9},{9,10},{10,1... | collective-permute-start | bytes 1179656 | tf_op jit(solution)/shard_map/ppermute | solution.py:292
  62.9 19.5 %collective-permute-start.13 = (bf16[384,512]{1,0:T(8,128)(2,1)S(1)}, bf16[384,512]{1,0:T(8,128)(2,1)S(1)}, u32[]{:S(2)}, u32[]{:S(2)}) collective-permute-start(bf16[384,512]{1,0:T(8,128)(2,1)S(1)} %collective-permute-done.12.refs_2_), channel_id=1, source_target_pairs={{0,7},{1,0},{2,1},{3,2},{4,3},{5,4},{6,5},{7,6},{8,15},{9,8},{10,9... | collective-permute-start | bytes 1179656 | tf_op jit(solution)/shard_map/ppermute | solution.py:292
  66.4 20.2 %collective-permute-start.9 = (bf16[384,512]{1,0:T(8,128)(2,1)S(1)}, bf16[384,512]{1,0:T(8,128)(2,1)S(1)}, u32[]{:S(2)}, u32[]{:S(2)}) collective-permute-start(bf16[384,512]{1,0:T(8,128)(2,1)S(1)} %collective-permute-done.8.refs_1_), channel_id=1, source_target_pairs={{0,1},{1,2},{2,3},{3,4},{4,5},{5,6},{6,7},{7,0},{8,9},{9,10},{10,1... | collective-permute-start | bytes 1179656 | tf_op jit(solution)/shard_map/ppermute | solution.py:292
  82.4 20.0 %collective-permute-start.14 = (bf16[384,512]{1,0:T(8,128)(2,1)S(1)}, bf16[384,512]{1,0:T(8,128)(2,1)S(1)}, u32[]{:S(2)}, u32[]{:S(2)}) collective-permute-start(bf16[384,512]{1,0:T(8,128)(2,1)S(1)} %collective-permute-done.13.refs_4_), channel_id=1, source_target_pairs={{0,7},{1,0},{2,1},{3,2},{4,3},{5,4},{6,5},{7,6},{8,15},{9,8},{10,9... | collective-permute-start | bytes 1179656 | tf_op jit(solution)/shard_map/ppermute | solution.py:292
  86.6 20.0 %collective-permute-start.10 = (bf16[384,512]{1,0:T(8,128)(2,1)S(1)}, bf16[384,512]{1,0:T(8,128)(2,1)S(1)}, u32[]{:S(2)}, u32[]{:S(2)}) collective-permute-start(bf16[384,512]{1,0:T(8,128)(2,1)S(1)} %collective-permute-done.9.refs_3_), channel_id=1, source_target_pairs={{0,1},{1,2},{2,3},{3,4},{4,5},{5,6},{6,7},{7,0},{8,9},{9,10},{10,1... | collective-permute-start | bytes 1179656 | tf_op jit(solution)/shard_map/ppermute | solution.py:292
  108.5 21.0 %collective-permute-start.24 = (bf16[4,4,512,128]{3,2,1,0:T(8,128)(2,1)S(1)}, bf16[4,4,512,128]{3,2,1,0:T(8,128)(2,1)S(1)}, u32[]{:S(2)}, u32[]{:S(2)}) collective-permute-start(bf16[4,4,512,128]{3,2,1,0:T(8,128)(2,1)S(1)} %shard_map.108), channel_id=1, source_target_pairs={{0,8},{8,0},{1,9},{9,1},{2,10},{10,2},{3,11},{11,3},{4,12},{12,4},... | collective-permute-start | bytes 6291464 | tf_op jit(solution)/shard_map/ppermute | solution.py:292
  111.5 6.5 %collective-permute-start.15 = (bf16[384,256]{1,0:T(8,128)(2,1)S(1)}, bf16[384,256]{1,0:T(8,128)(2,1)S(1)}, u32[]{:S(2)}, u32[]{:S(2)}) collective-permute-start(bf16[384,256]{1,0:T(8,128)(2,1)S(1)} %shard_map.100), channel_id=1, source_target_pairs={{0,7},{1,0},{2,1},{3,2},{4,3},{5,4},{6,5},{7,6},{8,15},{9,8},{10,9... | collective-permute-start | bytes 589832 | tf_op jit(solution)/shard_map/ppermute | solution.py:292
  111.7 7.7 %collective-permute-start.11 = (bf16[384,256]{1,0:T(8,128)(2,1)S(1)}, bf16[384,256]{1,0:T(8,128)(2,1)S(1)}, u32[]{:S(2)}, u32[]{:S(2)}) collective-permute-start(bf16[384,256]{1,0:T(8,128)(2,1)S(1)} %shard_map.99), channel_id=1, source_target_pairs={{0,1},{1,2},{2,3},{3,4},{4,5},{5,6},{6,7},{7,0},{8,9},{9,10},{10,1... | collective-permute-start | bytes 589832 | tf_op jit(solution)/shard_map/ppermute | solution.py:292
  120.3 9.2 %collective-permute-start.25 = (bf16[2,512,128]{2,1,0:T(8,128)(2,1)S(1)}, bf16[2,512,128]{2,1,0:T(8,128)(2,1)S(1)}, u32[]{:S(2)}, u32[]{:S(2)}) collective-permute-start(bf16[2,512,128]{2,1,0:T(8,128)(2,1)S(1)} %shard_map.109), channel_id=1, source_target_pairs={{0,8},{8,0},{1,9},{9,1},{2,10},{10,2},{3,11},{11,3},{4,12},{12,4},... | collective-permute-start | bytes 786440 | tf_op jit(solution)/shard_map/ppermute | solution.py:292
  127.0 9.8 %collective-permute-start.19 = (bf16[4,128,128]{2,1,0:T(8,128)(2,1)S(1)}, bf16[4,128,128]{2,1,0:T(8,128)(2,1)S(1)}, u32[]{:S(2)}, u32[]{:S(2)}) collective-permute-start(bf16[4,128,128]{2,1,0:T(8,128)(2,1)S(1)} %shard_map.104.t_ref), channel_id=1, source_target_pairs={{0,48},{8,200},{16,0},{24,216},{32,16},{40,232},{48,32},{56,248},{... | collective-permute-start | bytes 393224 | tf_op jit(solution)/shard_map/ppermute | solution.py:304
  131.6 29.9 %collective-permute-start.26 = (bf16[4,512,128]{2,1,0:T(8,128)(2,1)S(1)}, bf16[4,512,128]{2,1,0:T(8,128)(2,1)S(1)}, u32[]{:S(2)}, u32[]{:S(2)}) collective-permute-start(bf16[4,512,128]{2,1,0:T(8,128)(2,1)S(1)} %get-tuple-element.72), channel_id=1, source_target_pairs={{0,16},{8,72},{16,32},{24,88},{32,48},{40,104},{48,0},{56,120},{64... | collective-permute-start | bytes 1572872 | tf_op jit(solution)/shard_map/ppermute | solution.py:304
  131.7 29.8 %collective-permute-start.27 = (bf16[4,512,128]{2,1,0:T(8,128)(2,1)S(1)}, bf16[4,512,128]{2,1,0:T(8,128)(2,1)S(1)}, u32[]{:S(2)}, u32[]{:S(2)}) collective-permute-start(bf16[4,512,128]{2,1,0:T(8,128)(2,1)S(1)} %get-tuple-element.73), channel_id=1, source_target_pairs={{0,32},{8,136},{16,48},{24,152},{32,0},{40,168},{48,16},{56,184},{... | collective-permute-start | bytes 1572872 | tf_op jit(solution)/shard_map/ppermute | solution.py:304
  132.9 28.6 %collective-permute-start.28 = (bf16[4,512,128]{2,1,0:T(8,128)(2,1)S(1)}, bf16[4,512,128]{2,1,0:T(8,128)(2,1)S(1)}, u32[]{:S(2)}, u32[]{:S(2)}) collective-permute-start(bf16[4,512,128]{2,1,0:T(8,128)(2,1)S(1)} %get-tuple-element.74), channel_id=1, source_target_pairs={{0,48},{8,200},{16,0},{24,216},{32,16},{40,232},{48,32},{56,248},{... | collective-permute-start | bytes 1572872 | tf_op jit(solution)/shard_map/ppermute | solution.py:304
  134.4 12.2 %collective-permute-start.18 = (bf16[4,128,128]{2,1,0:T(8,128)(2,1)S(1)}, bf16[4,128,128]{2,1,0:T(8,128)(2,1)S(1)}, u32[]{:S(2)}, u32[]{:S(2)}) collective-permute-start(bf16[4,128,128]{2,1,0:T(8,128)(2,1)S(1)} %shard_map.104.t_ref), channel_id=1, source_target_pairs={{0,32},{8,136},{16,48},{24,152},{32,0},{40,168},{48,16},{56,184},{... | collective-permute-start | bytes 393224 | tf_op jit(solution)/shard_map/ppermute | solution.py:304
  136.8 12.6 %collective-permute-start.17 = (bf16[4,128,128]{2,1,0:T(8,128)(2,1)S(1)}, bf16[4,128,128]{2,1,0:T(8,128)(2,1)S(1)}, u32[]{:S(2)}, u32[]{:S(2)}) collective-permute-start(bf16[4,128,128]{2,1,0:T(8,128)(2,1)S(1)} %shard_map.104.t_ref), channel_id=1, source_target_pairs={{0,16},{8,72},{16,32},{24,88},{32,48},{40,104},{48,0},{56,120},{64... | collective-permute-start | bytes 393224 | tf_op jit(solution)/shard_map/ppermute | solution.py:304
  150.1 6.8 %collective-permute-start.20 = (bf16[4,128,128]{2,1,0:T(8,128)(2,1)S(1)}, bf16[4,128,128]{2,1,0:T(8,128)(2,1)S(1)}, u32[]{:S(2)}, u32[]{:S(2)}) collective-permute-start(bf16[4,128,128]{2,1,0:T(8,128)(2,1)S(1)} %get-tuple-element.64), channel_id=1, source_target_pairs={{0,64},{8,24},{16,80},{24,40},{32,96},{40,56},{48,112},{56,8},{64,... | collective-permute-start | bytes 393224 | tf_op jit(solution)/shard_map/ppermute | solution.py:304
  150.2 6.7 %collective-permute-start.21 = (bf16[4,128,128]{2,1,0:T(8,128)(2,1)S(1)}, bf16[4,128,128]{2,1,0:T(8,128)(2,1)S(1)}, u32[]{:S(2)}, u32[]{:S(2)}) collective-permute-start(bf16[4,128,128]{2,1,0:T(8,128)(2,1)S(1)} %get-tuple-element.65), channel_id=1, source_target_pairs={{0,128},{8,40},{16,144},{24,56},{32,160},{40,8},{48,176},{56,24},{... | collective-permute-start | bytes 393224 | tf_op jit(solution)/shard_map/ppermute | solution.py:304
  161.4 7.6 %collective-permute-start.23 = (bf16[4,128,128]{2,1,0:T(8,128)(2,1)S(1)}, bf16[4,128,128]{2,1,0:T(8,128)(2,1)S(1)}, u32[]{:S(2)}, u32[]{:S(2)}) collective-permute-start(bf16[4,128,128]{2,1,0:T(8,128)(2,1)S(1)} %get-tuple-element.68), channel_id=1, source_target_pairs={{0,8},{8,0},{1,9},{9,1},{2,10},{10,2},{3,11},{11,3},{4,12},{12,4},... | collective-permute-start | bytes 393224 | tf_op jit(solution)/shard_map/ppermute | solution.py:292
  162.4 8.9 %collective-permute-start.29 = (bf16[512,128]{1,0:T(8,128)(2,1)S(1)}, bf16[512,128]{1,0:T(8,128)(2,1)S(1)}, u32[]{:S(2)}, u32[]{:S(2)}) collective-permute-start(bf16[512,128]{1,0:T(8,128)(2,1)S(1)} %get-tuple-element.76), channel_id=1, source_target_pairs={{0,64},{8,24},{16,80},{24,40},{32,96},{40,56},{48,112},{56,8},{64,... | collective-permute-start | bytes 393224 | tf_op jit(solution)/shard_map/ppermute | solution.py:304
  162.7 8.6 %collective-permute-start.30 = (bf16[512,128]{1,0:T(8,128)(2,1)S(1)}, bf16[512,128]{1,0:T(8,128)(2,1)S(1)}, u32[]{:S(2)}, u32[]{:S(2)}) collective-permute-start(bf16[512,128]{1,0:T(8,128)(2,1)S(1)} %get-tuple-element.77), channel_id=1, source_target_pairs={{0,128},{8,40},{16,144},{24,56},{32,160},{40,8},{48,176},{56,24},{... | collective-permute-start | bytes 393224 | tf_op jit(solution)/shard_map/ppermute | solution.py:304
  (18 other events, 224.7 us)
Sparse Core Ops, SparseCore 0:
  44.1 65.9 reduce-scatter.1

commit v4 on v3

--- a/solution.py
+++ b/solution.py
@@ -23,11 +23,12 @@
     return lax.dot_general(a, b, (((ca,), (cb,)), ((), ())), preferred_element_type=F32)
 
 
-def call(body, outs, args, flops, scalar=False, scratch=()):
+def call(body, outs, args, flops, scalar=False, scratch=(), last=VMEM):
     size = sum(a.size * a.dtype.itemsize for a in args)
     size += sum(o.size * o.dtype.itemsize for o in outs)
     cost = pl.CostEstimate(flops=flops, bytes_accessed=size, transcendentals=0)
     specs = [pl.BlockSpec(memory_space=VMEM)] * len(args)
+    specs[-1] = pl.BlockSpec(memory_space=last)
     if scalar:
         specs[0] = pl.BlockSpec(memory_space=SMEM)
     return pl.pallas_call(
@@ -57,10 +58,13 @@
         send_ref[h] = dot(left[1 - mc, :, s], right[1 - mc, :, s], 0, 0).astype(BF16)
 
 
-def state_body(place, k_ref, v_ref, keep_ref, send_ref, k_out, v_out):
+def state_body(place, k_ref, v_ref, q_hbm, keep_ref, send_ref, k_out, v_out, q_out, sem):
+    copy = pltpu.make_async_copy(q_hbm, q_out, sem)
+    copy.start()
     local_states(place, k_ref, v_ref, keep_ref, send_ref)
     k_out[...] = k_ref[...]
     v_out[...] = v_ref[...]
+    copy.wait()
 
 
 def chip_body(keep_ref, got_ref, out_ref):
@@ -120,17 +124,18 @@
     lax.fori_loop(0, 2, body, 0)
 
 
-def intra_body(q_ref, k_ref, v_ref, scores_ref, intra_ref, q_out):
-    q_out[...] = q_ref[...]
+def masked_scores(lower, left, right):
+    return jnp.where(lower, dot(left, right, 1, 1) * SCALE, 0.0).astype(BF16)
+
+
+def intra_body(q_ref, k_ref, v_ref, intra_ref):
     lower = lower_mask(q_ref.shape[1])
 
     def step(b, h, i, s):
-        raw = dot(q_ref[b, :, s], k_ref[b, :, s], 1, 1) * SCALE
-        scores = jnp.where(lower, raw, 0.0).astype(BF16)
-        scores_ref[i] = scores
+        scores = masked_scores(lower, q_ref[b, :, s], k_ref[b, :, s])
         intra_ref[b, :, s] = dot(scores, v_ref[b, :, s], 1, 0)
 
-    each_head(q_ref.shape[2], step)
+    each_batch(q_ref.shape[2], step)
 
 
 def forward_body(place, q_ref, intra_ref, so_ref, sr_ref, normed_ref, attended_ref):
@@ -264,16 +269,17 @@
         copy.wait()
 
 
-def inner_body(place, q_ref, k_ref, v_ref, sc_ref, ag_ref, so, sr, dq_ref, dk_ref, dv_ref):
+def inner_body(place, q_ref, k_ref, v_ref, ag_ref, so, sr, dq_ref, dk_ref, dv_ref):
     lower = lower_mask(q_ref.shape[1])
 
     def step(b, h, i, s):
         ag = ag_ref[b, :, s]
-        sg = jnp.where(lower, dot(ag, v_ref[b, :, s], 1, 1) * SCALE, 0.0).astype(BF16)
+        sg = masked_scores(lower, ag, v_ref[b, :, s])
+        scores = masked_scores(lower, q_ref[b, :, s], k_ref[b, :, s])
         earlier = pick_state(place, so, sr, b, h)
         dq_ref[b, :, s] = (dot(sg, k_ref[b, :, s], 1, 0) + SCALE * dot(ag, earlier, 1, 1)).astype(BF16)
         dk_ref[b, :, s] = dot(sg, q_ref[b, :, s], 0, 0)
-        dv_ref[b, :, s] = dot(sc_ref[i], ag, 0, 0)
+        dv_ref[b, :, s] = dot(scores, ag, 0, 0)
 
     each_batch(q_ref.shape[2], step)
 
@@ -401,19 +407,21 @@
     place = jnp.stack([mx, my, mc, mz]).astype(jnp.int32)
     mat_flops = 2 * n_mat * length * DH * DH
     pair = [shape(half, F32), shape(half, BF16)]
-    keep, send, near_keys, near_values = call(
+    keep, send, near_keys, near_values, near_queries = call(
         state_body,
-        pair + [shape(queries.shape, BF16)] * 2,
-        [place, key_rows, value_rows],
+        pair + [shape(queries.shape, BF16)] * 3,
+        [place, key_rows, value_rows, queries],
         mat_flops,
         True,
-    )
-    scores, intra, near_queries = call(
+        [pltpu.SemaphoreType.DMA],
+        pltpu.HBM,
+    )
+    intra = call(
         intra_body,
-        [shape((n_mat, length, length), BF16), shape(queries.shape, F32), shape(queries.shape, BF16)],
-        [queries, near_keys, near_values],
+        [shape(queries.shape, F32)],
+        [near_queries, near_keys, near_values],
         3 * mat_flops,
-    )
+    )[0]
     state = exclusive(place, keep, send, False)
     normed, attended = call(
         forward_body,
@@ -450,7 +458,7 @@
     query_grad, inner_key, inner_value = call(
         inner_body,
         [shape(queries.shape, BF16)] + [shape(queries.shape, F32)] * 2,
-        [place, queries, key_rows, value_rows, scores, attended_grad, *state],
+        [place, queries, key_rows, value_rows, attended_grad, *state],
         5 * mat_flops,
         True,
     )

time: 179 us -> 176 us (0.983)
  waiting for transfers between devices: 89.4 us -> 75.7 us
  starting transfers between devices: 42.6 us -> 53.6 us
    ppermute x18, waiting for transfers between devices: 31.8 us -> 24.7 us  [shift_by_core(): lax.ppermute(value, CTX, [(index(*p), index(*target(*p))) for p in places])]
    ppermute x18, starting transfers between devices: 17.3 us -> 24.1 us  [shift_by_core(): lax.ppermute(value, CTX, [(index(*p), index(*target(*p))) for p in places])]
    ppermute x14, waiting for transfers between devices: 57.6 us -> 51 us  [shift(): return lax.ppermute(value, axis, [(i, (i + step) % n) for i in range(n)])]
    ppermute x14, starting transfers between devices: 25.2 us -> 29.5 us  [shift(): return lax.ppermute(value, axis, [(i, (i + step) % n) for i in range(n)])]
  transfers between devices with their start and end apart: 33 -> 33, of which waited for: 19 -> 18; matrix products, arithmetic and copies ran while one was open for 0% -> 0% of each run, Pallas kernels for 11% -> 11%
where the time goes in v4:
time: 176 us; the launch traced here: 175 us
  waiting for transfers between devices  75.7 us (43%)
  starting transfers between devices  53.6 us (30%)
  Pallas kernels  27.8 us (16%)
  between operations  14.3 us (8%)
  local copies, waits for them, and re-layouts  3.99 us (2%)
    ppermute x14, waiting for transfers between devices, shift(): return lax.ppermute(value, axis, [(i, (i + step) % n) for i in range(n)])  51 us
    ppermute x14, starting transfers between devices, shift(): return lax.ppermute(value, axis, [(i, (i + step) % n) for i in range(n)])  29.5 us
    pallas_call x21, Pallas kernels, call(): pl.pallas_call(body, out_shape=outs, in_specs=specs, out_specs=[pl.BlockS...  27.8 us
    ppermute x18, waiting for transfers between devices, shift_by_core(): lax.ppermute(value, CTX, [(index(*p), index(*target(*p))) for p in places])  24.7 us
    ppermute x18, starting transfers between devices, shift_by_core(): lax.ppermute(value, CTX, [(index(*p), index(*target(*p))) for p in places])  24.1 us
    unnamed x18, local copies, waits for them, and re-layouts  3.99 us
  transfers between devices with their start and end apart: 33, of which 18 were waited for; matrix products, arithmetic and copies ran while one was open for 0% of the time, Pallas kernels for 11%

profile of v4, /device:TPU:1, one launch (start us, length us, event | category | flops | bytes accessed | tf_op | source)
XLA Modules:
  0.0 175.4 jit_solution(6315950160866731614)
XLA Ops:
  11.4 3.3 %collective-permute-start = (bf16[4,128,128]{2,1,0:T(8,128)(2,1)S(1)}, bf16[4,128,128]{2,1,0:T(8,128)(2,1)S(1)}, u32[]{:S(2)}, u32[]{:S(2)}) collective-permute-start(bf16[4,128,128]{2,1,0:T(8,128)(2,1)S(1)} %get-tuple-element.44), channel_id=1, source_target_pairs={{0,8},{8,0},{1,9},{9,1},{2,10},{10,2},{3,11},{11,3},{4,12},{12,4},... | collective-permute-start | bytes 393224 | tf_op jit(solution)/shard_map/ppermute | solution.py:298
  18.9 3.6 %collective-permute-done.1.g1 = bf16[4,128,128]{2,1,0:T(8,128)(2,1)S(1)} collective-permute-done((bf16[4,128,128]{2,1,0:T(8,128)(2,1)S(1)}, bf16[4,128,128]{2,1,0:T(8,128)(2,1)S(1)}, u32[]{:S(2)}, u32[]{:S(2)}) %collective-permute-start.1) | collective-permute-done | bytes 131104 | tf_op jit(solution)/shard_map/ppermute | solution.py:310
  24.0 2.6 %collective-permute-start.5 = (bf16[4,128,128]{2,1,0:T(8,128)(2,1)S(1)}, bf16[4,128,128]{2,1,0:T(8,128)(2,1)S(1)}, u32[]{:S(2)}, u32[]{:S(2)}) collective-permute-start(bf16[4,128,128]{2,1,0:T(8,128)(2,1)S(1)} %get-tuple-element.47), channel_id=1, source_target_pairs={{0,128},{8,40},{16,144},{24,56},{32,160},{40,8},{48,176},{56,24},{... | collective-permute-start | bytes 393224 | tf_op jit(solution)/shard_map/ppermute | solution.py:310
  31.8 2.8 %collective-permute-start.7 = (bf16[4,128,128]{2,1,0:T(8,128)(2,1)S(1)}, bf16[4,128,128]{2,1,0:T(8,128)(2,1)S(1)}, u32[]{:S(2)}, u32[]{:S(2)}) collective-permute-start(bf16[4,128,128]{2,1,0:T(8,128)(2,1)S(1)} %get-tuple-element.50), channel_id=1, source_target_pairs={{0,8},{8,0},{1,9},{9,1},{2,10},{10,2},{3,11},{11,3},{4,12},{12,4},... | collective-permute-start | bytes 393224 | tf_op jit(solution)/shard_map/ppermute | solution.py:298
  37.7 3.9 %shard_map.98 = bf16[8,384,512]{2,1,0:T(8,128)(2,1)} custom-call(bf16[384,512]{1,0:T(8,128)(2,1)S(1)} %bitcast.8, bf16[512,4096]{1,0:T(8,128)(2,1)S(1)} %copy-done), custom_call_target="tpu_custom_call" | custom-call | flops 1610612736 | bytes 7733248 | tf_op jit(solution)/shard_map/pallas_call | solution.py:34
  44.2 3.9 %collective-permute-start.12 = (bf16[384,512]{1,0:T(8,128)(2,1)S(1)}, bf16[384,512]{1,0:T(8,128)(2,1)S(1)}, u32[]{:S(2)}, u32[]{:S(2)}) collective-permute-start(bf16[384,512]{1,0:T(8,128)(2,1)S(1)} %bitcast.13), channel_id=1, source_target_pairs={{0,7},{1,0},{2,1},{3,2},{4,3},{5,4},{6,5},{7,6},{8,15},{9,8},{10,9... | collective-permute-start | bytes 1179656 | tf_op jit(solution)/shard_map/ppermute | solution.py:298
  48.2 9.4 %collective-permute-done.8.refs_1_ = bf16[384,512]{1,0:T(8,128)(2,1)S(1)} collective-permute-done((bf16[384,512]{1,0:T(8,128)(2,1)S(1)}, bf16[384,512]{1,0:T(8,128)(2,1)S(1)}, u32[]{:S(2)}, u32[]{:S(2)}) %collective-permute-start.8) | collective-permute-done | bytes 393248 | tf_op jit(solution)/shard_map/ppermute | solution.py:298
  58.5 3.5 %collective-permute-start.13 = (bf16[384,512]{1,0:T(8,128)(2,1)S(1)}, bf16[384,512]{1,0:T(8,128)(2,1)S(1)}, u32[]{:S(2)}, u32[]{:S(2)}) collective-permute-start(bf16[384,512]{1,0:T(8,128)(2,1)S(1)} %collective-permute-done.12.refs_2_), channel_id=1, source_target_pairs={{0,7},{1,0},{2,1},{3,2},{4,3},{5,4},{6,5},{7,6},{8,15},{9,8},{10,9... | collective-permute-start | bytes 1179656 | tf_op jit(solution)/shard_map/ppermute | solution.py:298
  62.0 16.3 %collective-permute-done.9.refs_3_ = bf16[384,512]{1,0:T(8,128)(2,1)S(1)} collective-permute-done((bf16[384,512]{1,0:T(8,128)(2,1)S(1)}, bf16[384,512]{1,0:T(8,128)(2,1)S(1)}, u32[]{:S(2)}, u32[]{:S(2)}) %collective-permute-start.9) | collective-permute-done | bytes 393248 | tf_op jit(solution)/shard_map/ppermute | solution.py:298
  78.7 3.5 %collective-permute-start.14 = (bf16[384,512]{1,0:T(8,128)(2,1)S(1)}, bf16[384,512]{1,0:T(8,128)(2,1)S(1)}, u32[]{:S(2)}, u32[]{:S(2)}) collective-permute-start(bf16[384,512]{1,0:T(8,128)(2,1)S(1)} %collective-permute-done.13.refs_4_), channel_id=1, source_target_pairs={{0,7},{1,0},{2,1},{3,2},{4,3},{5,4},{6,5},{7,6},{8,15},{9,8},{10,9... | collective-permute-start | bytes 1179656 | tf_op jit(solution)/shard_map/ppermute | solution.py:298
  82.2 16.5 %collective-permute-done.10.x_ref.refs_5_ = bf16[384,512]{1,0:T(8,128)(2,1)S(1)} collective-permute-done((bf16[384,512]{1,0:T(8,128)(2,1)S(1)}, bf16[384,512]{1,0:T(8,128)(2,1)S(1)}, u32[]{:S(2)}, u32[]{:S(2)}) %collective-permute-start.10) | collective-permute-done | bytes 393248 | tf_op jit(solution)/shard_map/ppermute | solution.py:298
  100.5 3.4 %collective-permute-start.24 = (bf16[4,4,512,128]{3,2,1,0:T(8,128)(2,1)S(1)}, bf16[4,4,512,128]{3,2,1,0:T(8,128)(2,1)S(1)}, u32[]{:S(2)}, u32[]{:S(2)}) collective-permute-start(bf16[4,4,512,128]{3,2,1,0:T(8,128)(2,1)S(1)} %shard_map.108), channel_id=1, source_target_pairs={{0,8},{8,0},{1,9},{9,1},{2,10},{10,2},{3,11},{11,3},{4,12},{12,4},... | collective-permute-start | bytes 6291464 | tf_op jit(solution)/shard_map/ppermute | solution.py:298
  104.1 3.5 %collective-permute-start.15 = (bf16[384,256]{1,0:T(8,128)(2,1)S(1)}, bf16[384,256]{1,0:T(8,128)(2,1)S(1)}, u32[]{:S(2)}, u32[]{:S(2)}) collective-permute-start(bf16[384,256]{1,0:T(8,128)(2,1)S(1)} %shard_map.100), channel_id=1, source_target_pairs={{0,7},{1,0},{2,1},{3,2},{4,3},{5,4},{6,5},{7,6},{8,15},{9,8},{10,9... | collective-permute-start | bytes 589832 | tf_op jit(solution)/shard_map/ppermute | solution.py:298
  107.6 5.1 %collective-permute-done.11.refs_0_.r4.refs_7_ = bf16[384,256]{1,0:T(8,128)(2,1)S(1)} collective-permute-done((bf16[384,256]{1,0:T(8,128)(2,1)S(1)}, bf16[384,256]{1,0:T(8,128)(2,1)S(1)}, u32[]{:S(2)}, u32[]{:S(2)}) %collective-permute-start.11) | collective-permute-done | bytes 196640 | tf_op jit(solution)/shard_map/ppermute | solution.py:298
  114.3 2.2 %shard_map.101.refs_3_ = f32[384,512]{1,0:T(8,128)S(1)} custom-call(s32[4]{0:T(128)S(1)} %pad_add_fusion.place, bf16[384,512]{1,0:T(8,128)(2,1)S(1)} %bitcast.15, bf16[384,512]{1,0:T(8,128)(2,1)S(1)} %collective-permute-done.8.refs_1_, bf16[384,512]{1,0:T(8,128)(2,1)S(1)} %collective-permute-done.12.refs_2_, ...), custom_call_target="tpu_custom_call" | custom-call | flops 1409286144 | bytes 7733264 | tf_op jit(solution)/shard_map/pallas_call | solution.py:34
  116.5 2.1 %shard_map.102 = (bf16[2,192,512]{2,1,0:T(8,128)(2,1)S(1)}, f32[4,128,128]{2,1,0:T(8,128)S(1)}, bf16[4,128,128]{2,1,0:T(8,128)(2,1)S(1)}) custom-call(s32[4]{0:T(128)S(1)} %pad_add_fusion.place, bf16[384,256]{1,0:T(8,128)(2,1)S(1)} %collective-permute-done.11.refs_0_.r4.refs_7_, bf16[384,256]{1,0:T(8,128)(2,1)S(1)} %collective-permute-done.15.refs_1_.l4.refs_8_, ...), custom_call_target="tpu_custom_call" | custom-call | flops 201326592 | bytes 7340048 | tf_op jit(solution)/shard_map/pallas_call | solution.py:34
  120.8 2.2 %shard_map.110 = (bf16[4,512,128]{2,1,0:T(8,128)(2,1)S(1)}, bf16[4,512,128]{2,1,0:T(8,128)(2,1)S(1)}, bf16[4,512,128]{2,1,0:T(8,128)(2,1)S(1)}, bf16[4,512,128]{2,1,0:T(8,128)(2,1)S(1)}) custom-call(s32[4]{0:T(128)S(1)} %pad_add_fusion.place, bf16[384,512]{1,0:T(8,128)(2,1)S(1)} %bitcast.11, bf16[384,512]{1,0:T(8,128)(2,1)S(1)} %bitcast.16, ...), custom_call_target="tpu_custom_call" | custom-call | flops 805306368 | bytes 7995408 | tf_op jit(solution)/shard_map/pallas_call | solution.py:34
  123.4 2.8 %collective-permute-start.27 = (bf16[4,512,128]{2,1,0:T(8,128)(2,1)S(1)}, bf16[4,512,128]{2,1,0:T(8,128)(2,1)S(1)}, u32[]{:S(2)}, u32[]{:S(2)}) collective-permute-start(bf16[4,512,128]{2,1,0:T(8,128)(2,1)S(1)} %get-tuple-element.69), channel_id=1, source_target_pairs={{0,32},{8,136},{16,48},{24,152},{32,0},{40,168},{48,16},{56,184},{... | collective-permute-start | bytes 1572872 | tf_op jit(solution)/shard_map/ppermute | solution.py:310
  130.1 10.0 %collective-permute-done.18.g2 = bf16[4,128,128]{2,1,0:T(8,128)(2,1)S(1)} collective-permute-done((bf16[4,128,128]{2,1,0:T(8,128)(2,1)S(1)}, bf16[4,128,128]{2,1,0:T(8,128)(2,1)S(1)}, u32[]{:S(2)}, u32[]{:S(2)}) %collective-permute-start.18) | collective-permute-done | bytes 131104 | tf_op jit(solution)/shard_map/ppermute | solution.py:310
  142.9 2.9 %collective-permute-start.21 = (bf16[4,128,128]{2,1,0:T(8,128)(2,1)S(1)}, bf16[4,128,128]{2,1,0:T(8,128)(2,1)S(1)}, u32[]{:S(2)}, u32[]{:S(2)}) collective-permute-start(bf16[4,128,128]{2,1,0:T(8,128)(2,1)S(1)} %get-tuple-element.61), channel_id=1, source_target_pairs={{0,128},{8,40},{16,144},{24,56},{32,160},{40,8},{48,176},{56,24},{... | collective-permute-start | bytes 393224 | tf_op jit(solution)/shard_map/ppermute | solution.py:310
  149.5 2.1 %collective-permute-done.22.g3 = bf16[4,128,128]{2,1,0:T(8,128)(2,1)S(1)} collective-permute-done((bf16[4,128,128]{2,1,0:T(8,128)(2,1)S(1)}, bf16[4,128,128]{2,1,0:T(8,128)(2,1)S(1)}, u32[]{:S(2)}, u32[]{:S(2)}) %collective-permute-start.22) | collective-permute-done | bytes 131104 | tf_op jit(solution)/shard_map/ppermute | solution.py:310
  152.3 3.0 %collective-permute-start.23 = (bf16[4,128,128]{2,1,0:T(8,128)(2,1)S(1)}, bf16[4,128,128]{2,1,0:T(8,128)(2,1)S(1)}, u32[]{:S(2)}, u32[]{:S(2)}) collective-permute-start(bf16[4,128,128]{2,1,0:T(8,128)(2,1)S(1)} %get-tuple-element.64), channel_id=1, source_target_pairs={{0,8},{8,0},{1,9},{9,1},{2,10},{10,2},{3,11},{11,3},{4,12},{12,4},... | collective-permute-start | bytes 393224 | tf_op jit(solution)/shard_map/ppermute | solution.py:298
  161.5 4.0 %shard_map.103 = (bf16[2,192,512]{2,1,0:T(8,128)(2,1)}, f32[2,192,512]{2,1,0:T(8,128)S(1)}, f32[2,192,512]{2,1,0:T(8,128)S(1)}) custom-call(s32[4]{0:T(128)S(1)} %pad_add_fusion.place, bf16[2,192,512]{2,1,0:T(8,128)(2,1)S(1)} %copy-done.8, bf16[2,192,512]{2,1,0:T(8,128)(2,1)S(1)} %copy-done.4, bf16[2,192,512]{2,1,0:T(8,128)(2,1)S(1)} %copy-done.6, ...), custom_call_target="tpu_custom_call" | custom-call | flops 251658240 | bytes 3801104 | tf_op jit(solution)/shard_map/pallas_call | solution.py:34
  165.5 2.3 %shard_map.107 = (bf16[2,192,512]{2,1,0:T(8,128)(2,1)}, bf16[2,192,512]{2,1,0:T(8,128)(2,1)}) custom-call(s32[4]{0:T(128)S(1)} %pad_add_fusion.place, bf16[2,192,512]{2,1,0:T(8,128)(2,1)S(1)} %copy-done.4, bf16[2,192,512]{2,1,0:T(8,128)(2,1)S(1)} %copy-done.6, f32[2,192,512]{2,1,0:T(8,128)S(1)} %get-tuple-element.55.ik_ref, ...), custom_call_target="tpu_custom_call" | custom-call | flops 100663296 | bytes 3407888 | tf_op jit(solution)/shard_map/pallas_call | solution.py:34
  (83 shorter events, 46.2 us)
Async XLA Ops:
  7.2 161.4 %reduce-scatter.2.cloned.1.call-start = ((), (), s32[]{:S(2)}) async-start(), calls=%async_computation.1 | async-start | bytes 3538944 | tf_op jit(solution)/shard_map/reduce_scatter | solution.py:436
  15.7 6.8 %collective-permute-start.1 = (bf16[4,128,128]{2,1,0:T(8,128)(2,1)S(1)}, bf16[4,128,128]{2,1,0:T(8,128)(2,1)S(1)}, u32[]{:S(2)}, u32[]{:S(2)}) collective-permute-start(bf16[4,128,128]{2,1,0:T(8,128)(2,1)S(1)} %shard_map.94.t_ref), channel_id=1, source_target_pairs={{0,16},{8,72},{16,32},{24,88},{32,48},{40,104},{48,0},{56,120},{64... | collective-permute-start | bytes 393224 | tf_op jit(solution)/shard_map/ppermute | solution.py:310
  15.8 6.7 %collective-permute-start.2 = (bf16[4,128,128]{2,1,0:T(8,128)(2,1)S(1)}, bf16[4,128,128]{2,1,0:T(8,128)(2,1)S(1)}, u32[]{:S(2)}, u32[]{:S(2)}) collective-permute-start(bf16[4,128,128]{2,1,0:T(8,128)(2,1)S(1)} %shard_map.94.t_ref), channel_id=1, source_target_pairs={{0,32},{8,136},{16,48},{24,152},{32,0},{40,168},{48,16},{56,184},{... | collective-permute-start | bytes 393224 | tf_op jit(solution)/shard_map/ppermute | solution.py:310
  42.6 15.0 %collective-permute-start.8 = (bf16[384,512]{1,0:T(8,128)(2,1)S(1)}, bf16[384,512]{1,0:T(8,128)(2,1)S(1)}, u32[]{:S(2)}, u32[]{:S(2)}) collective-permute-start(bf16[384,512]{1,0:T(8,128)(2,1)S(1)} %bitcast.12), channel_id=1, source_target_pairs={{0,1},{1,2},{2,3},{3,4},{4,5},{5,6},{6,7},{7,0},{8,9},{9,10},{10,1... | collective-permute-start | bytes 1179656 | tf_op jit(solution)/shard_map/ppermute | solution.py:298
  44.2 14.2 %collective-permute-start.12 = (bf16[384,512]{1,0:T(8,128)(2,1)S(1)}, bf16[384,512]{1,0:T(8,128)(2,1)S(1)}, u32[]{:S(2)}, u32[]{:S(2)}) collective-permute-start(bf16[384,512]{1,0:T(8,128)(2,1)S(1)} %bitcast.13), channel_id=1, source_target_pairs={{0,7},{1,0},{2,1},{3,2},{4,3},{5,4},{6,5},{7,6},{8,15},{9,8},{10,9... | collective-permute-start | bytes 1179656 | tf_op jit(solution)/shard_map/ppermute | solution.py:298
  57.6 20.7 %collective-permute-start.9 = (bf16[384,512]{1,0:T(8,128)(2,1)S(1)}, bf16[384,512]{1,0:T(8,128)(2,1)S(1)}, u32[]{:S(2)}, u32[]{:S(2)}) collective-permute-start(bf16[384,512]{1,0:T(8,128)(2,1)S(1)} %collective-permute-done.8.refs_1_), channel_id=1, source_target_pairs={{0,1},{1,2},{2,3},{3,4},{4,5},{5,6},{6,7},{7,0},{8,9},{9,10},{10,1... | collective-permute-start | bytes 1179656 | tf_op jit(solution)/shard_map/ppermute | solution.py:298
  58.5 20.2 %collective-permute-start.13 = (bf16[384,512]{1,0:T(8,128)(2,1)S(1)}, bf16[384,512]{1,0:T(8,128)(2,1)S(1)}, u32[]{:S(2)}, u32[]{:S(2)}) collective-permute-start(bf16[384,512]{1,0:T(8,128)(2,1)S(1)} %collective-permute-done.12.refs_2_), channel_id=1, source_target_pairs={{0,7},{1,0},{2,1},{3,2},{4,3},{5,4},{6,5},{7,6},{8,15},{9,8},{10,9... | collective-permute-start | bytes 1179656 | tf_op jit(solution)/shard_map/ppermute | solution.py:298
  78.2 20.5 %collective-permute-start.10 = (bf16[384,512]{1,0:T(8,128)(2,1)S(1)}, bf16[384,512]{1,0:T(8,128)(2,1)S(1)}, u32[]{:S(2)}, u32[]{:S(2)}) collective-permute-start(bf16[384,512]{1,0:T(8,128)(2,1)S(1)} %collective-permute-done.9.refs_3_), channel_id=1, source_target_pairs={{0,1},{1,2},{2,3},{3,4},{4,5},{5,6},{6,7},{7,0},{8,9},{9,10},{10,1... | collective-permute-start | bytes 1179656 | tf_op jit(solution)/shard_map/ppermute | solution.py:298
  78.7 20.0 %collective-permute-start.14 = (bf16[384,512]{1,0:T(8,128)(2,1)S(1)}, bf16[384,512]{1,0:T(8,128)(2,1)S(1)}, u32[]{:S(2)}, u32[]{:S(2)}) collective-permute-start(bf16[384,512]{1,0:T(8,128)(2,1)S(1)} %collective-permute-done.13.refs_4_), channel_id=1, source_target_pairs={{0,7},{1,0},{2,1},{3,2},{4,3},{5,4},{6,5},{7,6},{8,15},{9,8},{10,9... | collective-permute-start | bytes 1179656 | tf_op jit(solution)/shard_map/ppermute | solution.py:298
  100.5 20.3 %collective-permute-start.24 = (bf16[4,4,512,128]{3,2,1,0:T(8,128)(2,1)S(1)}, bf16[4,4,512,128]{3,2,1,0:T(8,128)(2,1)S(1)}, u32[]{:S(2)}, u32[]{:S(2)}) collective-permute-start(bf16[4,4,512,128]{3,2,1,0:T(8,128)(2,1)S(1)} %shard_map.108), channel_id=1, source_target_pairs={{0,8},{8,0},{1,9},{9,1},{2,10},{10,2},{3,11},{11,3},{4,12},{12,4},... | collective-permute-start | bytes 6291464 | tf_op jit(solution)/shard_map/ppermute | solution.py:298
  104.0 8.7 %collective-permute-start.11 = (bf16[384,256]{1,0:T(8,128)(2,1)S(1)}, bf16[384,256]{1,0:T(8,128)(2,1)S(1)}, u32[]{:S(2)}, u32[]{:S(2)}) collective-permute-start(bf16[384,256]{1,0:T(8,128)(2,1)S(1)} %shard_map.99), channel_id=1, source_target_pairs={{0,1},{1,2},{2,3},{3,4},{4,5},{5,6},{6,7},{7,0},{8,9},{9,10},{10,1... | collective-permute-start | bytes 589832 | tf_op jit(solution)/shard_map/ppermute | solution.py:298
  104.1 8.6 %collective-permute-start.15 = (bf16[384,256]{1,0:T(8,128)(2,1)S(1)}, bf16[384,256]{1,0:T(8,128)(2,1)S(1)}, u32[]{:S(2)}, u32[]{:S(2)}) collective-permute-start(bf16[384,256]{1,0:T(8,128)(2,1)S(1)} %shard_map.100), channel_id=1, source_target_pairs={{0,7},{1,0},{2,1},{3,2},{4,3},{5,4},{6,5},{7,6},{8,15},{9,8},{10,9... | collective-permute-start | bytes 589832 | tf_op jit(solution)/shard_map/ppermute | solution.py:298
  113.6 7.2 %collective-permute-start.25 = (bf16[2,512,128]{2,1,0:T(8,128)(2,1)S(1)}, bf16[2,512,128]{2,1,0:T(8,128)(2,1)S(1)}, u32[]{:S(2)}, u32[]{:S(2)}) collective-permute-start(bf16[2,512,128]{2,1,0:T(8,128)(2,1)S(1)} %shard_map.109), channel_id=1, source_target_pairs={{0,8},{8,0},{1,9},{9,1},{2,10},{10,2},{3,11},{11,3},{4,12},{12,4},... | collective-permute-start | bytes 786440 | tf_op jit(solution)/shard_map/ppermute | solution.py:298
  120.0 8.1 %collective-permute-start.17 = (bf16[4,128,128]{2,1,0:T(8,128)(2,1)S(1)}, bf16[4,128,128]{2,1,0:T(8,128)(2,1)S(1)}, u32[]{:S(2)}, u32[]{:S(2)}) collective-permute-start(bf16[4,128,128]{2,1,0:T(8,128)(2,1)S(1)} %shard_map.104.t_ref), channel_id=1, source_target_pairs={{0,16},{8,72},{16,32},{24,88},{32,48},{40,104},{48,0},{56,120},{64... | collective-permute-start | bytes 393224 | tf_op jit(solution)/shard_map/ppermute | solution.py:310
  123.0 32.4 %collective-permute-start.26 = (bf16[4,512,128]{2,1,0:T(8,128)(2,1)S(1)}, bf16[4,512,128]{2,1,0:T(8,128)(2,1)S(1)}, u32[]{:S(2)}, u32[]{:S(2)}) collective-permute-start(bf16[4,512,128]{2,1,0:T(8,128)(2,1)S(1)} %get-tuple-element.68), channel_id=1, source_target_pairs={{0,16},{8,72},{16,32},{24,88},{32,48},{40,104},{48,0},{56,120},{64... | collective-permute-start | bytes 1572872 | tf_op jit(solution)/shard_map/ppermute | solution.py:310
  123.4 31.9 %collective-permute-start.27 = (bf16[4,512,128]{2,1,0:T(8,128)(2,1)S(1)}, bf16[4,512,128]{2,1,0:T(8,128)(2,1)S(1)}, u32[]{:S(2)}, u32[]{:S(2)}) collective-permute-start(bf16[4,512,128]{2,1,0:T(8,128)(2,1)S(1)} %get-tuple-element.69), channel_id=1, source_target_pairs={{0,32},{8,136},{16,48},{24,152},{32,0},{40,168},{48,16},{56,184},{... | collective-permute-start | bytes 1572872 | tf_op jit(solution)/shard_map/ppermute | solution.py:310
  126.2 29.1 %collective-permute-start.28 = (bf16[4,512,128]{2,1,0:T(8,128)(2,1)S(1)}, bf16[4,512,128]{2,1,0:T(8,128)(2,1)S(1)}, u32[]{:S(2)}, u32[]{:S(2)}) collective-permute-start(bf16[4,512,128]{2,1,0:T(8,128)(2,1)S(1)} %get-tuple-element.70), channel_id=1, source_target_pairs={{0,48},{8,200},{16,0},{24,216},{32,16},{40,232},{48,32},{56,248},{... | collective-permute-start | bytes 1572872 | tf_op jit(solution)/shard_map/ppermute | solution.py:310
  128.0 12.2 %collective-permute-start.18 = (bf16[4,128,128]{2,1,0:T(8,128)(2,1)S(1)}, bf16[4,128,128]{2,1,0:T(8,128)(2,1)S(1)}, u32[]{:S(2)}, u32[]{:S(2)}) collective-permute-start(bf16[4,128,128]{2,1,0:T(8,128)(2,1)S(1)} %shard_map.104.t_ref), channel_id=1, source_target_pairs={{0,32},{8,136},{16,48},{24,152},{32,0},{40,168},{48,16},{56,184},{... | collective-permute-start | bytes 393224 | tf_op jit(solution)/shard_map/ppermute | solution.py:310
  128.1 13.6 %collective-permute-start.19 = (bf16[4,128,128]{2,1,0:T(8,128)(2,1)S(1)}, bf16[4,128,128]{2,1,0:T(8,128)(2,1)S(1)}, u32[]{:S(2)}, u32[]{:S(2)}) collective-permute-start(bf16[4,128,128]{2,1,0:T(8,128)(2,1)S(1)} %shard_map.104.t_ref), channel_id=1, source_target_pairs={{0,48},{8,200},{16,0},{24,216},{32,16},{40,232},{48,32},{56,248},{... | collective-permute-start | bytes 393224 | tf_op jit(solution)/shard_map/ppermute | solution.py:310
  142.9 6.6 %collective-permute-start.21 = (bf16[4,128,128]{2,1,0:T(8,128)(2,1)S(1)}, bf16[4,128,128]{2,1,0:T(8,128)(2,1)S(1)}, u32[]{:S(2)}, u32[]{:S(2)}) collective-permute-start(bf16[4,128,128]{2,1,0:T(8,128)(2,1)S(1)} %get-tuple-element.61), channel_id=1, source_target_pairs={{0,128},{8,40},{16,144},{24,56},{32,160},{40,8},{48,176},{56,24},{... | collective-permute-start | bytes 393224 | tf_op jit(solution)/shard_map/ppermute | solution.py:310
  152.3 13.2 %collective-permute-start.23 = (bf16[4,128,128]{2,1,0:T(8,128)(2,1)S(1)}, bf16[4,128,128]{2,1,0:T(8,128)(2,1)S(1)}, u32[]{:S(2)}, u32[]{:S(2)}) collective-permute-start(bf16[4,128,128]{2,1,0:T(8,128)(2,1)S(1)} %get-tuple-element.64), channel_id=1, source_target_pairs={{0,8},{8,0},{1,9},{9,1},{2,10},{10,2},{3,11},{11,3},{4,12},{12,4},... | collective-permute-start | bytes 393224 | tf_op jit(solution)/shard_map/ppermute | solution.py:298
  156.2 11.6 %collective-permute-start.29 = (bf16[512,128]{1,0:T(8,128)(2,1)S(1)}, bf16[512,128]{1,0:T(8,128)(2,1)S(1)}, u32[]{:S(2)}, u32[]{:S(2)}) collective-permute-start(bf16[512,128]{1,0:T(8,128)(2,1)S(1)} %get-tuple-element.72), channel_id=1, source_target_pairs={{0,64},{8,24},{16,80},{24,40},{32,96},{40,56},{48,112},{56,8},{64,... | collective-permute-start | bytes 393224 | tf_op jit(solution)/shard_map/ppermute | solution.py:310
  157.9 9.9 %collective-permute-start.30 = (bf16[512,128]{1,0:T(8,128)(2,1)S(1)}, bf16[512,128]{1,0:T(8,128)(2,1)S(1)}, u32[]{:S(2)}, u32[]{:S(2)}) collective-permute-start(bf16[512,128]{1,0:T(8,128)(2,1)S(1)} %get-tuple-element.73), channel_id=1, source_target_pairs={{0,128},{8,40},{16,144},{24,56},{32,160},{40,8},{48,176},{56,24},{... | collective-permute-start | bytes 393224 | tf_op jit(solution)/shard_map/ppermute | solution.py:310
  159.7 8.0 %collective-permute-start.31 = (bf16[512,128]{1,0:T(8,128)(2,1)S(1)}, bf16[512,128]{1,0:T(8,128)(2,1)S(1)}, u32[]{:S(2)}, u32[]{:S(2)}) collective-permute-start(bf16[512,128]{1,0:T(8,128)(2,1)S(1)} %get-tuple-element.74), channel_id=1, source_target_pairs={{0,192},{8,56},{16,208},{24,8},{32,224},{40,24},{48,240},{56,40},{... | collective-permute-start | bytes 393224 | tf_op jit(solution)/shard_map/ppermute | solution.py:310
  (18 other events, 223.4 us)
Sparse Core Ops, SparseCore 0:
  41.8 63.4 reduce-scatter.1

commit v5 on v4

--- a/solution.py
+++ b/solution.py
@@ -23,7 +23,7 @@
     return lax.dot_general(a, b, (((ca,), (cb,)), ((), ())), preferred_element_type=F32)
 
 
-def call(body, outs, args, flops, scalar=False, scratch=(), last=VMEM):
+def call(body, outs, args, flops, scalar=False, scratch=(), last=VMEM, result=VMEM):
     size = sum(a.size * a.dtype.itemsize for a in args)
     size += sum(o.size * o.dtype.itemsize for o in outs)
     cost = pl.CostEstimate(flops=flops, bytes_accessed=size, transcendentals=0)
@@ -35,7 +35,7 @@
         body,
         out_shape=outs,
         in_specs=specs,
-        out_specs=[pl.BlockSpec(memory_space=VMEM)] * len(outs),
+        out_specs=[pl.BlockSpec(memory_space=result)] * len(outs),
         scratch_shapes=list(scratch),
         cost_estimate=cost,
         compiler_params=pltpu.CompilerParams(vmem_limit_bytes=LIMIT),
@@ -103,18 +103,6 @@
     return jnp.where(place[2] == b, own_ref[h], other_ref[h])
 
 
-def each_head(width, step):
-    n = width // DH
-
-    def body(i, carry):
-        for j in range(2):
-            b, h = i // (n // 2), 2 * (i % (n // 2)) + j
-            step(b, h, b * n + h, pl.ds(pl.multiple_of(h * DH, DH), DH))
-        return carry
-
-    lax.fori_loop(0, n, body, 0)
-
-
 def each_batch(width, step):
     def body(b, carry):
         for h in range(width // DH):
@@ -146,19 +134,25 @@
         mean = jnp.mean(attended * attended, axis=-1, keepdims=True)
         normed_ref[b, :, s] = (attended / jnp.sqrt(mean + EPS)).astype(BF16)
 
-    each_head(q_ref.shape[2], step)
-
-
-def project_body(n_ref, w_ref, out_ref):
-    width = n_ref.shape[1]
+    each_batch(q_ref.shape[2], step)
+
+
+def project_body(n_ref, w_ref, out_hbm, buf, sem):
+    chunks, _, width = buf.shape
+
+    def out(j):
+        return pltpu.make_async_copy(buf.at[j], out_hbm.at[j], sem.at[j])
 
     def body(i, carry):
         for j in (2 * i, 2 * i + 1):
             cols = pl.ds(pl.multiple_of(j * width, width), width)
-            out_ref[j] = dot(n_ref[...], w_ref[:, cols], 1, 0).astype(BF16)
+            buf[j] = dot(n_ref[...], w_ref[:, cols], 1, 0).astype(BF16)
+            out(j).start()
         return carry
 
-    lax.fori_loop(0, out_ref.shape[0] // 2, body, 0)
+    lax.fori_loop(0, chunks // 2, body, 0)
+    for j in range(chunks):
+        out(j).wait()
 
 
 def half_body(first, x_ref, out_ref):
@@ -212,7 +206,7 @@
         inner = jnp.mean(g * a, axis=-1, keepdims=True)
         ag_ref[b, :, s] = (g * root - a * (inner * root * root * root)).astype(BF16)
 
-    each_head(width, step)
+    each_batch(width, step)
     local_states(place, q_ref, ag_ref, keep_ref, send_ref)
 
 
@@ -290,7 +284,7 @@
         dk_ref[b, :, s] = (ik_ref[b, :, s] + SCALE * dot(v_ref[b, :, s], later, 1, 1)).astype(BF16)
         dv_ref[b, :, s] = (iv_ref[b, :, s] + SCALE * dot(k_ref[b, :, s], later, 1, 0)).astype(BF16)
 
-    each_head(k_ref.shape[2], step)
+    each_batch(k_ref.shape[2], step)
 
 
 def shift(value, axis, step):
@@ -432,7 +426,14 @@
     )
     normed = normed.reshape(rows, width)
     big = 2 * rows * width * width * n_head
-    partial = call(project_body, [shape((n_head, rows, width), BF16)], [normed, out_weight], big)[0]
+    partial = call(
+        project_body,
+        [shape((n_head, rows, width), BF16)],
+        [normed, out_weight],
+        big,
+        scratch=[VMEM((n_head, rows, width), BF16), pltpu.SemaphoreType.DMA((n_head,))],
+        result=pltpu.HBM,
+    )[0]
     layer_output = lax.psum_scatter(
         partial.reshape(n_head * rows, width), "head", scatter_dimension=0, tiled=True
     ).reshape(queries.shape)

time: 176 us -> 174 us (0.989)
  no operation moved by 1% of the time
where the time goes in v5:
time: 174 us
  waiting for transfers between devices  75.8 us (44%)
  starting transfers between devices  53.4 us (31%)
  Pallas kernels  26.1 us (15%)
  between operations  14.3 us (8%)
  local copies, waits for them, and re-layouts  3.98 us (2%)
    ppermute x14, waiting for transfers between devices, shift(): return lax.ppermute(value, axis, [(i, (i + step) % n) for i in range(n)])  50.9 us
    ppermute x14, starting transfers between devices, shift(): return lax.ppermute(value, axis, [(i, (i + step) % n) for i in range(n)])  29.5 us
    pallas_call x21, Pallas kernels, call(): pl.pallas_call(body, out_shape=outs, in_specs=specs, out_specs=[pl.BlockS...  26.1 us
    ppermute x18, waiting for transfers between devices, shift_by_core(): lax.ppermute(value, CTX, [(index(*p), index(*target(*p))) for p in places])  24.8 us
    ppermute x18, starting transfers between devices, shift_by_core(): lax.ppermute(value, CTX, [(index(*p), index(*target(*p))) for p in places])  23.9 us
    unnamed x18, local copies, waits for them, and re-layouts  3.98 us
  transfers between devices with their start and end apart: 33, of which 18 were waited for; matrix products, arithmetic and copies ran while one was open for 0% of the time, Pallas kernels for 11%

profile of v5, /device:TPU:1, one launch (start us, length us, event | category | flops | bytes accessed | tf_op | source)
XLA Modules:
  0.0 173.6 jit_solution(17706512222149329349)
XLA Ops:
  11.4 3.3 %collective-permute-start = (bf16[4,128,128]{2,1,0:T(8,128)(2,1)S(1)}, bf16[4,128,128]{2,1,0:T(8,128)(2,1)S(1)}, u32[]{:S(2)}, u32[]{:S(2)}) collective-permute-start(bf16[4,128,128]{2,1,0:T(8,128)(2,1)S(1)} %get-tuple-element.44), channel_id=1, source_target_pairs={{0,8},{8,0},{1,9},{9,1},{2,10},{10,2},{3,11},{11,3},{4,12},{12,4},... | collective-permute-start | bytes 393224 | tf_op jit(solution)/shard_map/ppermute | solution.py:292
  18.9 3.6 %collective-permute-done.1.g1 = bf16[4,128,128]{2,1,0:T(8,128)(2,1)S(1)} collective-permute-done((bf16[4,128,128]{2,1,0:T(8,128)(2,1)S(1)}, bf16[4,128,128]{2,1,0:T(8,128)(2,1)S(1)}, u32[]{:S(2)}, u32[]{:S(2)}) %collective-permute-start.1) | collective-permute-done | bytes 131104 | tf_op jit(solution)/shard_map/ppermute | solution.py:304
  24.0 2.6 %collective-permute-start.5 = (bf16[4,128,128]{2,1,0:T(8,128)(2,1)S(1)}, bf16[4,128,128]{2,1,0:T(8,128)(2,1)S(1)}, u32[]{:S(2)}, u32[]{:S(2)}) collective-permute-start(bf16[4,128,128]{2,1,0:T(8,128)(2,1)S(1)} %get-tuple-element.47), channel_id=1, source_target_pairs={{0,128},{8,40},{16,144},{24,56},{32,160},{40,8},{48,176},{56,24},{... | collective-permute-start | bytes 393224 | tf_op jit(solution)/shard_map/ppermute | solution.py:304
  31.8 2.8 %collective-permute-start.7 = (bf16[4,128,128]{2,1,0:T(8,128)(2,1)S(1)}, bf16[4,128,128]{2,1,0:T(8,128)(2,1)S(1)}, u32[]{:S(2)}, u32[]{:S(2)}) collective-permute-start(bf16[4,128,128]{2,1,0:T(8,128)(2,1)S(1)} %get-tuple-element.50), channel_id=1, source_target_pairs={{0,8},{8,0},{1,9},{9,1},{2,10},{10,2},{3,11},{11,3},{4,12},{12,4},... | collective-permute-start | bytes 393224 | tf_op jit(solution)/shard_map/ppermute | solution.py:292
  37.2 3.1 %shard_map.98 = bf16[8,384,512]{2,1,0:T(8,128)(2,1)} custom-call(bf16[384,512]{1,0:T(8,128)(2,1)S(1)} %bitcast.8, bf16[512,4096]{1,0:T(8,128)(2,1)S(1)} %copy-done), custom_call_target="tpu_custom_call" | custom-call | flops 1610612736 | bytes 7733248 | tf_op jit(solution)/shard_map/pallas_call | solution.py:34
  43.0 3.9 %collective-permute-start.12 = (bf16[384,512]{1,0:T(8,128)(2,1)S(1)}, bf16[384,512]{1,0:T(8,128)(2,1)S(1)}, u32[]{:S(2)}, u32[]{:S(2)}) collective-permute-start(bf16[384,512]{1,0:T(8,128)(2,1)S(1)} %bitcast.13), channel_id=1, source_target_pairs={{0,7},{1,0},{2,1},{3,2},{4,3},{5,4},{6,5},{7,6},{8,15},{9,8},{10,9... | collective-permute-start | bytes 1179656 | tf_op jit(solution)/shard_map/ppermute | solution.py:292
  46.9 9.4 %collective-permute-done.8.refs_1_ = bf16[384,512]{1,0:T(8,128)(2,1)S(1)} collective-permute-done((bf16[384,512]{1,0:T(8,128)(2,1)S(1)}, bf16[384,512]{1,0:T(8,128)(2,1)S(1)}, u32[]{:S(2)}, u32[]{:S(2)}) %collective-permute-start.8) | collective-permute-done | bytes 393248 | tf_op jit(solution)/shard_map/ppermute | solution.py:292
  57.2 3.5 %collective-permute-start.13 = (bf16[384,512]{1,0:T(8,128)(2,1)S(1)}, bf16[384,512]{1,0:T(8,128)(2,1)S(1)}, u32[]{:S(2)}, u32[]{:S(2)}) collective-permute-start(bf16[384,512]{1,0:T(8,128)(2,1)S(1)} %collective-permute-done.12.refs_2_), channel_id=1, source_target_pairs={{0,7},{1,0},{2,1},{3,2},{4,3},{5,4},{6,5},{7,6},{8,15},{9,8},{10,9... | collective-permute-start | bytes 1179656 | tf_op jit(solution)/shard_map/ppermute | solution.py:292
  60.7 16.3 %collective-permute-done.9.refs_3_ = bf16[384,512]{1,0:T(8,128)(2,1)S(1)} collective-permute-done((bf16[384,512]{1,0:T(8,128)(2,1)S(1)}, bf16[384,512]{1,0:T(8,128)(2,1)S(1)}, u32[]{:S(2)}, u32[]{:S(2)}) %collective-permute-start.9) | collective-permute-done | bytes 393248 | tf_op jit(solution)/shard_map/ppermute | solution.py:292
  77.4 3.5 %collective-permute-start.14 = (bf16[384,512]{1,0:T(8,128)(2,1)S(1)}, bf16[384,512]{1,0:T(8,128)(2,1)S(1)}, u32[]{:S(2)}, u32[]{:S(2)}) collective-permute-start(bf16[384,512]{1,0:T(8,128)(2,1)S(1)} %collective-permute-done.13.refs_4_), channel_id=1, source_target_pairs={{0,7},{1,0},{2,1},{3,2},{4,3},{5,4},{6,5},{7,6},{8,15},{9,8},{10,9... | collective-permute-start | bytes 1179656 | tf_op jit(solution)/shard_map/ppermute | solution.py:292
  80.9 16.5 %collective-permute-done.10.x_ref.refs_5_ = bf16[384,512]{1,0:T(8,128)(2,1)S(1)} collective-permute-done((bf16[384,512]{1,0:T(8,128)(2,1)S(1)}, bf16[384,512]{1,0:T(8,128)(2,1)S(1)}, u32[]{:S(2)}, u32[]{:S(2)}) %collective-permute-start.10) | collective-permute-done | bytes 393248 | tf_op jit(solution)/shard_map/ppermute | solution.py:292
  99.3 3.4 %collective-permute-start.24 = (bf16[4,4,512,128]{3,2,1,0:T(8,128)(2,1)S(1)}, bf16[4,4,512,128]{3,2,1,0:T(8,128)(2,1)S(1)}, u32[]{:S(2)}, u32[]{:S(2)}) collective-permute-start(bf16[4,4,512,128]{3,2,1,0:T(8,128)(2,1)S(1)} %shard_map.108), channel_id=1, source_target_pairs={{0,8},{8,0},{1,9},{9,1},{2,10},{10,2},{3,11},{11,3},{4,12},{12,4},... | collective-permute-start | bytes 6291464 | tf_op jit(solution)/shard_map/ppermute | solution.py:292
  102.8 3.5 %collective-permute-start.15 = (bf16[384,256]{1,0:T(8,128)(2,1)S(1)}, bf16[384,256]{1,0:T(8,128)(2,1)S(1)}, u32[]{:S(2)}, u32[]{:S(2)}) collective-permute-start(bf16[384,256]{1,0:T(8,128)(2,1)S(1)} %shard_map.100), channel_id=1, source_target_pairs={{0,7},{1,0},{2,1},{3,2},{4,3},{5,4},{6,5},{7,6},{8,15},{9,8},{10,9... | collective-permute-start | bytes 589832 | tf_op jit(solution)/shard_map/ppermute | solution.py:292
  106.3 5.1 %collective-permute-done.11.refs_0_.r4.refs_7_ = bf16[384,256]{1,0:T(8,128)(2,1)S(1)} collective-permute-done((bf16[384,256]{1,0:T(8,128)(2,1)S(1)}, bf16[384,256]{1,0:T(8,128)(2,1)S(1)}, u32[]{:S(2)}, u32[]{:S(2)}) %collective-permute-start.11) | collective-permute-done | bytes 196640 | tf_op jit(solution)/shard_map/ppermute | solution.py:292
  113.0 2.2 %shard_map.101.refs_3_ = f32[384,512]{1,0:T(8,128)S(1)} custom-call(s32[4]{0:T(128)S(1)} %pad_add_fusion.place, bf16[384,512]{1,0:T(8,128)(2,1)S(1)} %bitcast.15, bf16[384,512]{1,0:T(8,128)(2,1)S(1)} %collective-permute-done.8.refs_1_, bf16[384,512]{1,0:T(8,128)(2,1)S(1)} %collective-permute-done.12.refs_2_, ...), custom_call_target="tpu_custom_call" | custom-call | flops 1409286144 | bytes 7733264 | tf_op jit(solution)/shard_map/pallas_call | solution.py:34
  119.4 2.2 %shard_map.110 = (bf16[4,512,128]{2,1,0:T(8,128)(2,1)S(1)}, bf16[4,512,128]{2,1,0:T(8,128)(2,1)S(1)}, bf16[4,512,128]{2,1,0:T(8,128)(2,1)S(1)}, bf16[4,512,128]{2,1,0:T(8,128)(2,1)S(1)}) custom-call(s32[4]{0:T(128)S(1)} %pad_add_fusion.place, bf16[384,512]{1,0:T(8,128)(2,1)S(1)} %bitcast.11, bf16[384,512]{1,0:T(8,128)(2,1)S(1)} %bitcast.16, ...), custom_call_target="tpu_custom_call" | custom-call | flops 805306368 | bytes 7995408 | tf_op jit(solution)/shard_map/pallas_call | solution.py:34
  122.0 2.8 %collective-permute-start.27 = (bf16[4,512,128]{2,1,0:T(8,128)(2,1)S(1)}, bf16[4,512,128]{2,1,0:T(8,128)(2,1)S(1)}, u32[]{:S(2)}, u32[]{:S(2)}) collective-permute-start(bf16[4,512,128]{2,1,0:T(8,128)(2,1)S(1)} %get-tuple-element.69), channel_id=1, source_target_pairs={{0,32},{8,136},{16,48},{24,152},{32,0},{40,168},{48,16},{56,184},{... | collective-permute-start | bytes 1572872 | tf_op jit(solution)/shard_map/ppermute | solution.py:304
  128.7 10.0 %collective-permute-done.18.g2 = bf16[4,128,128]{2,1,0:T(8,128)(2,1)S(1)} collective-permute-done((bf16[4,128,128]{2,1,0:T(8,128)(2,1)S(1)}, bf16[4,128,128]{2,1,0:T(8,128)(2,1)S(1)}, u32[]{:S(2)}, u32[]{:S(2)}) %collective-permute-start.18) | collective-permute-done | bytes 131104 | tf_op jit(solution)/shard_map/ppermute | solution.py:304
  141.5 2.9 %collective-permute-start.21 = (bf16[4,128,128]{2,1,0:T(8,128)(2,1)S(1)}, bf16[4,128,128]{2,1,0:T(8,128)(2,1)S(1)}, u32[]{:S(2)}, u32[]{:S(2)}) collective-permute-start(bf16[4,128,128]{2,1,0:T(8,128)(2,1)S(1)} %get-tuple-element.61), channel_id=1, source_target_pairs={{0,128},{8,40},{16,144},{24,56},{32,160},{40,8},{48,176},{56,24},{... | collective-permute-start | bytes 393224 | tf_op jit(solution)/shard_map/ppermute | solution.py:304
  144.3 2.1 %collective-permute-done.20.g1 = bf16[4,128,128]{2,1,0:T(8,128)(2,1)S(1)} collective-permute-done((bf16[4,128,128]{2,1,0:T(8,128)(2,1)S(1)}, bf16[4,128,128]{2,1,0:T(8,128)(2,1)S(1)}, u32[]{:S(2)}, u32[]{:S(2)}) %collective-permute-start.20) | collective-permute-done | bytes 131104 | tf_op jit(solution)/shard_map/ppermute | solution.py:304
  148.1 2.2 %collective-permute-done.22.g3 = bf16[4,128,128]{2,1,0:T(8,128)(2,1)S(1)} collective-permute-done((bf16[4,128,128]{2,1,0:T(8,128)(2,1)S(1)}, bf16[4,128,128]{2,1,0:T(8,128)(2,1)S(1)}, u32[]{:S(2)}, u32[]{:S(2)}) %collective-permute-start.22) | collective-permute-done | bytes 131104 | tf_op jit(solution)/shard_map/ppermute | solution.py:304
  150.9 3.0 %collective-permute-start.23 = (bf16[4,128,128]{2,1,0:T(8,128)(2,1)S(1)}, bf16[4,128,128]{2,1,0:T(8,128)(2,1)S(1)}, u32[]{:S(2)}, u32[]{:S(2)}) collective-permute-start(bf16[4,128,128]{2,1,0:T(8,128)(2,1)S(1)} %get-tuple-element.64), channel_id=1, source_target_pairs={{0,8},{8,0},{1,9},{9,1},{2,10},{10,2},{3,11},{11,3},{4,12},{12,4},... | collective-permute-start | bytes 393224 | tf_op jit(solution)/shard_map/ppermute | solution.py:292
  160.0 4.0 %shard_map.103 = (bf16[2,192,512]{2,1,0:T(8,128)(2,1)}, f32[2,192,512]{2,1,0:T(8,128)S(1)}, f32[2,192,512]{2,1,0:T(8,128)S(1)}) custom-call(s32[4]{0:T(128)S(1)} %pad_add_fusion.place, bf16[2,192,512]{2,1,0:T(8,128)(2,1)S(1)} %copy-done.8, bf16[2,192,512]{2,1,0:T(8,128)(2,1)S(1)} %copy-done.4, bf16[2,192,512]{2,1,0:T(8,128)(2,1)S(1)} %copy-done.6, ...), custom_call_target="tpu_custom_call" | custom-call | flops 251658240 | bytes 3801104 | tf_op jit(solution)/shard_map/pallas_call | solution.py:34
  164.0 2.0 %shard_map.107 = (bf16[2,192,512]{2,1,0:T(8,128)(2,1)}, bf16[2,192,512]{2,1,0:T(8,128)(2,1)}) custom-call(s32[4]{0:T(128)S(1)} %pad_add_fusion.place, bf16[2,192,512]{2,1,0:T(8,128)(2,1)S(1)} %copy-done.4, bf16[2,192,512]{2,1,0:T(8,128)(2,1)S(1)} %copy-done.6, f32[2,192,512]{2,1,0:T(8,128)S(1)} %get-tuple-element.55.ik_ref, ...), custom_call_target="tpu_custom_call" | custom-call | flops 100663296 | bytes 3407888 | tf_op jit(solution)/shard_map/pallas_call | solution.py:34
  (83 shorter events, 45.4 us)
Async XLA Ops:
  7.2 159.5 %reduce-scatter.2.cloned.1.call-start = ((), (), s32[]{:S(2)}) async-start(), calls=%async_computation.1 | async-start | bytes 3538944 | tf_op jit(solution)/shard_map/reduce_scatter | solution.py:437
  15.7 6.8 %collective-permute-start.1 = (bf16[4,128,128]{2,1,0:T(8,128)(2,1)S(1)}, bf16[4,128,128]{2,1,0:T(8,128)(2,1)S(1)}, u32[]{:S(2)}, u32[]{:S(2)}) collective-permute-start(bf16[4,128,128]{2,1,0:T(8,128)(2,1)S(1)} %shard_map.94.t_ref), channel_id=1, source_target_pairs={{0,16},{8,72},{16,32},{24,88},{32,48},{40,104},{48,0},{56,120},{64... | collective-permute-start | bytes 393224 | tf_op jit(solution)/shard_map/ppermute | solution.py:304
  15.8 6.7 %collective-permute-start.2 = (bf16[4,128,128]{2,1,0:T(8,128)(2,1)S(1)}, bf16[4,128,128]{2,1,0:T(8,128)(2,1)S(1)}, u32[]{:S(2)}, u32[]{:S(2)}) collective-permute-start(bf16[4,128,128]{2,1,0:T(8,128)(2,1)S(1)} %shard_map.94.t_ref), channel_id=1, source_target_pairs={{0,32},{8,136},{16,48},{24,152},{32,0},{40,168},{48,16},{56,184},{... | collective-permute-start | bytes 393224 | tf_op jit(solution)/shard_map/ppermute | solution.py:304
  41.4 15.0 %collective-permute-start.8 = (bf16[384,512]{1,0:T(8,128)(2,1)S(1)}, bf16[384,512]{1,0:T(8,128)(2,1)S(1)}, u32[]{:S(2)}, u32[]{:S(2)}) collective-permute-start(bf16[384,512]{1,0:T(8,128)(2,1)S(1)} %bitcast.12), channel_id=1, source_target_pairs={{0,1},{1,2},{2,3},{3,4},{4,5},{5,6},{6,7},{7,0},{8,9},{9,10},{10,1... | collective-permute-start | bytes 1179656 | tf_op jit(solution)/shard_map/ppermute | solution.py:292
  43.0 14.2 %collective-permute-start.12 = (bf16[384,512]{1,0:T(8,128)(2,1)S(1)}, bf16[384,512]{1,0:T(8,128)(2,1)S(1)}, u32[]{:S(2)}, u32[]{:S(2)}) collective-permute-start(bf16[384,512]{1,0:T(8,128)(2,1)S(1)} %bitcast.13), channel_id=1, source_target_pairs={{0,7},{1,0},{2,1},{3,2},{4,3},{5,4},{6,5},{7,6},{8,15},{9,8},{10,9... | collective-permute-start | bytes 1179656 | tf_op jit(solution)/shard_map/ppermute | solution.py:292
  56.3 20.7 %collective-permute-start.9 = (bf16[384,512]{1,0:T(8,128)(2,1)S(1)}, bf16[384,512]{1,0:T(8,128)(2,1)S(1)}, u32[]{:S(2)}, u32[]{:S(2)}) collective-permute-start(bf16[384,512]{1,0:T(8,128)(2,1)S(1)} %collective-permute-done.8.refs_1_), channel_id=1, source_target_pairs={{0,1},{1,2},{2,3},{3,4},{4,5},{5,6},{6,7},{7,0},{8,9},{9,10},{10,1... | collective-permute-start | bytes 1179656 | tf_op jit(solution)/shard_map/ppermute | solution.py:292
  57.2 20.2 %collective-permute-start.13 = (bf16[384,512]{1,0:T(8,128)(2,1)S(1)}, bf16[384,512]{1,0:T(8,128)(2,1)S(1)}, u32[]{:S(2)}, u32[]{:S(2)}) collective-permute-start(bf16[384,512]{1,0:T(8,128)(2,1)S(1)} %collective-permute-done.12.refs_2_), channel_id=1, source_target_pairs={{0,7},{1,0},{2,1},{3,2},{4,3},{5,4},{6,5},{7,6},{8,15},{9,8},{10,9... | collective-permute-start | bytes 1179656 | tf_op jit(solution)/shard_map/ppermute | solution.py:292
  77.0 20.5 %collective-permute-start.10 = (bf16[384,512]{1,0:T(8,128)(2,1)S(1)}, bf16[384,512]{1,0:T(8,128)(2,1)S(1)}, u32[]{:S(2)}, u32[]{:S(2)}) collective-permute-start(bf16[384,512]{1,0:T(8,128)(2,1)S(1)} %collective-permute-done.9.refs_3_), channel_id=1, source_target_pairs={{0,1},{1,2},{2,3},{3,4},{4,5},{5,6},{6,7},{7,0},{8,9},{9,10},{10,1... | collective-permute-start | bytes 1179656 | tf_op jit(solution)/shard_map/ppermute | solution.py:292
  77.4 20.0 %collective-permute-start.14 = (bf16[384,512]{1,0:T(8,128)(2,1)S(1)}, bf16[384,512]{1,0:T(8,128)(2,1)S(1)}, u32[]{:S(2)}, u32[]{:S(2)}) collective-permute-start(bf16[384,512]{1,0:T(8,128)(2,1)S(1)} %collective-permute-done.13.refs_4_), channel_id=1, source_target_pairs={{0,7},{1,0},{2,1},{3,2},{4,3},{5,4},{6,5},{7,6},{8,15},{9,8},{10,9... | collective-permute-start | bytes 1179656 | tf_op jit(solution)/shard_map/ppermute | solution.py:292
  99.3 20.1 %collective-permute-start.24 = (bf16[4,4,512,128]{3,2,1,0:T(8,128)(2,1)S(1)}, bf16[4,4,512,128]{3,2,1,0:T(8,128)(2,1)S(1)}, u32[]{:S(2)}, u32[]{:S(2)}) collective-permute-start(bf16[4,4,512,128]{3,2,1,0:T(8,128)(2,1)S(1)} %shard_map.108), channel_id=1, source_target_pairs={{0,8},{8,0},{1,9},{9,1},{2,10},{10,2},{3,11},{11,3},{4,12},{12,4},... | collective-permute-start | bytes 6291464 | tf_op jit(solution)/shard_map/ppermute | solution.py:292
  102.7 8.7 %collective-permute-start.11 = (bf16[384,256]{1,0:T(8,128)(2,1)S(1)}, bf16[384,256]{1,0:T(8,128)(2,1)S(1)}, u32[]{:S(2)}, u32[]{:S(2)}) collective-permute-start(bf16[384,256]{1,0:T(8,128)(2,1)S(1)} %shard_map.99), channel_id=1, source_target_pairs={{0,1},{1,2},{2,3},{3,4},{4,5},{5,6},{6,7},{7,0},{8,9},{9,10},{10,1... | collective-permute-start | bytes 589832 | tf_op jit(solution)/shard_map/ppermute | solution.py:292
  102.8 8.6 %collective-permute-start.15 = (bf16[384,256]{1,0:T(8,128)(2,1)S(1)}, bf16[384,256]{1,0:T(8,128)(2,1)S(1)}, u32[]{:S(2)}, u32[]{:S(2)}) collective-permute-start(bf16[384,256]{1,0:T(8,128)(2,1)S(1)} %shard_map.100), channel_id=1, source_target_pairs={{0,7},{1,0},{2,1},{3,2},{4,3},{5,4},{6,5},{7,6},{8,15},{9,8},{10,9... | collective-permute-start | bytes 589832 | tf_op jit(solution)/shard_map/ppermute | solution.py:292
  112.3 7.1 %collective-permute-start.25 = (bf16[2,512,128]{2,1,0:T(8,128)(2,1)S(1)}, bf16[2,512,128]{2,1,0:T(8,128)(2,1)S(1)}, u32[]{:S(2)}, u32[]{:S(2)}) collective-permute-start(bf16[2,512,128]{2,1,0:T(8,128)(2,1)S(1)} %shard_map.109), channel_id=1, source_target_pairs={{0,8},{8,0},{1,9},{9,1},{2,10},{10,2},{3,11},{11,3},{4,12},{12,4},... | collective-permute-start | bytes 786440 | tf_op jit(solution)/shard_map/ppermute | solution.py:292
  118.6 8.1 %collective-permute-start.17 = (bf16[4,128,128]{2,1,0:T(8,128)(2,1)S(1)}, bf16[4,128,128]{2,1,0:T(8,128)(2,1)S(1)}, u32[]{:S(2)}, u32[]{:S(2)}) collective-permute-start(bf16[4,128,128]{2,1,0:T(8,128)(2,1)S(1)} %shard_map.104.t_ref), channel_id=1, source_target_pairs={{0,16},{8,72},{16,32},{24,88},{32,48},{40,104},{48,0},{56,120},{64... | collective-permute-start | bytes 393224 | tf_op jit(solution)/shard_map/ppermute | solution.py:304
  121.6 32.3 %collective-permute-start.26 = (bf16[4,512,128]{2,1,0:T(8,128)(2,1)S(1)}, bf16[4,512,128]{2,1,0:T(8,128)(2,1)S(1)}, u32[]{:S(2)}, u32[]{:S(2)}) collective-permute-start(bf16[4,512,128]{2,1,0:T(8,128)(2,1)S(1)} %get-tuple-element.68), channel_id=1, source_target_pairs={{0,16},{8,72},{16,32},{24,88},{32,48},{40,104},{48,0},{56,120},{64... | collective-permute-start | bytes 1572872 | tf_op jit(solution)/shard_map/ppermute | solution.py:304
  122.0 31.9 %collective-permute-start.27 = (bf16[4,512,128]{2,1,0:T(8,128)(2,1)S(1)}, bf16[4,512,128]{2,1,0:T(8,128)(2,1)S(1)}, u32[]{:S(2)}, u32[]{:S(2)}) collective-permute-start(bf16[4,512,128]{2,1,0:T(8,128)(2,1)S(1)} %get-tuple-element.69), channel_id=1, source_target_pairs={{0,32},{8,136},{16,48},{24,152},{32,0},{40,168},{48,16},{56,184},{... | collective-permute-start | bytes 1572872 | tf_op jit(solution)/shard_map/ppermute | solution.py:304
  124.8 29.1 %collective-permute-start.28 = (bf16[4,512,128]{2,1,0:T(8,128)(2,1)S(1)}, bf16[4,512,128]{2,1,0:T(8,128)(2,1)S(1)}, u32[]{:S(2)}, u32[]{:S(2)}) collective-permute-start(bf16[4,512,128]{2,1,0:T(8,128)(2,1)S(1)} %get-tuple-element.70), channel_id=1, source_target_pairs={{0,48},{8,200},{16,0},{24,216},{32,16},{40,232},{48,32},{56,248},{... | collective-permute-start | bytes 1572872 | tf_op jit(solution)/shard_map/ppermute | solution.py:304
  126.5 12.2 %collective-permute-start.18 = (bf16[4,128,128]{2,1,0:T(8,128)(2,1)S(1)}, bf16[4,128,128]{2,1,0:T(8,128)(2,1)S(1)}, u32[]{:S(2)}, u32[]{:S(2)}) collective-permute-start(bf16[4,128,128]{2,1,0:T(8,128)(2,1)S(1)} %shard_map.104.t_ref), channel_id=1, source_target_pairs={{0,32},{8,136},{16,48},{24,152},{32,0},{40,168},{48,16},{56,184},{... | collective-permute-start | bytes 393224 | tf_op jit(solution)/shard_map/ppermute | solution.py:304
  126.7 13.6 %collective-permute-start.19 = (bf16[4,128,128]{2,1,0:T(8,128)(2,1)S(1)}, bf16[4,128,128]{2,1,0:T(8,128)(2,1)S(1)}, u32[]{:S(2)}, u32[]{:S(2)}) collective-permute-start(bf16[4,128,128]{2,1,0:T(8,128)(2,1)S(1)} %shard_map.104.t_ref), channel_id=1, source_target_pairs={{0,48},{8,200},{16,0},{24,216},{32,16},{40,232},{48,32},{56,248},{... | collective-permute-start | bytes 393224 | tf_op jit(solution)/shard_map/ppermute | solution.py:304
  141.5 6.6 %collective-permute-start.21 = (bf16[4,128,128]{2,1,0:T(8,128)(2,1)S(1)}, bf16[4,128,128]{2,1,0:T(8,128)(2,1)S(1)}, u32[]{:S(2)}, u32[]{:S(2)}) collective-permute-start(bf16[4,128,128]{2,1,0:T(8,128)(2,1)S(1)} %get-tuple-element.61), channel_id=1, source_target_pairs={{0,128},{8,40},{16,144},{24,56},{32,160},{40,8},{48,176},{56,24},{... | collective-permute-start | bytes 393224 | tf_op jit(solution)/shard_map/ppermute | solution.py:304
  150.9 13.0 %collective-permute-start.23 = (bf16[4,128,128]{2,1,0:T(8,128)(2,1)S(1)}, bf16[4,128,128]{2,1,0:T(8,128)(2,1)S(1)}, u32[]{:S(2)}, u32[]{:S(2)}) collective-permute-start(bf16[4,128,128]{2,1,0:T(8,128)(2,1)S(1)} %get-tuple-element.64), channel_id=1, source_target_pairs={{0,8},{8,0},{1,9},{9,1},{2,10},{10,2},{3,11},{11,3},{4,12},{12,4},... | collective-permute-start | bytes 393224 | tf_op jit(solution)/shard_map/ppermute | solution.py:292
  154.7 11.2 %collective-permute-start.29 = (bf16[512,128]{1,0:T(8,128)(2,1)S(1)}, bf16[512,128]{1,0:T(8,128)(2,1)S(1)}, u32[]{:S(2)}, u32[]{:S(2)}) collective-permute-start(bf16[512,128]{1,0:T(8,128)(2,1)S(1)} %get-tuple-element.72), channel_id=1, source_target_pairs={{0,64},{8,24},{16,80},{24,40},{32,96},{40,56},{48,112},{56,8},{64,... | collective-permute-start | bytes 393224 | tf_op jit(solution)/shard_map/ppermute | solution.py:304
  156.5 9.4 %collective-permute-start.30 = (bf16[512,128]{1,0:T(8,128)(2,1)S(1)}, bf16[512,128]{1,0:T(8,128)(2,1)S(1)}, u32[]{:S(2)}, u32[]{:S(2)}) collective-permute-start(bf16[512,128]{1,0:T(8,128)(2,1)S(1)} %get-tuple-element.73), channel_id=1, source_target_pairs={{0,128},{8,40},{16,144},{24,56},{32,160},{40,8},{48,176},{56,24},{... | collective-permute-start | bytes 393224 | tf_op jit(solution)/shard_map/ppermute | solution.py:304
  158.3 7.6 %collective-permute-start.31 = (bf16[512,128]{1,0:T(8,128)(2,1)S(1)}, bf16[512,128]{1,0:T(8,128)(2,1)S(1)}, u32[]{:S(2)}, u32[]{:S(2)}) collective-permute-start(bf16[512,128]{1,0:T(8,128)(2,1)S(1)} %get-tuple-element.74), channel_id=1, source_target_pairs={{0,192},{8,56},{16,208},{24,8},{32,224},{40,24},{48,240},{56,40},{... | collective-permute-start | bytes 393224 | tf_op jit(solution)/shard_map/ppermute | solution.py:304
  (18 other events, 222.7 us)
Sparse Core Ops, SparseCore 0:
  40.5 63.4 reduce-scatter.1

commit v6 on v4

--- a/solution.py
+++ b/solution.py
@@ -52,10 +52,14 @@
 
 def local_states(place, left, right, keep_ref, send_ref):
     mc = place[2]
-    for h in range(keep_ref.shape[0]):
-        s = slice(h * DH, (h + 1) * DH)
+
+    def body(h, carry):
+        s = pl.ds(pl.multiple_of(h * DH, DH), DH)
         keep_ref[h] = dot(left[mc, :, s], right[mc, :, s], 0, 0)
         send_ref[h] = dot(left[1 - mc, :, s], right[1 - mc, :, s], 0, 0).astype(BF16)
+        return carry
+
+    lax.fori_loop(0, keep_ref.shape[0], body, 0)
 
 
 def state_body(place, k_ref, v_ref, q_hbm, keep_ref, send_ref, k_out, v_out, q_out, sem):
@@ -75,19 +79,24 @@
     rows_first = place[2] == 0
     first = jnp.where(rows_first, place[1], place[0])
     second = jnp.where(rows_first, place[0], place[1])
-    chip = t_ref[...].astype(F32)
-    every, some = chip, jnp.zeros_like(chip)
-    for d, g in ((1, g1), (2, g2), (3, g3)):
-        value = g[...].astype(F32)
-        every = every + value
-        taken = first < d if reverse else first >= d
-        some = some + jnp.where(taken, value, 0.0)
-    own_ref[...] = some
-    base = jnp.where(rows_first, 0.0, some)
-    extra = jnp.where(rows_first, every, chip)
-    for d, m in ((1, m1), (2, m2), (3, m3)):
-        given = second + d >= 4 if reverse else second + d < 4
-        m[...] = (base + jnp.where(given, extra, 0.0)).astype(BF16)
+
+    def body(h, carry):
+        chip = t_ref[h].astype(F32)
+        every, some = chip, jnp.zeros_like(chip)
+        for d, g in ((1, g1), (2, g2), (3, g3)):
+            value = g[h].astype(F32)
+            every = every + value
+            taken = first < d if reverse else first >= d
+            some = some + jnp.where(taken, value, 0.0)
+        own_ref[h] = some
+        base = jnp.where(rows_first, 0.0, some)
+        extra = jnp.where(rows_first, every, chip)
+        for d, m in ((1, m1), (2, m2), (3, m3)):
+            given = second + d >= 4 if reverse else second + d < 4
+            m[h] = (base + jnp.where(given, extra, 0.0)).astype(BF16)
+        return carry
+
+    lax.fori_loop(0, t_ref.shape[0], body, 0)
 
 
 def second_axis_body(reverse, place, own_ref, g1, g2, g3, keep_ref, got_ref, out_ref, send_ref):
@@ -103,25 +112,16 @@
     return jnp.where(place[2] == b, own_ref[h], other_ref[h])
 
 
-def each_head(width, step):
+def each_head(width, step, group=2):
     n = width // DH
 
     def body(i, carry):
-        for j in range(2):
-            b, h = i // (n // 2), 2 * (i % (n // 2)) + j
+        for j in range(group):
+            b, h = i // (n // group), group * (i % (n // group)) + j
             step(b, h, b * n + h, pl.ds(pl.multiple_of(h * DH, DH), DH))
         return carry
 
-    lax.fori_loop(0, n, body, 0)
-
-
-def each_batch(width, step):
-    def body(b, carry):
-        for h in range(width // DH):
-            step(b, h, b * (width // DH) + h, slice(h * DH, (h + 1) * DH))
-        return carry
-
-    lax.fori_loop(0, 2, body, 0)
+    lax.fori_loop(0, 2 * n // group, body, 0)
 
 
 def masked_scores(lower, left, right):
@@ -135,7 +135,7 @@
         scores = masked_scores(lower, q_ref[b, :, s], k_ref[b, :, s])
         intra_ref[b, :, s] = dot(scores, v_ref[b, :, s], 1, 0)
 
-    each_batch(q_ref.shape[2], step)
+    each_head(q_ref.shape[2], step)
 
 
 def forward_body(place, q_ref, intra_ref, so_ref, sr_ref, normed_ref, attended_ref):
@@ -149,30 +149,25 @@
     each_head(q_ref.shape[2], step)
 
 
-def project_body(n_ref, w_ref, out_ref):
-    width = n_ref.shape[1]
-
-    def body(i, carry):
-        for j in (2 * i, 2 * i + 1):
-            cols = pl.ds(pl.multiple_of(j * width, width), width)
-            out_ref[j] = dot(n_ref[...], w_ref[:, cols], 1, 0).astype(BF16)
-        return carry
-
-    lax.fori_loop(0, out_ref.shape[0] // 2, body, 0)
-
-
 def half_body(first, x_ref, out_ref):
     out_ref[...] = x_ref[:, first : first + out_ref.shape[1]]
 
 
 def combine_body(place, o_ref, g1, g2, g3, own_ref, s1, s2, s3):
     me = jnp.where(place[2] == 0, place[0], place[1])
-    for d, out in enumerate((own_ref, s1, s2, s3)):
-        i = (me + d) % 4
-        total = o_ref[i].astype(F32)
-        for g in (g1, g2, g3):
-            total = total + g[i].astype(F32)
-        out[...] = total.astype(out.dtype)
+    step = 128
+
+    def body(k, carry):
+        part = pl.ds(pl.multiple_of(k * step, step), step)
+        for d, out in enumerate((own_ref, s1, s2, s3)):
+            i = (me + d) % 4
+            total = o_ref[i, part].astype(F32)
+            for g in (g1, g2, g3):
+                total = total + g[i, part].astype(F32)
+            out[part] = total.astype(out.dtype)
+        return carry
+
+    lax.fori_loop(0, own_ref.shape[0] // step, body, 0)
 
 
 def finish_body(factor, own_ref, g1, g2, g3, out_ref):
@@ -190,6 +185,38 @@
     width = w_ref.shape[0]
     start = pl.multiple_of(owner_of(place, step) * width + first, DH)
     return dot(ref[...], w_ref[:, pl.ds(start, ref.shape[1])], 1, 1)
+
+
+def column_product(place, step, n_ref, w_ref):
+    width = n_ref.shape[1]
+    start = pl.multiple_of(owner_of(place, step) * width, width)
+    return dot(n_ref[...], w_ref[:, pl.ds(start, width)], 1, 0)
+
+
+def out_first_body(place, n_ref, w_ref, right_ref, left_ref):
+    half = right_ref.shape[1]
+    total = column_product(place, 4, n_ref, w_ref)
+    right_ref[...] = total[:, :half].astype(BF16)
+    left_ref[...] = total[:, half:].astype(BF16)
+
+
+def out_step_body(step, place, n_ref, w_ref, r_ref, l_ref, right_ref, left_ref):
+    half = n_ref.shape[1] // 2
+    right = column_product(place, step, n_ref, w_ref)
+    left = column_product(place, -step, n_ref, w_ref)
+    if step == 3:
+        right_ref[:, :half] = (right[:, :half] + r_ref[...].astype(F32)).astype(BF16)
+        right_ref[:, half:] = right[:, half:].astype(BF16)
+        left_ref[:, :half] = left[:, :half].astype(BF16)
+        left_ref[:, half:] = (left[:, half:] + l_ref[...].astype(F32)).astype(BF16)
+    else:
+        right_ref[...] = (right + r_ref[...].astype(F32)).astype(BF16)
+        left_ref[...] = (left + l_ref[...].astype(F32)).astype(BF16)
+
+
+def out_last_body(place, n_ref, w_ref, r_ref, l_ref, out_ref):
+    total = column_product(place, 0, n_ref, w_ref)
+    out_ref[...] = (total + r_ref[...].astype(F32) + l_ref[...].astype(F32)).astype(BF16)
 
 
 def grad_near_body(steps, place, *refs):
@@ -212,7 +239,7 @@
         inner = jnp.mean(g * a, axis=-1, keepdims=True)
         ag_ref[b, :, s] = (g * root - a * (inner * root * root * root)).astype(BF16)
 
-    each_head(width, step)
+    each_head(width, step, 1)
     local_states(place, q_ref, ag_ref, keep_ref, send_ref)
 
 
@@ -281,7 +308,7 @@
         dk_ref[b, :, s] = dot(sg, q_ref[b, :, s], 0, 0)
         dv_ref[b, :, s] = dot(scores, ag, 0, 0)
 
-    each_batch(q_ref.shape[2], step)
+    each_head(q_ref.shape[2], step)
 
 
 def outer_body(place, k_ref, v_ref, ik_ref, iv_ref, go, gr, dk_ref, dv_ref):
@@ -290,7 +317,7 @@
         dk_ref[b, :, s] = (ik_ref[b, :, s] + SCALE * dot(v_ref[b, :, s], later, 1, 1)).astype(BF16)
         dv_ref[b, :, s] = (iv_ref[b, :, s] + SCALE * dot(k_ref[b, :, s], later, 1, 0)).astype(BF16)
 
-    each_head(k_ref.shape[2], step)
+    each_head(k_ref.shape[2], step, 1)
 
 
 def shift(value, axis, step):
@@ -349,6 +376,26 @@
         left = shift(left, "head", -1)
         near += [right, left]
     return near
+
+
+def output_ring(place, normed, weight):
+    rows, width = normed.shape
+    flops = 2 * rows * width * width
+    half, whole = [shape((rows, width // 2), BF16)] * 2, [shape((rows, width), BF16)] * 2
+    right, left = call(out_first_body, half, [place, normed, weight], flops, True)
+    for step in (3, 2, 1):
+        right = shift(right, "head", 1)
+        left = shift(left, "head", -1)
+        right, left = call(
+            functools.partial(out_step_body, step),
+            whole,
+            [place, normed, weight, right, left],
+            2 * flops,
+            True,
+        )
+    right = shift(right, "head", 1)
+    left = shift(left, "head", -1)
+    return call(out_last_body, whole[:1], [place, normed, weight, right, left], flops, True)[0]
 
 
 def send_near(place, normed, blocks):
@@ -432,10 +479,7 @@
     )
     normed = normed.reshape(rows, width)
     big = 2 * rows * width * width * n_head
-    partial = call(project_body, [shape((n_head, rows, width), BF16)], [normed, out_weight], big)[0]
-    layer_output = lax.psum_scatter(
-        partial.reshape(n_head * rows, width), "head", scatter_dimension=0, tiled=True
-    ).reshape(queries.shape)
+    layer_output = output_ring(place, normed, out_weight).reshape(queries.shape)
     near = send_near(place, normed, blocks)
     part_grad = call(
         functools.partial(grad_near_body, STEPS),

time: 176 us -> 135 us (0.77)
  waiting for transfers between devices: 75.7 us -> 30.8 us
  between operations: 14.3 us -> 0.94 us
  starting transfers between devices: 53.6 us -> 66.7 us
  Pallas kernels: 27.8 us -> 33.2 us
    ppermute x14 -> x22, waiting for transfers between devices: 51 us -> 21 us  [shift(): return lax.ppermute(value, axis, [(i, (i + step) % n) for i in range(n)])]
    ppermute x18, waiting for transfers between devices: 24.7 us -> 9.76 us  [shift_by_core(): lax.ppermute(value, CTX, [(index(*p), index(*target(*p))) for p in places])]
    ppermute x14 -> x22, starting transfers between devices: 29.5 us -> 40.2 us  [shift(): return lax.ppermute(value, axis, [(i, (i + step) % n) for i in range(n)])]
    pallas_call x21 -> x25, Pallas kernels: 27.8 us -> 33.2 us  [call(): pl.pallas_call(body, out_shape=outs, in_specs=specs, out_specs=[pl.BlockS...]
    ppermute x18, starting transfers between devices: 24.1 us -> 26.5 us  [shift_by_core(): lax.ppermute(value, CTX, [(index(*p), index(*target(*p))) for p in places])]
    unnamed x18 -> x16, local copies, waits for them, and re-layouts: 3.99 us -> 3.1 us
  transfers between devices with their start and end apart: 33 -> 40, of which waited for: 18 -> 14; matrix products, arithmetic and copies ran while one was open for 0% -> 0% of each run, Pallas kernels for 11% -> 23%
where the time goes in v6:
time: 135 us
  starting transfers between devices  66.7 us (49%)
  Pallas kernels  33.2 us (25%)
  waiting for transfers between devices  30.8 us (23%)
  local copies, waits for them, and re-layouts  3.1 us (2%)
    ppermute x22, starting transfers between devices, shift(): return lax.ppermute(value, axis, [(i, (i + step) % n) for i in range(n)])  40.2 us
    pallas_call x25, Pallas kernels, call(): pl.pallas_call(body, out_shape=outs, in_specs=specs, out_specs=[pl.BlockS...  33.2 us
    ppermute x18, starting transfers between devices, shift_by_core(): lax.ppermute(value, CTX, [(index(*p), index(*target(*p))) for p in places])  26.5 us
    ppermute x22, waiting for transfers between devices, shift(): return lax.ppermute(value, axis, [(i, (i + step) % n) for i in range(n)])  21 us
    ppermute x18, waiting for transfers between devices, shift_by_core(): lax.ppermute(value, CTX, [(index(*p), index(*target(*p))) for p in places])  9.76 us
    unnamed x16, local copies, waits for them, and re-layouts  3.1 us
  transfers between devices with their start and end apart: 40, of which 14 were waited for; matrix products, arithmetic and copies ran while one was open for 0% of the time, Pallas kernels for 23%

profile of v6, /device:TPU:1, one launch (start us, length us, event | category | flops | bytes accessed | tf_op | source)
XLA Modules:
  0.0 134.8 jit_solution(6935686536032292172)
XLA Ops:
  0.6 2.5 %collective-permute-start.16 = (bf16[384,512]{1,0:T(8,128)(2,1)}, bf16[384,512]{1,0:T(8,128)(2,1)S(1)}, u32[]{:S(2)}, u32[]{:S(2)}) collective-permute-start(bf16[384,512]{1,0:T(8,128)(2,1)} %bitcast.15), channel_id=1, source_target_pairs={{0,1},{1,2},{2,3},{3,4},{4,5},{5,6},{6,7},{7,0},{8,9},{9,10},{10,1... | collective-permute-start | bytes 1179656 | tf_op jit(solution)/shard_map/ppermute | solution.py:325
  3.2 4.0 %collective-permute-start.20 = (bf16[384,512]{1,0:T(8,128)(2,1)}, bf16[384,512]{1,0:T(8,128)(2,1)S(1)}, u32[]{:S(2)}, u32[]{:S(2)}) collective-permute-start(bf16[384,512]{1,0:T(8,128)(2,1)} %bitcast.16), channel_id=1, source_target_pairs={{0,7},{1,0},{2,1},{3,2},{4,3},{5,4},{6,5},{7,6},{8,15},{9,8},{10,9... | collective-permute-start | bytes 1179656 | tf_op jit(solution)/shard_map/ppermute | solution.py:325
  7.2 8.9 %collective-permute-done.16.refs_1_ = bf16[384,512]{1,0:T(8,128)(2,1)S(1)} collective-permute-done((bf16[384,512]{1,0:T(8,128)(2,1)}, bf16[384,512]{1,0:T(8,128)(2,1)S(1)}, u32[]{:S(2)}, u32[]{:S(2)}) %collective-permute-start.16) | collective-permute-done | bytes 393248 | tf_op jit(solution)/shard_map/ppermute | solution.py:325
  16.1 2.7 %collective-permute-start.21 = (bf16[384,512]{1,0:T(8,128)(2,1)S(1)}, bf16[384,512]{1,0:T(8,128)(2,1)S(1)}, u32[]{:S(2)}, u32[]{:S(2)}) collective-permute-start(bf16[384,512]{1,0:T(8,128)(2,1)S(1)} %collective-permute-done.20.refs_2_), channel_id=1, source_target_pairs={{0,7},{1,0},{2,1},{3,2},{4,3},{5,4},{6,5},{7,6},{8,15},{9,8},{10,9... | collective-permute-start | bytes 1179656 | tf_op jit(solution)/shard_map/ppermute | solution.py:325
  27.8 2.5 %collective-permute-start.2 = (bf16[4,128,128]{2,1,0:T(8,128)(2,1)S(1)}, bf16[4,128,128]{2,1,0:T(8,128)(2,1)S(1)}, u32[]{:S(2)}, u32[]{:S(2)}) collective-permute-start(bf16[4,128,128]{2,1,0:T(8,128)(2,1)S(1)} %shard_map.94.t_ref), channel_id=1, source_target_pairs={{0,32},{8,136},{16,48},{24,152},{32,0},{40,168},{48,16},{56,184},{... | collective-permute-start | bytes 393224 | tf_op jit(solution)/shard_map/ppermute | solution.py:337
  31.4 2.7 %collective-permute-start.22 = (bf16[384,512]{1,0:T(8,128)(2,1)S(1)}, bf16[384,512]{1,0:T(8,128)(2,1)S(1)}, u32[]{:S(2)}, u32[]{:S(2)}) collective-permute-start(bf16[384,512]{1,0:T(8,128)(2,1)S(1)} %collective-permute-done.21.refs_4_), channel_id=1, source_target_pairs={{0,7},{1,0},{2,1},{3,2},{4,3},{5,4},{6,5},{7,6},{8,15},{9,8},{10,9... | collective-permute-start | bytes 1179656 | tf_op jit(solution)/shard_map/ppermute | solution.py:325
  36.5 2.6 %collective-permute-start.5 = (bf16[4,128,128]{2,1,0:T(8,128)(2,1)S(1)}, bf16[4,128,128]{2,1,0:T(8,128)(2,1)S(1)}, u32[]{:S(2)}, u32[]{:S(2)}) collective-permute-start(bf16[4,128,128]{2,1,0:T(8,128)(2,1)S(1)} %get-tuple-element.55), channel_id=1, source_target_pairs={{0,128},{8,40},{16,144},{24,56},{32,160},{40,8},{48,176},{56,24},{... | collective-permute-start | bytes 393224 | tf_op jit(solution)/shard_map/ppermute | solution.py:337
  40.6 2.3 %collective-permute-done.5.g2 = bf16[4,128,128]{2,1,0:T(8,128)(2,1)S(1)} collective-permute-done((bf16[4,128,128]{2,1,0:T(8,128)(2,1)S(1)}, bf16[4,128,128]{2,1,0:T(8,128)(2,1)S(1)}, u32[]{:S(2)}, u32[]{:S(2)}) %collective-permute-start.5) | collective-permute-done | bytes 131104 | tf_op jit(solution)/shard_map/ppermute | solution.py:337
  43.9 3.3 %collective-permute-start.7 = (bf16[4,128,128]{2,1,0:T(8,128)(2,1)S(1)}, bf16[4,128,128]{2,1,0:T(8,128)(2,1)S(1)}, u32[]{:S(2)}, u32[]{:S(2)}) collective-permute-start(bf16[4,128,128]{2,1,0:T(8,128)(2,1)S(1)} %get-tuple-element.58), channel_id=1, source_target_pairs={{0,8},{8,0},{1,9},{9,1},{2,10},{10,2},{3,11},{11,3},{4,12},{12,4},... | collective-permute-start | bytes 393224 | tf_op jit(solution)/shard_map/ppermute | solution.py:325
  54.2 2.7 %collective-permute-start.9 = (bf16[384,256]{1,0:T(8,128)(2,1)S(1)}, bf16[384,256]{1,0:T(8,128)(2,1)S(1)}, u32[]{:S(2)}, u32[]{:S(2)}) collective-permute-start(bf16[384,256]{1,0:T(8,128)(2,1)S(1)} %get-tuple-element.61), channel_id=1, source_target_pairs={{0,7},{1,0},{2,1},{3,2},{4,3},{5,4},{6,5},{7,6},{8,15},{9,8},{10,9... | collective-permute-start | bytes 589832 | tf_op jit(solution)/shard_map/ppermute | solution.py:325
  56.9 4.6 %collective-permute-done.8.r_ref = bf16[384,256]{1,0:T(8,128)(2,1)S(1)} collective-permute-done((bf16[384,256]{1,0:T(8,128)(2,1)S(1)}, bf16[384,256]{1,0:T(8,128)(2,1)S(1)}, u32[]{:S(2)}, u32[]{:S(2)}) %collective-permute-start.8) | collective-permute-done | bytes 196640 | tf_op jit(solution)/shard_map/ppermute | solution.py:325
  62.7 2.7 %collective-permute-start.11 = (bf16[384,512]{1,0:T(8,128)(2,1)S(1)}, bf16[384,512]{1,0:T(8,128)(2,1)S(1)}, u32[]{:S(2)}, u32[]{:S(2)}) collective-permute-start(bf16[384,512]{1,0:T(8,128)(2,1)S(1)} %get-tuple-element.63), channel_id=1, source_target_pairs={{0,7},{1,0},{2,1},{3,2},{4,3},{5,4},{6,5},{7,6},{8,15},{9,8},{10,9... | collective-permute-start | bytes 1179656 | tf_op jit(solution)/shard_map/ppermute | solution.py:325
  65.5 2.7 %collective-permute-start.23 = (bf16[384,256]{1,0:T(8,128)(2,1)S(1)}, bf16[384,256]{1,0:T(8,128)(2,1)S(1)}, u32[]{:S(2)}, u32[]{:S(2)}) collective-permute-start(bf16[384,256]{1,0:T(8,128)(2,1)S(1)} %shard_map.104), channel_id=1, source_target_pairs={{0,7},{1,0},{2,1},{3,2},{4,3},{5,4},{6,5},{7,6},{8,15},{9,8},{10,9... | collective-permute-start | bytes 589832 | tf_op jit(solution)/shard_map/ppermute | solution.py:325
  68.2 5.1 %collective-permute-done.10.r_ref = bf16[384,512]{1,0:T(8,128)(2,1)S(1)} collective-permute-done((bf16[384,512]{1,0:T(8,128)(2,1)S(1)}, bf16[384,512]{1,0:T(8,128)(2,1)S(1)}, u32[]{:S(2)}, u32[]{:S(2)}) %collective-permute-start.10) | collective-permute-done | bytes 393248 | tf_op jit(solution)/shard_map/ppermute | solution.py:325
  78.4 3.4 %collective-permute-start.33 = (bf16[2,512,128]{2,1,0:T(8,128)(2,1)S(1)}, bf16[2,512,128]{2,1,0:T(8,128)(2,1)S(1)}, u32[]{:S(2)}, u32[]{:S(2)}) collective-permute-start(bf16[2,512,128]{2,1,0:T(8,128)(2,1)S(1)} %shard_map.113), channel_id=1, source_target_pairs={{0,8},{8,0},{1,9},{9,1},{2,10},{10,2},{3,11},{11,3},{4,12},{12,4},... | collective-permute-start | bytes 786440 | tf_op jit(solution)/shard_map/ppermute | solution.py:325
  84.0 3.0 %shard_map.106 = (bf16[2,192,512]{2,1,0:T(8,128)(2,1)S(1)}, f32[4,128,128]{2,1,0:T(8,128)S(1)}, bf16[4,128,128]{2,1,0:T(8,128)(2,1)S(1)}) custom-call(s32[4]{0:T(128)S(1)} %pad_add_fusion.place, bf16[384,256]{1,0:T(8,128)(2,1)S(1)} %collective-permute-done.19.refs_0_.r4.refs_7_, bf16[384,256]{1,0:T(8,128)(2,1)S(1)} %collective-permute-done.23.refs_1_.l4.refs_8_, ...), custom_call_target="tpu_custom_call" | custom-call | flops 201326592 | bytes 7340048 | tf_op jit(solution)/shard_map/pallas_call | solution.py:34
  89.8 2.5 %collective-permute-start.26 = (bf16[4,128,128]{2,1,0:T(8,128)(2,1)S(1)}, bf16[4,128,128]{2,1,0:T(8,128)(2,1)S(1)}, u32[]{:S(2)}, u32[]{:S(2)}) collective-permute-start(bf16[4,128,128]{2,1,0:T(8,128)(2,1)S(1)} %shard_map.108.t_ref), channel_id=1, source_target_pairs={{0,32},{8,136},{16,48},{24,152},{32,0},{40,168},{48,16},{56,184},{... | collective-permute-start | bytes 393224 | tf_op jit(solution)/shard_map/ppermute | solution.py:337
  101.5 2.7 %collective-permute-start.29 = (bf16[4,128,128]{2,1,0:T(8,128)(2,1)S(1)}, bf16[4,128,128]{2,1,0:T(8,128)(2,1)S(1)}, u32[]{:S(2)}, u32[]{:S(2)}) collective-permute-start(bf16[4,128,128]{2,1,0:T(8,128)(2,1)S(1)} %get-tuple-element.77), channel_id=1, source_target_pairs={{0,128},{8,40},{16,144},{24,56},{32,160},{40,8},{48,176},{56,24},{... | collective-permute-start | bytes 393224 | tf_op jit(solution)/shard_map/ppermute | solution.py:337
  106.3 2.3 %collective-permute-done.29.g2 = bf16[4,128,128]{2,1,0:T(8,128)(2,1)S(1)} collective-permute-done((bf16[4,128,128]{2,1,0:T(8,128)(2,1)S(1)}, bf16[4,128,128]{2,1,0:T(8,128)(2,1)S(1)}, u32[]{:S(2)}, u32[]{:S(2)}) %collective-permute-start.29) | collective-permute-done | bytes 131104 | tf_op jit(solution)/shard_map/ppermute | solution.py:337
  109.9 3.7 %collective-permute-done.30.g3 = bf16[4,128,128]{2,1,0:T(8,128)(2,1)S(1)} collective-permute-done((bf16[4,128,128]{2,1,0:T(8,128)(2,1)S(1)}, bf16[4,128,128]{2,1,0:T(8,128)(2,1)S(1)}, u32[]{:S(2)}, u32[]{:S(2)}) %collective-permute-start.30) | collective-permute-done | bytes 131104 | tf_op jit(solution)/shard_map/ppermute | solution.py:337
  115.1 5.6 %collective-permute-start.31 = (bf16[4,128,128]{2,1,0:T(8,128)(2,1)S(1)}, bf16[4,128,128]{2,1,0:T(8,128)(2,1)S(1)}, u32[]{:S(2)}, u32[]{:S(2)}) collective-permute-start(bf16[4,128,128]{2,1,0:T(8,128)(2,1)S(1)} %get-tuple-element.80), channel_id=1, source_target_pairs={{0,8},{8,0},{1,9},{9,1},{2,10},{10,2},{3,11},{11,3},{4,12},{12,4},... | collective-permute-start | bytes 393224 | tf_op jit(solution)/shard_map/ppermute | solution.py:325
  122.4 2.2 %collective-permute-start.38 = (bf16[512,128]{1,0:T(8,128)(2,1)S(1)}, bf16[512,128]{1,0:T(8,128)(2,1)S(1)}, u32[]{:S(2)}, u32[]{:S(2)}) collective-permute-start(bf16[512,128]{1,0:T(8,128)(2,1)S(1)} %get-tuple-element.89), channel_id=1, source_target_pairs={{0,128},{8,40},{16,144},{24,56},{32,160},{40,8},{48,176},{56,24},{... | collective-permute-start | bytes 393224 | tf_op jit(solution)/shard_map/ppermute | solution.py:337
  125.1 4.3 %shard_map.107 = (bf16[2,192,512]{2,1,0:T(8,128)(2,1)}, f32[2,192,512]{2,1,0:T(8,128)S(1)}, f32[2,192,512]{2,1,0:T(8,128)S(1)}) custom-call(s32[4]{0:T(128)S(1)} %pad_add_fusion.place, bf16[2,192,512]{2,1,0:T(8,128)(2,1)S(1)} %copy-done.7, bf16[2,192,512]{2,1,0:T(8,128)(2,1)S(1)} %copy-done.3, bf16[2,192,512]{2,1,0:T(8,128)(2,1)S(1)} %copy-done.5, ...), custom_call_target="tpu_custom_call" | custom-call | flops 251658240 | bytes 3801104 | tf_op jit(solution)/shard_map/pallas_call | solution.py:34
  129.5 2.9 %shard_map.111 = (bf16[2,192,512]{2,1,0:T(8,128)(2,1)}, bf16[2,192,512]{2,1,0:T(8,128)(2,1)}) custom-call(s32[4]{0:T(128)S(1)} %pad_add_fusion.place, bf16[2,192,512]{2,1,0:T(8,128)(2,1)S(1)} %copy-done.3, bf16[2,192,512]{2,1,0:T(8,128)(2,1)S(1)} %copy-done.5, f32[2,192,512]{2,1,0:T(8,128)S(1)} %get-tuple-element.71.ik_ref, ...), custom_call_target="tpu_custom_call" | custom-call | flops 100663296 | bytes 3407888 | tf_op jit(solution)/shard_map/pallas_call | solution.py:34
  (98 shorter events, 51.9 us)
Async XLA Ops:
  0.6 15.5 %collective-permute-start.16 = (bf16[384,512]{1,0:T(8,128)(2,1)}, bf16[384,512]{1,0:T(8,128)(2,1)S(1)}, u32[]{:S(2)}, u32[]{:S(2)}) collective-permute-start(bf16[384,512]{1,0:T(8,128)(2,1)} %bitcast.15), channel_id=1, source_target_pairs={{0,1},{1,2},{2,3},{3,4},{4,5},{5,6},{6,7},{7,0},{8,9},{9,10},{10,1... | collective-permute-start | bytes 1179656 | tf_op jit(solution)/shard_map/ppermute | solution.py:325
  3.2 13.0 %collective-permute-start.20 = (bf16[384,512]{1,0:T(8,128)(2,1)}, bf16[384,512]{1,0:T(8,128)(2,1)S(1)}, u32[]{:S(2)}, u32[]{:S(2)}) collective-permute-start(bf16[384,512]{1,0:T(8,128)(2,1)} %bitcast.16), channel_id=1, source_target_pairs={{0,7},{1,0},{2,1},{3,2},{4,3},{5,4},{6,5},{7,6},{8,15},{9,8},{10,9... | collective-permute-start | bytes 1179656 | tf_op jit(solution)/shard_map/ppermute | solution.py:325
  16.1 15.2 %collective-permute-start.17 = (bf16[384,512]{1,0:T(8,128)(2,1)S(1)}, bf16[384,512]{1,0:T(8,128)(2,1)S(1)}, u32[]{:S(2)}, u32[]{:S(2)}) collective-permute-start(bf16[384,512]{1,0:T(8,128)(2,1)S(1)} %collective-permute-done.16.refs_1_), channel_id=1, source_target_pairs={{0,1},{1,2},{2,3},{3,4},{4,5},{5,6},{6,7},{7,0},{8,9},{9,10},{10,1... | collective-permute-start | bytes 1179656 | tf_op jit(solution)/shard_map/ppermute | solution.py:325
  16.1 15.2 %collective-permute-start.21 = (bf16[384,512]{1,0:T(8,128)(2,1)S(1)}, bf16[384,512]{1,0:T(8,128)(2,1)S(1)}, u32[]{:S(2)}, u32[]{:S(2)}) collective-permute-start(bf16[384,512]{1,0:T(8,128)(2,1)S(1)} %collective-permute-done.20.refs_2_), channel_id=1, source_target_pairs={{0,7},{1,0},{2,1},{3,2},{4,3},{5,4},{6,5},{7,6},{8,15},{9,8},{10,9... | collective-permute-start | bytes 1179656 | tf_op jit(solution)/shard_map/ppermute | solution.py:325
  31.4 19.6 %collective-permute-start.18 = (bf16[384,512]{1,0:T(8,128)(2,1)S(1)}, bf16[384,512]{1,0:T(8,128)(2,1)S(1)}, u32[]{:S(2)}, u32[]{:S(2)}) collective-permute-start(bf16[384,512]{1,0:T(8,128)(2,1)S(1)} %collective-permute-done.17.refs_3_), channel_id=1, source_target_pairs={{0,1},{1,2},{2,3},{3,4},{4,5},{5,6},{6,7},{7,0},{8,9},{9,10},{10,1... | collective-permute-start | bytes 1179656 | tf_op jit(solution)/shard_map/ppermute | solution.py:325
  31.4 19.6 %collective-permute-start.22 = (bf16[384,512]{1,0:T(8,128)(2,1)S(1)}, bf16[384,512]{1,0:T(8,128)(2,1)S(1)}, u32[]{:S(2)}, u32[]{:S(2)}) collective-permute-start(bf16[384,512]{1,0:T(8,128)(2,1)S(1)} %collective-permute-done.21.refs_4_), channel_id=1, source_target_pairs={{0,7},{1,0},{2,1},{3,2},{4,3},{5,4},{6,5},{7,6},{8,15},{9,8},{10,9... | collective-permute-start | bytes 1179656 | tf_op jit(solution)/shard_map/ppermute | solution.py:325
  52.9 39.5 %collective-permute-start.32 = (bf16[4,4,512,128]{3,2,1,0:T(8,128)(2,1)S(1)}, bf16[4,4,512,128]{3,2,1,0:T(8,128)(2,1)S(1)}, u32[]{:S(2)}, u32[]{:S(2)}) collective-permute-start(bf16[4,4,512,128]{3,2,1,0:T(8,128)(2,1)S(1)} %shard_map.112), channel_id=1, source_target_pairs={{0,8},{8,0},{1,9},{9,1},{2,10},{10,2},{3,11},{11,3},{4,12},{12,4},... | collective-permute-start | bytes 6291464 | tf_op jit(solution)/shard_map/ppermute | solution.py:325
  62.6 10.7 %collective-permute-start.10 = (bf16[384,512]{1,0:T(8,128)(2,1)S(1)}, bf16[384,512]{1,0:T(8,128)(2,1)S(1)}, u32[]{:S(2)}, u32[]{:S(2)}) collective-permute-start(bf16[384,512]{1,0:T(8,128)(2,1)S(1)} %get-tuple-element.62), channel_id=1, source_target_pairs={{0,1},{1,2},{2,3},{3,4},{4,5},{5,6},{6,7},{7,0},{8,9},{9,10},{10,1... | collective-permute-start | bytes 1179656 | tf_op jit(solution)/shard_map/ppermute | solution.py:325
  62.7 10.6 %collective-permute-start.11 = (bf16[384,512]{1,0:T(8,128)(2,1)S(1)}, bf16[384,512]{1,0:T(8,128)(2,1)S(1)}, u32[]{:S(2)}, u32[]{:S(2)}) collective-permute-start(bf16[384,512]{1,0:T(8,128)(2,1)S(1)} %get-tuple-element.63), channel_id=1, source_target_pairs={{0,7},{1,0},{2,1},{3,2},{4,3},{5,4},{6,5},{7,6},{8,15},{9,8},{10,9... | collective-permute-start | bytes 1179656 | tf_op jit(solution)/shard_map/ppermute | solution.py:325
  65.4 12.1 %collective-permute-start.19 = (bf16[384,256]{1,0:T(8,128)(2,1)S(1)}, bf16[384,256]{1,0:T(8,128)(2,1)S(1)}, u32[]{:S(2)}, u32[]{:S(2)}) collective-permute-start(bf16[384,256]{1,0:T(8,128)(2,1)S(1)} %shard_map.103), channel_id=1, source_target_pairs={{0,1},{1,2},{2,3},{3,4},{4,5},{5,6},{6,7},{7,0},{8,9},{9,10},{10,1... | collective-permute-start | bytes 589832 | tf_op jit(solution)/shard_map/ppermute | solution.py:325
  65.5 12.0 %collective-permute-start.23 = (bf16[384,256]{1,0:T(8,128)(2,1)S(1)}, bf16[384,256]{1,0:T(8,128)(2,1)S(1)}, u32[]{:S(2)}, u32[]{:S(2)}) collective-permute-start(bf16[384,256]{1,0:T(8,128)(2,1)S(1)} %shard_map.104), channel_id=1, source_target_pairs={{0,7},{1,0},{2,1},{3,2},{4,3},{5,4},{6,5},{7,6},{8,15},{9,8},{10,9... | collective-permute-start | bytes 589832 | tf_op jit(solution)/shard_map/ppermute | solution.py:325
  74.4 25.3 %collective-permute-start.12 = (bf16[384,512]{1,0:T(8,128)(2,1)S(1)}, bf16[384,512]{1,0:T(8,128)(2,1)S(1)}, u32[]{:S(2)}, u32[]{:S(2)}) collective-permute-start(bf16[384,512]{1,0:T(8,128)(2,1)S(1)} %get-tuple-element.64), channel_id=1, source_target_pairs={{0,1},{1,2},{2,3},{3,4},{4,5},{5,6},{6,7},{7,0},{8,9},{9,10},{10,1... | collective-permute-start | bytes 1179656 | tf_op jit(solution)/shard_map/ppermute | solution.py:325
  78.4 11.4 %collective-permute-start.33 = (bf16[2,512,128]{2,1,0:T(8,128)(2,1)S(1)}, bf16[2,512,128]{2,1,0:T(8,128)(2,1)S(1)}, u32[]{:S(2)}, u32[]{:S(2)}) collective-permute-start(bf16[2,512,128]{2,1,0:T(8,128)(2,1)S(1)} %shard_map.113), channel_id=1, source_target_pairs={{0,8},{8,0},{1,9},{9,1},{2,10},{10,2},{3,11},{11,3},{4,12},{12,4},... | collective-permute-start | bytes 786440 | tf_op jit(solution)/shard_map/ppermute | solution.py:325
  87.1 14.4 %collective-permute-start.13 = (bf16[384,512]{1,0:T(8,128)(2,1)S(1)}, bf16[384,512]{1,0:T(8,128)(2,1)S(1)}, u32[]{:S(2)}, u32[]{:S(2)}) collective-permute-start(bf16[384,512]{1,0:T(8,128)(2,1)S(1)} %get-tuple-element.65), channel_id=1, source_target_pairs={{0,7},{1,0},{2,1},{3,2},{4,3},{5,4},{6,5},{7,6},{8,15},{9,8},{10,9... | collective-permute-start | bytes 1179656 | tf_op jit(solution)/shard_map/ppermute | solution.py:325
  95.1 20.0 %collective-permute-start.34 = (bf16[4,512,128]{2,1,0:T(8,128)(2,1)S(1)}, bf16[4,512,128]{2,1,0:T(8,128)(2,1)S(1)}, u32[]{:S(2)}, u32[]{:S(2)}) collective-permute-start(bf16[4,512,128]{2,1,0:T(8,128)(2,1)S(1)} %get-tuple-element.84), channel_id=1, source_target_pairs={{0,16},{8,72},{16,32},{24,88},{32,48},{40,104},{48,0},{56,120},{64... | collective-permute-start | bytes 1572872 | tf_op jit(solution)/shard_map/ppermute | solution.py:337
  98.1 22.6 %collective-permute-start.35 = (bf16[4,512,128]{2,1,0:T(8,128)(2,1)S(1)}, bf16[4,512,128]{2,1,0:T(8,128)(2,1)S(1)}, u32[]{:S(2)}, u32[]{:S(2)}) collective-permute-start(bf16[4,512,128]{2,1,0:T(8,128)(2,1)S(1)} %get-tuple-element.85), channel_id=1, source_target_pairs={{0,32},{8,136},{16,48},{24,152},{32,0},{40,168},{48,16},{56,184},{... | collective-permute-start | bytes 1572872 | tf_op jit(solution)/shard_map/ppermute | solution.py:337
  99.7 21.0 %collective-permute-start.36 = (bf16[4,512,128]{2,1,0:T(8,128)(2,1)S(1)}, bf16[4,512,128]{2,1,0:T(8,128)(2,1)S(1)}, u32[]{:S(2)}, u32[]{:S(2)}) collective-permute-start(bf16[4,512,128]{2,1,0:T(8,128)(2,1)S(1)} %get-tuple-element.86), channel_id=1, source_target_pairs={{0,48},{8,200},{16,0},{24,216},{32,16},{40,232},{48,32},{56,248},{... | collective-permute-start | bytes 1572872 | tf_op jit(solution)/shard_map/ppermute | solution.py:337
  104.3 9.4 %collective-permute-start.30 = (bf16[4,128,128]{2,1,0:T(8,128)(2,1)S(1)}, bf16[4,128,128]{2,1,0:T(8,128)(2,1)S(1)}, u32[]{:S(2)}, u32[]{:S(2)}) collective-permute-start(bf16[4,128,128]{2,1,0:T(8,128)(2,1)S(1)} %get-tuple-element.78), channel_id=1, source_target_pairs={{0,192},{8,56},{16,208},{24,8},{32,224},{40,24},{48,240},{56,40},{... | collective-permute-start | bytes 393224 | tf_op jit(solution)/shard_map/ppermute | solution.py:337
  108.6 23.7 %collective-permute-start.14 = (bf16[384,512]{1,0:T(8,128)(2,1)S(1)}, bf16[384,512]{1,0:T(8,128)(2,1)S(1)}, u32[]{:S(2)}, u32[]{:S(2)}) collective-permute-start(bf16[384,512]{1,0:T(8,128)(2,1)S(1)} %get-tuple-element.66), channel_id=1, source_target_pairs={{0,1},{1,2},{2,3},{3,4},{4,5},{5,6},{6,7},{7,0},{8,9},{9,10},{10,1... | collective-permute-start | bytes 1179656 | tf_op jit(solution)/shard_map/ppermute | solution.py:325
  113.6 18.7 %collective-permute-start.15 = (bf16[384,512]{1,0:T(8,128)(2,1)S(1)}, bf16[384,512]{1,0:T(8,128)(2,1)S(1)}, u32[]{:S(2)}, u32[]{:S(2)}) collective-permute-start(bf16[384,512]{1,0:T(8,128)(2,1)S(1)} %get-tuple-element.67), channel_id=1, source_target_pairs={{0,7},{1,0},{2,1},{3,2},{4,3},{5,4},{6,5},{7,6},{8,15},{9,8},{10,9... | collective-permute-start | bytes 1179656 | tf_op jit(solution)/shard_map/ppermute | solution.py:325
  115.1 9.6 %collective-permute-start.31 = (bf16[4,128,128]{2,1,0:T(8,128)(2,1)S(1)}, bf16[4,128,128]{2,1,0:T(8,128)(2,1)S(1)}, u32[]{:S(2)}, u32[]{:S(2)}) collective-permute-start(bf16[4,128,128]{2,1,0:T(8,128)(2,1)S(1)} %get-tuple-element.80), channel_id=1, source_target_pairs={{0,8},{8,0},{1,9},{9,1},{2,10},{10,2},{3,11},{11,3},{4,12},{12,4},... | collective-permute-start | bytes 393224 | tf_op jit(solution)/shard_map/ppermute | solution.py:325
  121.5 12.5 %collective-permute-start.37 = (bf16[512,128]{1,0:T(8,128)(2,1)S(1)}, bf16[512,128]{1,0:T(8,128)(2,1)S(1)}, u32[]{:S(2)}, u32[]{:S(2)}) collective-permute-start(bf16[512,128]{1,0:T(8,128)(2,1)S(1)} %get-tuple-element.88), channel_id=1, source_target_pairs={{0,64},{8,24},{16,80},{24,40},{32,96},{40,56},{48,112},{56,8},{64,... | collective-permute-start | bytes 393224 | tf_op jit(solution)/shard_map/ppermute | solution.py:337
  122.4 11.6 %collective-permute-start.38 = (bf16[512,128]{1,0:T(8,128)(2,1)S(1)}, bf16[512,128]{1,0:T(8,128)(2,1)S(1)}, u32[]{:S(2)}, u32[]{:S(2)}) collective-permute-start(bf16[512,128]{1,0:T(8,128)(2,1)S(1)} %get-tuple-element.89), channel_id=1, source_target_pairs={{0,128},{8,40},{16,144},{24,56},{32,160},{40,8},{48,176},{56,24},{... | collective-permute-start | bytes 393224 | tf_op jit(solution)/shard_map/ppermute | solution.py:337
  124.7 9.4 %collective-permute-start.39 = (bf16[512,128]{1,0:T(8,128)(2,1)S(1)}, bf16[512,128]{1,0:T(8,128)(2,1)S(1)}, u32[]{:S(2)}, u32[]{:S(2)}) collective-permute-start(bf16[512,128]{1,0:T(8,128)(2,1)S(1)} %get-tuple-element.90), channel_id=1, source_target_pairs={{0,192},{8,56},{16,208},{24,8},{32,224},{40,24},{48,240},{56,40},{... | collective-permute-start | bytes 393224 | tf_op jit(solution)/shard_map/ppermute | solution.py:337
  (24 other events, 146.1 us)

commit v7 on v6

--- a/solution.py
+++ b/solution.py
@@ -53,13 +53,14 @@
 def local_states(place, left, right, keep_ref, send_ref):
     mc = place[2]
 
-    def body(h, carry):
-        s = pl.ds(pl.multiple_of(h * DH, DH), DH)
-        keep_ref[h] = dot(left[mc, :, s], right[mc, :, s], 0, 0)
-        send_ref[h] = dot(left[1 - mc, :, s], right[1 - mc, :, s], 0, 0).astype(BF16)
+    def body(i, carry):
+        for h in (2 * i, 2 * i + 1):
+            s = pl.ds(pl.multiple_of(h * DH, DH), DH)
+            keep_ref[h] = dot(left[mc, :, s], right[mc, :, s], 0, 0)
+            send_ref[h] = dot(left[1 - mc, :, s], right[1 - mc, :, s], 0, 0).astype(BF16)
         return carry
 
-    lax.fori_loop(0, keep_ref.shape[0], body, 0)
+    lax.fori_loop(0, keep_ref.shape[0] // 2, body, 0)
 
 
 def state_body(place, k_ref, v_ref, q_hbm, keep_ref, send_ref, k_out, v_out, q_out, sem):
@@ -112,6 +113,15 @@
     return jnp.where(place[2] == b, own_ref[h], other_ref[h])
 
 
+def each_batch(width, step):
+    def body(b, carry):
+        for h in range(width // DH):
+            step(b, h, b * (width // DH) + h, slice(h * DH, (h + 1) * DH))
+        return carry
+
+    lax.fori_loop(0, 2, body, 0)
+
+
 def each_head(width, step, group=2):
     n = width // DH
 
@@ -135,7 +145,7 @@
         scores = masked_scores(lower, q_ref[b, :, s], k_ref[b, :, s])
         intra_ref[b, :, s] = dot(scores, v_ref[b, :, s], 1, 0)
 
-    each_head(q_ref.shape[2], step)
+    each_batch(q_ref.shape[2], step)
 
 
 def forward_body(place, q_ref, intra_ref, so_ref, sr_ref, normed_ref, attended_ref):
@@ -146,7 +156,7 @@
         mean = jnp.mean(attended * attended, axis=-1, keepdims=True)
         normed_ref[b, :, s] = (attended / jnp.sqrt(mean + EPS)).astype(BF16)
 
-    each_head(q_ref.shape[2], step)
+    each_batch(q_ref.shape[2], step)
 
 
 def half_body(first, x_ref, out_ref):
@@ -239,7 +249,7 @@
         inner = jnp.mean(g * a, axis=-1, keepdims=True)
         ag_ref[b, :, s] = (g * root - a * (inner * root * root * root)).astype(BF16)
 
-    each_head(width, step, 1)
+    each_head(width, step, 2)
     local_states(place, q_ref, ag_ref, keep_ref, send_ref)
 
 
@@ -261,32 +271,28 @@
     return r[:, :DH], r[:, DH:]
 
 
-def weight_near_body(steps, place, n_ref, *refs):
-    *blocks, out_ref = refs
+def weight_out_body(steps, place, n_ref, *refs):
+    *blocks, r4, l4, out_ref = refs
     mc = 1 - place[2]
     for step, ref in zip(steps, blocks):
         pieces = weight_pair(mc, n_ref, ref, ref, 0, 2 * DH)
         for (far, other), piece in zip(weight_tiles(place, mc, step), pieces):
             out_ref[far, other] = piece.astype(BF16)
-    for far, other in weight_tiles(place, mc, 4):
-        out_ref[far, other] = jnp.zeros(out_ref.shape[2:], BF16)
-
-
-def weight_far_body(place, n_ref, r4, l4, out_ref):
-    for j, piece in enumerate(weight_pair(1 - place[2], n_ref, r4, l4, 0, 0)):
-        out_ref[j] = piece.astype(BF16)
+    pieces = weight_pair(mc, n_ref, r4, l4, 0, 0)
+    for (far, other), piece in zip(weight_tiles(place, mc, 4), pieces):
+        out_ref[far, other] = piece.astype(BF16)
 
 
 def weight_add_body(steps, place, n_ref, *refs):
-    *blocks, r4, l4, near_ref, far_ref, o0, o1, o2, o3, buf, sem = refs
+    *blocks, r4, l4, in_ref, o0, o1, o2, o3, buf, sem = refs
     mc = place[2]
     for step, ref in zip(steps, blocks):
         pieces = weight_pair(mc, n_ref, ref, ref, 0, 2 * DH)
         for (far, other), piece in zip(weight_tiles(place, mc, step), pieces):
-            buf[far, other] = (piece + near_ref[far, other].astype(F32)).astype(BF16)
+            buf[far, other] = (piece + in_ref[far, other].astype(F32)).astype(BF16)
     pieces = weight_pair(mc, n_ref, r4, l4, 0, 0)
-    for j, ((far, other), piece) in enumerate(zip(weight_tiles(place, mc, 4), pieces)):
-        buf[far, other] = (piece + far_ref[j].astype(F32)).astype(BF16)
+    for (far, other), piece in zip(weight_tiles(place, mc, 4), pieces):
+        buf[far, other] = (piece + in_ref[far, other].astype(F32)).astype(BF16)
     copies = [
         pltpu.make_async_copy(buf.at[d], o, sem.at[d]) for d, o in enumerate((o0, o1, o2, o3))
     ]
@@ -317,7 +323,7 @@
         dk_ref[b, :, s] = (ik_ref[b, :, s] + SCALE * dot(v_ref[b, :, s], later, 1, 1)).astype(BF16)
         dv_ref[b, :, s] = (iv_ref[b, :, s] + SCALE * dot(k_ref[b, :, s], later, 1, 0)).astype(BF16)
 
-    each_head(k_ref.shape[2], step, 1)
+    each_batch(k_ref.shape[2], step)
 
 
 def shift(value, axis, step):
@@ -398,30 +404,26 @@
     return call(out_last_body, whole[:1], [place, normed, weight, right, left], flops, True)[0]
 
 
-def send_near(place, normed, blocks):
+def send_weight(place, normed, blocks):
     rows, width = normed.shape
-    near = call(
-        functools.partial(weight_near_body, STEPS),
+    theirs = call(
+        functools.partial(weight_out_body, STEPS),
         [shape((4, 4, width, DH), BF16)],
-        [place, normed, *blocks[:7]],
-        rows * width * width * 7,
+        [place, normed, *blocks],
+        rows * width * width * 8,
         True,
     )[0]
-    return shift(near, "ctx_2", 1)
-
-
-def reduce_weight(place, normed, blocks, near, factor):
+    return shift(theirs, "ctx_2", 1)
+
+
+def reduce_weight(place, normed, blocks, theirs, factor):
     rows, width = normed.shape
     flops = rows * width * width
-    far = call(
-        weight_far_body, [shape((2, width, DH), BF16)], [place, normed, *blocks[7:]], flops, True
-    )[0]
-    far = shift(far, "ctx_2", 1)
     whole = (4, width, DH)
     own, *send = call(
         functools.partial(weight_add_body, STEPS),
         [shape(whole, BF16)] * 4,
-        [place, normed, *blocks, near, far],
+        [place, normed, *blocks, theirs],
         flops * 8,
         True,
         [VMEM((4, *whole), BF16), pltpu.SemaphoreType.DMA((4,))],
@@ -480,7 +482,7 @@
     normed = normed.reshape(rows, width)
     big = 2 * rows * width * width * n_head
     layer_output = output_ring(place, normed, out_weight).reshape(queries.shape)
-    near = send_near(place, normed, blocks)
+    theirs = send_weight(place, normed, blocks)
     part_grad = call(
         functools.partial(grad_near_body, STEPS),
         [shape((rows, width), F32)],
@@ -497,7 +499,7 @@
         [VMEM(queries.shape, F32)],
     )
     factor = (rows * lax.axis_size(CTX)) ** (-0.5)
-    weight_grad = reduce_weight(place, normed, blocks, near, factor)
+    weight_grad = reduce_weight(place, normed, blocks, theirs, factor)
     grad_state = exclusive(place, keep, send, True)
     query_grad, inner_key, inner_value = call(
         inner_body,

time: 135 us -> 141 us (1.044)
  waiting for transfers between devices: 30.8 us -> 42 us
  Pallas kernels: 33.2 us -> 29.2 us
  starting transfers between devices: 66.7 us -> 65 us
    ppermute x22 -> x21, waiting for transfers between devices: 21 us -> 31.3 us  [shift(): return lax.ppermute(value, axis, [(i, (i + step) % n) for i in range(n)])]
    pallas_call x25 -> x24, Pallas kernels: 33.2 us -> 29.2 us  [call(): pl.pallas_call(body, out_shape=outs, in_specs=specs, out_specs=[pl.BlockS...]
    ppermute x18, starting transfers between devices: 26.5 us -> 24.5 us  [shift_by_core(): lax.ppermute(value, CTX, [(index(*p), index(*target(*p))) for p in places])]
    ppermute x22 -> x21, starting transfers between devices: 40.2 us -> 40.6 us  [shift(): return lax.ppermute(value, axis, [(i, (i + step) % n) for i in range(n)])]
  transfers between devices with their start and end apart: 40 -> 39, of which waited for: 14 -> 14; matrix products, arithmetic and copies ran while one was open for 0% -> 0% of each run, Pallas kernels for 23% -> 19%
where the time goes in v7:
time: 141 us; the launch traced here: 140 us
  starting transfers between devices  65 us (46%)
  waiting for transfers between devices  42 us (30%)
  Pallas kernels  29.2 us (21%)
  local copies, waits for them, and re-layouts  3.04 us (2%)
    ppermute x21, starting transfers between devices, shift(): return lax.ppermute(value, axis, [(i, (i + step) % n) for i in range(n)])  40.6 us
    ppermute x21, waiting for transfers between devices, shift(): return lax.ppermute(value, axis, [(i, (i + step) % n) for i in range(n)])  31.3 us
    pallas_call x24, Pallas kernels, call(): pl.pallas_call(body, out_shape=outs, in_specs=specs, out_specs=[pl.BlockS...  29.2 us
    ppermute x18, starting transfers between devices, shift_by_core(): lax.ppermute(value, CTX, [(index(*p), index(*target(*p))) for p in places])  24.5 us
    ppermute x18, waiting for transfers between devices, shift_by_core(): lax.ppermute(value, CTX, [(index(*p), index(*target(*p))) for p in places])  10.7 us
    unnamed x16, local copies, waits for them, and re-layouts  3.04 us
  transfers between devices with their start and end apart: 39, of which 14 were waited for; matrix products, arithmetic and copies ran while one was open for 0% of the time, Pallas kernels for 19%

profile of v7, /device:TPU:1, one launch (start us, length us, event | category | flops | bytes accessed | tf_op | source)
XLA Modules:
  0.0 140.3 jit_solution(15129946637549645903)
XLA Ops:
  0.6 2.5 %collective-permute-start.16 = (bf16[384,512]{1,0:T(8,128)(2,1)}, bf16[384,512]{1,0:T(8,128)(2,1)S(1)}, u32[]{:S(2)}, u32[]{:S(2)}) collective-permute-start(bf16[384,512]{1,0:T(8,128)(2,1)} %bitcast.14), channel_id=1, source_target_pairs={{0,1},{1,2},{2,3},{3,4},{4,5},{5,6},{6,7},{7,0},{8,9},{9,10},{10,1... | collective-permute-start | bytes 1179656 | tf_op jit(solution)/shard_map/ppermute | solution.py:331
  3.2 4.0 %collective-permute-start.20 = (bf16[384,512]{1,0:T(8,128)(2,1)}, bf16[384,512]{1,0:T(8,128)(2,1)S(1)}, u32[]{:S(2)}, u32[]{:S(2)}) collective-permute-start(bf16[384,512]{1,0:T(8,128)(2,1)} %bitcast.15), channel_id=1, source_target_pairs={{0,7},{1,0},{2,1},{3,2},{4,3},{5,4},{6,5},{7,6},{8,15},{9,8},{10,9... | collective-permute-start | bytes 1179656 | tf_op jit(solution)/shard_map/ppermute | solution.py:331
  7.2 8.9 %collective-permute-done.16.refs_1_ = bf16[384,512]{1,0:T(8,128)(2,1)S(1)} collective-permute-done((bf16[384,512]{1,0:T(8,128)(2,1)}, bf16[384,512]{1,0:T(8,128)(2,1)S(1)}, u32[]{:S(2)}, u32[]{:S(2)}) %collective-permute-start.16) | collective-permute-done | bytes 393248 | tf_op jit(solution)/shard_map/ppermute | solution.py:331
  16.1 2.7 %collective-permute-start.21 = (bf16[384,512]{1,0:T(8,128)(2,1)S(1)}, bf16[384,512]{1,0:T(8,128)(2,1)S(1)}, u32[]{:S(2)}, u32[]{:S(2)}) collective-permute-start(bf16[384,512]{1,0:T(8,128)(2,1)S(1)} %collective-permute-done.20.refs_2_), channel_id=1, source_target_pairs={{0,7},{1,0},{2,1},{3,2},{4,3},{5,4},{6,5},{7,6},{8,15},{9,8},{10,9... | collective-permute-start | bytes 1179656 | tf_op jit(solution)/shard_map/ppermute | solution.py:331
  18.8 8.0 %collective-permute-done.17.refs_3_ = bf16[384,512]{1,0:T(8,128)(2,1)S(1)} collective-permute-done((bf16[384,512]{1,0:T(8,128)(2,1)S(1)}, bf16[384,512]{1,0:T(8,128)(2,1)S(1)}, u32[]{:S(2)}, u32[]{:S(2)}) %collective-permute-start.17) | collective-permute-done | bytes 393248 | tf_op jit(solution)/shard_map/ppermute | solution.py:331
  26.8 2.7 %collective-permute-start.22 = (bf16[384,512]{1,0:T(8,128)(2,1)S(1)}, bf16[384,512]{1,0:T(8,128)(2,1)S(1)}, u32[]{:S(2)}, u32[]{:S(2)}) collective-permute-start(bf16[384,512]{1,0:T(8,128)(2,1)S(1)} %collective-permute-done.21.refs_4_), channel_id=1, source_target_pairs={{0,7},{1,0},{2,1},{3,2},{4,3},{5,4},{6,5},{7,6},{8,15},{9,8},{10,9... | collective-permute-start | bytes 1179656 | tf_op jit(solution)/shard_map/ppermute | solution.py:331
  33.8 2.8 %collective-permute-start = (bf16[4,128,128]{2,1,0:T(8,128)(2,1)S(1)}, bf16[4,128,128]{2,1,0:T(8,128)(2,1)S(1)}, u32[]{:S(2)}, u32[]{:S(2)}) collective-permute-start(bf16[4,128,128]{2,1,0:T(8,128)(2,1)S(1)} %get-tuple-element.52), channel_id=1, source_target_pairs={{0,8},{8,0},{1,9},{9,1},{2,10},{10,2},{3,11},{11,3},{4,12},{12,4},... | collective-permute-start | bytes 393224 | tf_op jit(solution)/shard_map/ppermute | solution.py:331
  38.9 2.4 %collective-permute-start.2 = (bf16[4,128,128]{2,1,0:T(8,128)(2,1)S(1)}, bf16[4,128,128]{2,1,0:T(8,128)(2,1)S(1)}, u32[]{:S(2)}, u32[]{:S(2)}) collective-permute-start(bf16[4,128,128]{2,1,0:T(8,128)(2,1)S(1)} %shard_map.94.t_ref), channel_id=1, source_target_pairs={{0,32},{8,136},{16,48},{24,152},{32,0},{40,168},{48,16},{56,184},{... | collective-permute-start | bytes 393224 | tf_op jit(solution)/shard_map/ppermute | solution.py:343
  43.0 2.4 %collective-permute-done.2.g2 = bf16[4,128,128]{2,1,0:T(8,128)(2,1)S(1)} collective-permute-done((bf16[4,128,128]{2,1,0:T(8,128)(2,1)S(1)}, bf16[4,128,128]{2,1,0:T(8,128)(2,1)S(1)}, u32[]{:S(2)}, u32[]{:S(2)}) %collective-permute-start.2) | collective-permute-done | bytes 131104 | tf_op jit(solution)/shard_map/ppermute | solution.py:343
  47.6 2.6 %collective-permute-start.5 = (bf16[4,128,128]{2,1,0:T(8,128)(2,1)S(1)}, bf16[4,128,128]{2,1,0:T(8,128)(2,1)S(1)}, u32[]{:S(2)}, u32[]{:S(2)}) collective-permute-start(bf16[4,128,128]{2,1,0:T(8,128)(2,1)S(1)} %get-tuple-element.55), channel_id=1, source_target_pairs={{0,128},{8,40},{16,144},{24,56},{32,160},{40,8},{48,176},{56,24},{... | collective-permute-start | bytes 393224 | tf_op jit(solution)/shard_map/ppermute | solution.py:343
  51.4 2.7 %collective-permute-start.23 = (bf16[384,256]{1,0:T(8,128)(2,1)S(1)}, bf16[384,256]{1,0:T(8,128)(2,1)S(1)}, u32[]{:S(2)}, u32[]{:S(2)}) collective-permute-start(bf16[384,256]{1,0:T(8,128)(2,1)S(1)} %shard_map.104), channel_id=1, source_target_pairs={{0,7},{1,0},{2,1},{3,2},{4,3},{5,4},{6,5},{7,6},{8,15},{9,8},{10,9... | collective-permute-start | bytes 589832 | tf_op jit(solution)/shard_map/ppermute | solution.py:331
  54.8 3.6 %collective-permute-start.7 = (bf16[4,128,128]{2,1,0:T(8,128)(2,1)S(1)}, bf16[4,128,128]{2,1,0:T(8,128)(2,1)S(1)}, u32[]{:S(2)}, u32[]{:S(2)}) collective-permute-start(bf16[4,128,128]{2,1,0:T(8,128)(2,1)S(1)} %get-tuple-element.58), channel_id=1, source_target_pairs={{0,8},{8,0},{1,9},{9,1},{2,10},{10,2},{3,11},{11,3},{4,12},{12,4},... | collective-permute-start | bytes 393224 | tf_op jit(solution)/shard_map/ppermute | solution.py:331
  64.3 2.9 %collective-permute-start.9 = (bf16[384,256]{1,0:T(8,128)(2,1)S(1)}, bf16[384,256]{1,0:T(8,128)(2,1)S(1)}, u32[]{:S(2)}, u32[]{:S(2)}) collective-permute-start(bf16[384,256]{1,0:T(8,128)(2,1)S(1)} %get-tuple-element.61), channel_id=1, source_target_pairs={{0,7},{1,0},{2,1},{3,2},{4,3},{5,4},{6,5},{7,6},{8,15},{9,8},{10,9... | collective-permute-start | bytes 589832 | tf_op jit(solution)/shard_map/ppermute | solution.py:331
  67.2 4.7 %collective-permute-done.8.r_ref = bf16[384,256]{1,0:T(8,128)(2,1)S(1)} collective-permute-done((bf16[384,256]{1,0:T(8,128)(2,1)S(1)}, bf16[384,256]{1,0:T(8,128)(2,1)S(1)}, u32[]{:S(2)}, u32[]{:S(2)}) %collective-permute-start.8) | collective-permute-done | bytes 196640 | tf_op jit(solution)/shard_map/ppermute | solution.py:331
  75.8 8.1 %collective-permute-done.10.r_ref = bf16[384,512]{1,0:T(8,128)(2,1)S(1)} collective-permute-done((bf16[384,512]{1,0:T(8,128)(2,1)S(1)}, bf16[384,512]{1,0:T(8,128)(2,1)S(1)}, u32[]{:S(2)}, u32[]{:S(2)}) %collective-permute-start.10) | collective-permute-done | bytes 393248 | tf_op jit(solution)/shard_map/ppermute | solution.py:331
  86.6 2.2 %shard_map.105.refs_3_ = f32[384,512]{1,0:T(8,128)S(1)} custom-call(s32[4]{0:T(128)S(1)} %pad_add_fusion.place, bf16[384,512]{1,0:T(8,128)(2,1)S(1)} %bitcast.17, bf16[384,512]{1,0:T(8,128)(2,1)S(1)} %collective-permute-done.16.refs_1_, bf16[384,512]{1,0:T(8,128)(2,1)S(1)} %collective-permute-done.20.refs_2_, ...), custom_call_target="tpu_custom_call" | custom-call | flops 1409286144 | bytes 7733264 | tf_op jit(solution)/shard_map/pallas_call | solution.py:34
  88.8 2.3 %shard_map.106 = (bf16[2,192,512]{2,1,0:T(8,128)(2,1)S(1)}, f32[4,128,128]{2,1,0:T(8,128)S(1)}, bf16[4,128,128]{2,1,0:T(8,128)(2,1)S(1)}) custom-call(s32[4]{0:T(128)S(1)} %pad_add_fusion.place, bf16[384,256]{1,0:T(8,128)(2,1)S(1)} %collective-permute-done.19.refs_0_.refs_7_, bf16[384,256]{1,0:T(8,128)(2,1)S(1)} %collective-permute-done.23.refs_1_.refs_8_, ...), custom_call_target="tpu_custom_call" | custom-call | flops 201326592 | bytes 7340048 | tf_op jit(solution)/shard_map/pallas_call | solution.py:34
  91.1 2.8 %collective-permute-start.24 = (bf16[4,128,128]{2,1,0:T(8,128)(2,1)S(1)}, bf16[4,128,128]{2,1,0:T(8,128)(2,1)S(1)}, u32[]{:S(2)}, u32[]{:S(2)}) collective-permute-start(bf16[4,128,128]{2,1,0:T(8,128)(2,1)S(1)} %get-tuple-element.74), channel_id=1, source_target_pairs={{0,8},{8,0},{1,9},{9,1},{2,10},{10,2},{3,11},{11,3},{4,12},{12,4},... | collective-permute-start | bytes 393224 | tf_op jit(solution)/shard_map/ppermute | solution.py:331
  95.8 2.2 %collective-permute-start.26 = (bf16[4,128,128]{2,1,0:T(8,128)(2,1)S(1)}, bf16[4,128,128]{2,1,0:T(8,128)(2,1)S(1)}, u32[]{:S(2)}, u32[]{:S(2)}) collective-permute-start(bf16[4,128,128]{2,1,0:T(8,128)(2,1)S(1)} %shard_map.108.t_ref), channel_id=1, source_target_pairs={{0,32},{8,136},{16,48},{24,152},{32,0},{40,168},{48,16},{56,184},{... | collective-permute-start | bytes 393224 | tf_op jit(solution)/shard_map/ppermute | solution.py:343
  107.1 2.7 %collective-permute-start.29 = (bf16[4,128,128]{2,1,0:T(8,128)(2,1)S(1)}, bf16[4,128,128]{2,1,0:T(8,128)(2,1)S(1)}, u32[]{:S(2)}, u32[]{:S(2)}) collective-permute-start(bf16[4,128,128]{2,1,0:T(8,128)(2,1)S(1)} %get-tuple-element.77), channel_id=1, source_target_pairs={{0,128},{8,40},{16,144},{24,56},{32,160},{40,8},{48,176},{56,24},{... | collective-permute-start | bytes 393224 | tf_op jit(solution)/shard_map/ppermute | solution.py:343
  115.5 3.8 %collective-permute-done.30.g3 = bf16[4,128,128]{2,1,0:T(8,128)(2,1)S(1)} collective-permute-done((bf16[4,128,128]{2,1,0:T(8,128)(2,1)S(1)}, bf16[4,128,128]{2,1,0:T(8,128)(2,1)S(1)}, u32[]{:S(2)}, u32[]{:S(2)}) %collective-permute-start.30) | collective-permute-done | bytes 131104 | tf_op jit(solution)/shard_map/ppermute | solution.py:343
  121.0 5.6 %collective-permute-start.31 = (bf16[4,128,128]{2,1,0:T(8,128)(2,1)S(1)}, bf16[4,128,128]{2,1,0:T(8,128)(2,1)S(1)}, u32[]{:S(2)}, u32[]{:S(2)}) collective-permute-start(bf16[4,128,128]{2,1,0:T(8,128)(2,1)S(1)} %get-tuple-element.80), channel_id=1, source_target_pairs={{0,8},{8,0},{1,9},{9,1},{2,10},{10,2},{3,11},{11,3},{4,12},{12,4},... | collective-permute-start | bytes 393224 | tf_op jit(solution)/shard_map/ppermute | solution.py:331
  128.2 2.7 %collective-permute-start.37 = (bf16[512,128]{1,0:T(8,128)(2,1)S(1)}, bf16[512,128]{1,0:T(8,128)(2,1)S(1)}, u32[]{:S(2)}, u32[]{:S(2)}) collective-permute-start(bf16[512,128]{1,0:T(8,128)(2,1)S(1)} %get-tuple-element.89), channel_id=1, source_target_pairs={{0,128},{8,40},{16,144},{24,56},{32,160},{40,8},{48,176},{56,24},{... | collective-permute-start | bytes 393224 | tf_op jit(solution)/shard_map/ppermute | solution.py:343
  131.5 4.3 %shard_map.107 = (bf16[2,192,512]{2,1,0:T(8,128)(2,1)}, f32[2,192,512]{2,1,0:T(8,128)S(1)}, f32[2,192,512]{2,1,0:T(8,128)S(1)}) custom-call(s32[4]{0:T(128)S(1)} %pad_add_fusion.place, bf16[2,192,512]{2,1,0:T(8,128)(2,1)S(1)} %copy-done.7, bf16[2,192,512]{2,1,0:T(8,128)(2,1)S(1)} %copy-done.3, bf16[2,192,512]{2,1,0:T(8,128)(2,1)S(1)} %copy-done.5, ...), custom_call_target="tpu_custom_call" | custom-call | flops 251658240 | bytes 3801104 | tf_op jit(solution)/shard_map/pallas_call | solution.py:34
  (95 shorter events, 49.7 us)
Async XLA Ops:
  0.6 15.5 %collective-permute-start.16 = (bf16[384,512]{1,0:T(8,128)(2,1)}, bf16[384,512]{1,0:T(8,128)(2,1)S(1)}, u32[]{:S(2)}, u32[]{:S(2)}) collective-permute-start(bf16[384,512]{1,0:T(8,128)(2,1)} %bitcast.14), channel_id=1, source_target_pairs={{0,1},{1,2},{2,3},{3,4},{4,5},{5,6},{6,7},{7,0},{8,9},{9,10},{10,1... | collective-permute-start | bytes 1179656 | tf_op jit(solution)/shard_map/ppermute | solution.py:331
  3.2 13.0 %collective-permute-start.20 = (bf16[384,512]{1,0:T(8,128)(2,1)}, bf16[384,512]{1,0:T(8,128)(2,1)S(1)}, u32[]{:S(2)}, u32[]{:S(2)}) collective-permute-start(bf16[384,512]{1,0:T(8,128)(2,1)} %bitcast.15), channel_id=1, source_target_pairs={{0,7},{1,0},{2,1},{3,2},{4,3},{5,4},{6,5},{7,6},{8,15},{9,8},{10,9... | collective-permute-start | bytes 1179656 | tf_op jit(solution)/shard_map/ppermute | solution.py:331
  16.1 10.6 %collective-permute-start.17 = (bf16[384,512]{1,0:T(8,128)(2,1)S(1)}, bf16[384,512]{1,0:T(8,128)(2,1)S(1)}, u32[]{:S(2)}, u32[]{:S(2)}) collective-permute-start(bf16[384,512]{1,0:T(8,128)(2,1)S(1)} %collective-permute-done.16.refs_1_), channel_id=1, source_target_pairs={{0,1},{1,2},{2,3},{3,4},{4,5},{5,6},{6,7},{7,0},{8,9},{9,10},{10,1... | collective-permute-start | bytes 1179656 | tf_op jit(solution)/shard_map/ppermute | solution.py:331
  16.1 10.6 %collective-permute-start.21 = (bf16[384,512]{1,0:T(8,128)(2,1)S(1)}, bf16[384,512]{1,0:T(8,128)(2,1)S(1)}, u32[]{:S(2)}, u32[]{:S(2)}) collective-permute-start(bf16[384,512]{1,0:T(8,128)(2,1)S(1)} %collective-permute-done.20.refs_2_), channel_id=1, source_target_pairs={{0,7},{1,0},{2,1},{3,2},{4,3},{5,4},{6,5},{7,6},{8,15},{9,8},{10,9... | collective-permute-start | bytes 1179656 | tf_op jit(solution)/shard_map/ppermute | solution.py:331
  26.8 24.5 %collective-permute-start.18 = (bf16[384,512]{1,0:T(8,128)(2,1)S(1)}, bf16[384,512]{1,0:T(8,128)(2,1)S(1)}, u32[]{:S(2)}, u32[]{:S(2)}) collective-permute-start(bf16[384,512]{1,0:T(8,128)(2,1)S(1)} %collective-permute-done.17.refs_3_), channel_id=1, source_target_pairs={{0,1},{1,2},{2,3},{3,4},{4,5},{5,6},{6,7},{7,0},{8,9},{9,10},{10,1... | collective-permute-start | bytes 1179656 | tf_op jit(solution)/shard_map/ppermute | solution.py:331
  26.8 24.6 %collective-permute-start.22 = (bf16[384,512]{1,0:T(8,128)(2,1)S(1)}, bf16[384,512]{1,0:T(8,128)(2,1)S(1)}, u32[]{:S(2)}, u32[]{:S(2)}) collective-permute-start(bf16[384,512]{1,0:T(8,128)(2,1)S(1)} %collective-permute-done.21.refs_4_), channel_id=1, source_target_pairs={{0,7},{1,0},{2,1},{3,2},{4,3},{5,4},{6,5},{7,6},{8,15},{9,8},{10,9... | collective-permute-start | bytes 1179656 | tf_op jit(solution)/shard_map/ppermute | solution.py:331
  46.2 7.9 %collective-permute-start.4 = (bf16[4,128,128]{2,1,0:T(8,128)(2,1)S(1)}, bf16[4,128,128]{2,1,0:T(8,128)(2,1)S(1)}, u32[]{:S(2)}, u32[]{:S(2)}) collective-permute-start(bf16[4,128,128]{2,1,0:T(8,128)(2,1)S(1)} %get-tuple-element.54), channel_id=1, source_target_pairs={{0,64},{8,24},{16,80},{24,40},{32,96},{40,56},{48,112},{56,8},{64,... | collective-permute-start | bytes 393224 | tf_op jit(solution)/shard_map/ppermute | solution.py:343
  51.3 9.7 %collective-permute-start.19 = (bf16[384,256]{1,0:T(8,128)(2,1)S(1)}, bf16[384,256]{1,0:T(8,128)(2,1)S(1)}, u32[]{:S(2)}, u32[]{:S(2)}) collective-permute-start(bf16[384,256]{1,0:T(8,128)(2,1)S(1)} %shard_map.103), channel_id=1, source_target_pairs={{0,1},{1,2},{2,3},{3,4},{4,5},{5,6},{6,7},{7,0},{8,9},{9,10},{10,1... | collective-permute-start | bytes 589832 | tf_op jit(solution)/shard_map/ppermute | solution.py:331
  51.4 9.6 %collective-permute-start.23 = (bf16[384,256]{1,0:T(8,128)(2,1)S(1)}, bf16[384,256]{1,0:T(8,128)(2,1)S(1)}, u32[]{:S(2)}, u32[]{:S(2)}) collective-permute-start(bf16[384,256]{1,0:T(8,128)(2,1)S(1)} %shard_map.104), channel_id=1, source_target_pairs={{0,7},{1,0},{2,1},{3,2},{4,3},{5,4},{6,5},{7,6},{8,15},{9,8},{10,9... | collective-permute-start | bytes 589832 | tf_op jit(solution)/shard_map/ppermute | solution.py:331
  63.0 34.9 %collective-permute-start.32 = (bf16[4,4,512,128]{3,2,1,0:T(8,128)(2,1)S(1)}, bf16[4,4,512,128]{3,2,1,0:T(8,128)(2,1)S(1)}, u32[]{:S(2)}, u32[]{:S(2)}) collective-permute-start(bf16[4,4,512,128]{3,2,1,0:T(8,128)(2,1)S(1)} %shard_map.112), channel_id=1, source_target_pairs={{0,8},{8,0},{1,9},{9,1},{2,10},{10,2},{3,11},{11,3},{4,12},{12,4},... | collective-permute-start | bytes 6291464 | tf_op jit(solution)/shard_map/ppermute | solution.py:331
  73.0 10.9 %collective-permute-start.10 = (bf16[384,512]{1,0:T(8,128)(2,1)S(1)}, bf16[384,512]{1,0:T(8,128)(2,1)S(1)}, u32[]{:S(2)}, u32[]{:S(2)}) collective-permute-start(bf16[384,512]{1,0:T(8,128)(2,1)S(1)} %get-tuple-element.62), channel_id=1, source_target_pairs={{0,1},{1,2},{2,3},{3,4},{4,5},{5,6},{6,7},{7,0},{8,9},{9,10},{10,1... | collective-permute-start | bytes 1179656 | tf_op jit(solution)/shard_map/ppermute | solution.py:331
  75.1 9.4 %collective-permute-start.11 = (bf16[384,512]{1,0:T(8,128)(2,1)S(1)}, bf16[384,512]{1,0:T(8,128)(2,1)S(1)}, u32[]{:S(2)}, u32[]{:S(2)}) collective-permute-start(bf16[384,512]{1,0:T(8,128)(2,1)S(1)} %get-tuple-element.63), channel_id=1, source_target_pairs={{0,7},{1,0},{2,1},{3,2},{4,3},{5,4},{6,5},{7,6},{8,15},{9,8},{10,9... | collective-permute-start | bytes 1179656 | tf_op jit(solution)/shard_map/ppermute | solution.py:331
  85.6 19.7 %collective-permute-start.12 = (bf16[384,512]{1,0:T(8,128)(2,1)S(1)}, bf16[384,512]{1,0:T(8,128)(2,1)S(1)}, u32[]{:S(2)}, u32[]{:S(2)}) collective-permute-start(bf16[384,512]{1,0:T(8,128)(2,1)S(1)} %get-tuple-element.64), channel_id=1, source_target_pairs={{0,1},{1,2},{2,3},{3,4},{4,5},{5,6},{6,7},{7,0},{8,9},{9,10},{10,1... | collective-permute-start | bytes 1179656 | tf_op jit(solution)/shard_map/ppermute | solution.py:331
  93.9 13.2 %collective-permute-start.13 = (bf16[384,512]{1,0:T(8,128)(2,1)S(1)}, bf16[384,512]{1,0:T(8,128)(2,1)S(1)}, u32[]{:S(2)}, u32[]{:S(2)}) collective-permute-start(bf16[384,512]{1,0:T(8,128)(2,1)S(1)} %get-tuple-element.65), channel_id=1, source_target_pairs={{0,7},{1,0},{2,1},{3,2},{4,3},{5,4},{6,5},{7,6},{8,15},{9,8},{10,9... | collective-permute-start | bytes 1179656 | tf_op jit(solution)/shard_map/ppermute | solution.py:331
  101.9 19.1 %collective-permute-start.33 = (bf16[4,512,128]{2,1,0:T(8,128)(2,1)S(1)}, bf16[4,512,128]{2,1,0:T(8,128)(2,1)S(1)}, u32[]{:S(2)}, u32[]{:S(2)}) collective-permute-start(bf16[4,512,128]{2,1,0:T(8,128)(2,1)S(1)} %get-tuple-element.84), channel_id=1, source_target_pairs={{0,16},{8,72},{16,32},{24,88},{32,48},{40,104},{48,0},{56,120},{64... | collective-permute-start | bytes 1572872 | tf_op jit(solution)/shard_map/ppermute | solution.py:343
  104.4 22.2 %collective-permute-start.34 = (bf16[4,512,128]{2,1,0:T(8,128)(2,1)S(1)}, bf16[4,512,128]{2,1,0:T(8,128)(2,1)S(1)}, u32[]{:S(2)}, u32[]{:S(2)}) collective-permute-start(bf16[4,512,128]{2,1,0:T(8,128)(2,1)S(1)} %get-tuple-element.85), channel_id=1, source_target_pairs={{0,32},{8,136},{16,48},{24,152},{32,0},{40,168},{48,16},{56,184},{... | collective-permute-start | bytes 1572872 | tf_op jit(solution)/shard_map/ppermute | solution.py:343
  105.3 21.3 %collective-permute-start.35 = (bf16[4,512,128]{2,1,0:T(8,128)(2,1)S(1)}, bf16[4,512,128]{2,1,0:T(8,128)(2,1)S(1)}, u32[]{:S(2)}, u32[]{:S(2)}) collective-permute-start(bf16[4,512,128]{2,1,0:T(8,128)(2,1)S(1)} %get-tuple-element.86), channel_id=1, source_target_pairs={{0,48},{8,200},{16,0},{24,216},{32,16},{40,232},{48,32},{56,248},{... | collective-permute-start | bytes 1572872 | tf_op jit(solution)/shard_map/ppermute | solution.py:343
  110.4 8.9 %collective-permute-start.30 = (bf16[4,128,128]{2,1,0:T(8,128)(2,1)S(1)}, bf16[4,128,128]{2,1,0:T(8,128)(2,1)S(1)}, u32[]{:S(2)}, u32[]{:S(2)}) collective-permute-start(bf16[4,128,128]{2,1,0:T(8,128)(2,1)S(1)} %get-tuple-element.78), channel_id=1, source_target_pairs={{0,192},{8,56},{16,208},{24,8},{32,224},{40,24},{48,240},{56,40},{... | collective-permute-start | bytes 393224 | tf_op jit(solution)/shard_map/ppermute | solution.py:343
  113.8 24.0 %collective-permute-start.14 = (bf16[384,512]{1,0:T(8,128)(2,1)S(1)}, bf16[384,512]{1,0:T(8,128)(2,1)S(1)}, u32[]{:S(2)}, u32[]{:S(2)}) collective-permute-start(bf16[384,512]{1,0:T(8,128)(2,1)S(1)} %get-tuple-element.66), channel_id=1, source_target_pairs={{0,1},{1,2},{2,3},{3,4},{4,5},{5,6},{6,7},{7,0},{8,9},{9,10},{10,1... | collective-permute-start | bytes 1179656 | tf_op jit(solution)/shard_map/ppermute | solution.py:331
  119.3 18.5 %collective-permute-start.15 = (bf16[384,512]{1,0:T(8,128)(2,1)S(1)}, bf16[384,512]{1,0:T(8,128)(2,1)S(1)}, u32[]{:S(2)}, u32[]{:S(2)}) collective-permute-start(bf16[384,512]{1,0:T(8,128)(2,1)S(1)} %get-tuple-element.67), channel_id=1, source_target_pairs={{0,7},{1,0},{2,1},{3,2},{4,3},{5,4},{6,5},{7,6},{8,15},{9,8},{10,9... | collective-permute-start | bytes 1179656 | tf_op jit(solution)/shard_map/ppermute | solution.py:331
  121.0 9.9 %collective-permute-start.31 = (bf16[4,128,128]{2,1,0:T(8,128)(2,1)S(1)}, bf16[4,128,128]{2,1,0:T(8,128)(2,1)S(1)}, u32[]{:S(2)}, u32[]{:S(2)}) collective-permute-start(bf16[4,128,128]{2,1,0:T(8,128)(2,1)S(1)} %get-tuple-element.80), channel_id=1, source_target_pairs={{0,8},{8,0},{1,9},{9,1},{2,10},{10,2},{3,11},{11,3},{4,12},{12,4},... | collective-permute-start | bytes 393224 | tf_op jit(solution)/shard_map/ppermute | solution.py:331
  127.4 12.1 %collective-permute-start.36 = (bf16[512,128]{1,0:T(8,128)(2,1)S(1)}, bf16[512,128]{1,0:T(8,128)(2,1)S(1)}, u32[]{:S(2)}, u32[]{:S(2)}) collective-permute-start(bf16[512,128]{1,0:T(8,128)(2,1)S(1)} %get-tuple-element.88), channel_id=1, source_target_pairs={{0,64},{8,24},{16,80},{24,40},{32,96},{40,56},{48,112},{56,8},{64,... | collective-permute-start | bytes 393224 | tf_op jit(solution)/shard_map/ppermute | solution.py:343
  128.2 11.3 %collective-permute-start.37 = (bf16[512,128]{1,0:T(8,128)(2,1)S(1)}, bf16[512,128]{1,0:T(8,128)(2,1)S(1)}, u32[]{:S(2)}, u32[]{:S(2)}) collective-permute-start(bf16[512,128]{1,0:T(8,128)(2,1)S(1)} %get-tuple-element.89), channel_id=1, source_target_pairs={{0,128},{8,40},{16,144},{24,56},{32,160},{40,8},{48,176},{56,24},{... | collective-permute-start | bytes 393224 | tf_op jit(solution)/shard_map/ppermute | solution.py:343
  130.9 8.6 %collective-permute-start.38 = (bf16[512,128]{1,0:T(8,128)(2,1)S(1)}, bf16[512,128]{1,0:T(8,128)(2,1)S(1)}, u32[]{:S(2)}, u32[]{:S(2)}) collective-permute-start(bf16[512,128]{1,0:T(8,128)(2,1)S(1)} %get-tuple-element.90), channel_id=1, source_target_pairs={{0,192},{8,56},{16,208},{24,8},{32,224},{40,24},{48,240},{56,40},{... | collective-permute-start | bytes 393224 | tf_op jit(solution)/shard_map/ppermute | solution.py:343
  (23 other events, 138.9 us)
